TPU v7x, 128 devices: a whole 4x4x4 slice. The times are simulated.
128 devices in a mesh: dp: 8 (over z, y_lo), ctx: 8 (over x, y_hi), tp: 2 (over core).
Axes of the slice: x: 4, y: 4 (y_hi: 2, y_lo: 2; y = y_hi * 2 + y_lo), z: 4, core: 2. Of those that a mesh axis runs over, the one named last changes fastest.
Arguments:
- hidden_in: bfloat16 [16, 1024, 1536], P('dp', 'ctx'), may hold values from -6 to 6
- context: bfloat16 [16, 130, 1536], P('dp'), may hold values from -6 to 6
- lengths: int32 [16], P('dp'), may hold values from 128 to 1024, as said below
- cond_mask: int32 [16, 130], P('dp'), may hold values from 0 to 1, as said below
- out_grad: bfloat16 [16, 1024, 1536], P('dp', 'ctx'), may hold values from -6 to 6
- gain_attn: bfloat16 [1536], P('dp'), may hold values from 0.099609375 to 1.8984375
- self_proj: bfloat16 [1536, 3, 1536], P('dp', None, 'tp')
- self_out: bfloat16 [1536, 1536], P('dp', 'tp'), may hold values from -2.5 to 2.5
- gain_cross: bfloat16 [1536], P('dp'), may hold values from 0.099609375 to 1.8984375
- cross_query: bfloat16 [1536, 1536], P('dp', 'tp'), may hold values from -0.15625 to 0.15625
- cross_keyval: bfloat16 [1536, 2, 1536], P('dp', None, 'tp'), may hold values from -0.15625 to 0.15625
- cross_out: bfloat16 [1536, 1536], P('dp', 'tp'), may hold values from -0.875 to 0.875
- gain_feed: bfloat16 [1536], P('dp'), may hold values from 0.099609375 to 1.8984375
- feed_in: bfloat16 [1536, 2, 6144], P('dp', None, 'tp'), may hold values from -0.15625 to 0.15625
- feed_out: bfloat16 [1536, 6144], P('dp', 'tp'), may hold values from -0.078125 to 0.078125
Outputs:
- layer_out: bfloat16 [16, 1024, 1536], P('dp', 'ctx')
- in_grad: float32 [16, 1024, 1536], P('dp', 'ctx')
- cond_grad: float32 [16, 130, 1536], P('dp')
- layer_stats: float32 [16, 5], P('dp')
- grad_gain_attn: float32 [1536], P('dp')
- grad_self_proj: float32 [1536, 3, 1536], P('dp', None, 'tp')
- grad_self_out: float32 [1536, 1536], P('dp', 'tp')
- grad_gain_cross: float32 [1536], P('dp')
- grad_cross_query: float32 [1536, 1536], P('dp', 'tp')
- grad_cross_keyval: float32 [1536, 2, 1536], P('dp', None, 'tp')
- grad_cross_out: float32 [1536, 1536], P('dp', 'tp')
- grad_gain_feed: float32 [1536], P('dp')
- grad_feed_in: float32 [1536, 2, 6144], P('dp', None, 'tp')
- grad_feed_out: float32 [1536, 6144], P('dp', 'tp')
Inputs may be any that keep to these rules, and one draw needn't show every extreme that they name: `lengths`: one sequence has exactly 1024 valid tokens. `cond_mask`: the first conditioning token of every sequence is valid.
All inputs are finite; a program needn't handle non-finite values.
Results may differ from a plain program's by a relative error of at most 0.025.
Values may be sent and summed in bfloat16 or wider, within the bound.
No kernel may reach another device: no remote copies, remote signals or barrier semaphores. Data moves between devices by JAX's collectives and lax.ppermute only.
A program may use at most 256 MiB of HBM per device.

v0:
```python
import jax
import jax.numpy as jnp
from jax import lax
from jax.sharding import PartitionSpec as P

HD = 64
ROT = 32


norm_eps = 1e-05
masked_fill = -1e30


def shortened(shard):
    return jax.tree.map(lambda a: a.astype(jnp.bfloat16) if a.dtype == jnp.float32 else a, shard)


def sent_to_all(shard, axis):
    copies = jnp.broadcast_to(shard, (lax.axis_size(axis), *shard.shape))
    return lax.all_to_all(copies, axis, split_axis=0, concat_axis=0, tiled=True)


def over_copies(shard, axis):
    everything = sent_to_all(shard, axis)
    return jnp.sum(everything, axis=0)


def padded_to(lines, count):
    spare = -len(lines) % count
    return jnp.pad(lines, [(0, spare)] + [(0, 0)] * (lines.ndim - 1))


def total_of(shard, axis):
    lines = shard.reshape(-1, *shard.shape[1:][-1:])
    padded = padded_to(lines, lax.axis_size(axis))
    own = lax.psum_scatter(padded, axis, scatter_dimension=0, tiled=True)
    whole = lax.all_gather(own, axis, axis=0, tiled=True)
    return whole[: len(lines)].reshape(shard.shape)


def layer_norm(field_in, gain_vec):
    average = jnp.mean(field_in, axis=-1, keepdims=True)
    centered = field_in - average
    variance = jnp.mean(centered * centered, axis=-1, keepdims=True)
    return centered * lax.rsqrt(variance + norm_eps) * gain_vec


def rotate_half(vector):
    half_size = vector.shape[-1] // 2
    return jnp.concatenate([-vector[..., half_size:], vector[..., :half_size]], axis=-1)


def rotary_tables(first_row, number_rows, turned_size):
    positions = (first_row + jnp.arange(number_rows, dtype=jnp.int32)).astype(jnp.float32)
    exponent = jnp.arange(turned_size // 2, dtype=jnp.int32).astype(jnp.float32) * (
        2.0 / turned_size
    )
    frequency = jnp.power(jnp.float32(10000.0), -exponent)
    angles = positions[:, None] * frequency[None, :]
    angles = jnp.concatenate([angles, angles], axis=-1)
    return (jnp.cos(angles), jnp.sin(angles))


def rotate(vector, cosine_table, sine_table):
    turned_size = cosine_table.shape[-1]
    turned = vector[..., :turned_size]
    turned = turned * cosine_table + rotate_half(turned) * sine_table
    return jnp.concatenate([turned, vector[..., turned_size:]], axis=-1)


def softmax_rows(scores, valid_mask):
    masked = jnp.where(valid_mask, scores, masked_fill)
    maximum = jnp.max(masked, axis=-1, keepdims=True)
    exponent = jnp.exp(masked - maximum)
    row_total = jnp.sum(exponent, axis=-1, keepdims=True)
    return (exponent / row_total, maximum + jnp.log(row_total))


def softmax_back(weights_in, grad_weights):
    return weights_in * (grad_weights - jnp.sum(grad_weights * weights_in, axis=-1, keepdims=True))


def glu_unit(gate_part, upward):
    return gate_part * jax.nn.sigmoid(gate_part) * upward


def gather_weights(params):
    return jax.tree.map(
        lambda part, own: part.astype(own.dtype),
        lax.all_gather(shortened(params), "dp", axis=0, tiled=True),
        params,
    )


def head_sum(partial_value):
    return over_copies(partial_value, "tp")


def reduce_grads(gradients):
    summed_rows = jax.tree.map(
        lambda part: part.astype(jnp.float32),
        lax.psum_scatter(shortened(gradients), "dp", scatter_dimension=0, tiled=True),
    )
    return jax.tree.map(
        lambda part: part.astype(jnp.float32), lax.psum(shortened(summed_rows), "ctx")
    )


def per_device(
    hidden_in,
    context,
    lengths,
    cond_mask,
    out_grad,
    gain_attn,
    self_proj,
    self_out,
    gain_cross,
    cross_query,
    cross_keyval,
    cross_out,
    gain_feed,
    feed_in,
    feed_out,
):
    seqs_here, block_rows, model_width = hidden_in.shape
    cond_count = context.shape[1]
    local_width = self_proj.shape[2]
    local_heads = local_width // HD
    head_scale = HD ** (-0.5)
    seq_len = block_rows * lax.axis_size("ctx")
    block_start = lax.axis_index("ctx") * block_rows
    cosine_table, sine_table = rotary_tables(block_start, block_rows, ROT)
    cosine_table = cosine_table[None, :, None, :]
    sine_table = sine_table[None, :, None, :]
    key_valid = (jnp.arange(seq_len, dtype=jnp.int32)[None, :] < lengths[:, None])[:, None, None, :]
    query_valid = (block_start + jnp.arange(block_rows, dtype=jnp.int32))[None, :] < lengths[
        :, None
    ]
    cond_valid = (cond_mask > 0)[:, None, None, :]
    token_rows = hidden_in.astype(jnp.float32)

    def rope_scaled(vector):
        return rotate(vector, cosine_table, sine_table) * head_scale

    def rope_plain(vector):
        return rotate(vector, cosine_table, sine_table)

    attn_set = gather_weights((gain_attn, self_proj, self_out))
    normed_full, norm_back_one = jax.vjp(layer_norm, token_rows, attn_set[0].astype(jnp.float32))
    normed_one = normed_full.astype(jnp.bfloat16)
    projected = jnp.einsum(
        "sbd,dke->sbke", normed_one, attn_set[1], preferred_element_type=jnp.float32
    )
    projected = projected.reshape(seqs_here, block_rows, 3, local_heads, HD)
    query_raw = projected[:, :, 0]
    key_raw = projected[:, :, 1]
    queries = rope_scaled(query_raw).astype(jnp.bfloat16)
    rotated_keys = rope_plain(key_raw).astype(jnp.bfloat16)
    value_rows = projected[:, :, 2].astype(jnp.bfloat16)
    all_keys, all_values = (
        lax.all_gather(rotated_keys, "ctx", axis=1, tiled=True),
        lax.all_gather(value_rows, "ctx", axis=1, tiled=True),
    )
    scores = jnp.einsum("sqhe,skhe->shqk", queries, all_keys, preferred_element_type=jnp.float32)
    attn_probs, log_total = softmax_rows(scores, key_valid)
    probs_low = attn_probs.astype(jnp.bfloat16)
    attended = jnp.einsum(
        "shqk,skhe->sqhe", probs_low, all_values, preferred_element_type=jnp.float32
    )
    attended = attended.astype(jnp.bfloat16).reshape(seqs_here, block_rows, local_width)
    attn_branch = head_sum(
        jnp.einsum("sbi,oi->sbo", attended, attn_set[2], preferred_element_type=jnp.float32)
    )
    resid_one = token_rows + attn_branch
    cross_set = gather_weights((gain_cross, cross_query, cross_keyval, cross_out))
    normed_full, norm_back_two = jax.vjp(layer_norm, resid_one, cross_set[0].astype(jnp.float32))
    normed_two = normed_full.astype(jnp.bfloat16)
    cross_q = (
        jnp.einsum("sbd,de->sbe", normed_two, cross_set[1], preferred_element_type=jnp.float32)
        * head_scale
    )
    cross_q = cross_q.astype(jnp.bfloat16).reshape(seqs_here, block_rows, local_heads, HD)
    cond_proj = jnp.einsum(
        "sci,ike->scke", context, cross_set[2], preferred_element_type=jnp.float32
    )
    cross_k = (
        cond_proj[:, :, 0].astype(jnp.bfloat16).reshape(seqs_here, cond_count, local_heads, HD)
    )
    cross_v = (
        cond_proj[:, :, 1].astype(jnp.bfloat16).reshape(seqs_here, cond_count, local_heads, HD)
    )
    cross_scores = jnp.einsum(
        "sqhe,skhe->shqk", cross_q, cross_k, preferred_element_type=jnp.float32
    )
    cross_probs = softmax_rows(cross_scores, cond_valid)[0]
    cross_low = cross_probs.astype(jnp.bfloat16)
    cross_att = jnp.einsum(
        "shqk,skhe->sqhe", cross_low, cross_v, preferred_element_type=jnp.float32
    )
    cross_att = cross_att.astype(jnp.bfloat16).reshape(seqs_here, block_rows, local_width)
    cross_branch = head_sum(
        jnp.einsum("sbi,oi->sbo", cross_att, cross_set[3], preferred_element_type=jnp.float32)
    )
    resid_two = resid_one + cross_branch
    feed_set = gather_weights((gain_feed, feed_in, feed_out))
    normed_full, norm_back_three = jax.vjp(layer_norm, resid_two, feed_set[0].astype(jnp.float32))
    normed_three = normed_full.astype(jnp.bfloat16)
    gate_up = jnp.einsum(
        "sbd,dkf->sbkf", normed_three, feed_set[1], preferred_element_type=jnp.float32
    )
    hidden_full, glu_back = jax.vjp(glu_unit, gate_up[:, :, 0], gate_up[:, :, 1])
    hidden = hidden_full.astype(jnp.bfloat16)
    feed_branch = head_sum(
        jnp.einsum("sbf,of->sbo", hidden, feed_set[2], preferred_element_type=jnp.float32)
    )
    output = resid_two + feed_branch

    def square_sums(field_in):
        return jnp.sum(jnp.where(query_valid[:, :, None], field_in * field_in, 0.0), axis=(1, 2))

    partial_value = jnp.stack(
        [
            square_sums(field_in)
            for field_in in (token_rows, attn_branch, cross_branch, feed_branch, output)
        ],
        axis=1,
    )
    stat_totals = lax.psum(partial_value, "ctx")
    layer_stats = jnp.sqrt(stat_totals / (lengths.astype(jnp.float32)[:, None] * model_width))
    upstream = out_grad.astype(jnp.float32)
    feed_back = gather_weights((feed_in, feed_out))
    grad_feed = upstream.astype(jnp.bfloat16)
    grad_hidden = jnp.einsum(
        "sbo,of->sbf", grad_feed, feed_back[1], preferred_element_type=jnp.float32
    )
    grad_feed_out = jnp.einsum("sbo,sbf->of", grad_feed, hidden, preferred_element_type=jnp.float32)
    grad_gate, grad_up = glu_back(grad_hidden)
    grad_gate_up = jnp.stack([grad_gate, grad_up], axis=2).astype(jnp.bfloat16)
    grad_normed_three = head_sum(
        jnp.einsum("sbkf,dkf->sbd", grad_gate_up, feed_back[0], preferred_element_type=jnp.float32)
    )
    grad_feed_in = jnp.einsum(
        "sbd,sbkf->dkf", normed_three, grad_gate_up, preferred_element_type=jnp.float32
    )
    grad_resid_norm, grad_gain_three = norm_back_three(grad_normed_three)
    grad_resid_two = upstream + grad_resid_norm
    feed_grads = reduce_grads((grad_gain_three, grad_feed_in, grad_feed_out))
    cross_back = gather_weights((cross_query, cross_keyval, cross_out))
    grad_cross = grad_resid_two.astype(jnp.bfloat16)
    grad_cross_att = jnp.einsum(
        "sbo,oi->sbi", grad_cross, cross_back[2], preferred_element_type=jnp.float32
    ).astype(jnp.bfloat16)
    grad_cross_out = jnp.einsum(
        "sbo,sbi->oi", grad_cross, cross_att, preferred_element_type=jnp.float32
    )
    grad_cross_heads = grad_cross_att.reshape(seqs_here, block_rows, local_heads, HD)
    grad_cross_probs = jnp.einsum(
        "sqhe,skhe->shqk", grad_cross_heads, cross_v, preferred_element_type=jnp.float32
    )
    grad_cross_scores = softmax_back(cross_probs, grad_cross_probs).astype(jnp.bfloat16)
    grad_cq = (
        jnp.einsum(
            "shqk,skhe->sqhe", grad_cross_scores, cross_k, preferred_element_type=jnp.float32
        )
        * head_scale
    )
    grad_cq = grad_cq.astype(jnp.bfloat16).reshape(seqs_here, block_rows, local_width)
    grad_ck = jnp.einsum(
        "shqk,sqhe->skhe", grad_cross_scores, cross_q, preferred_element_type=jnp.float32
    )
    grad_cv = jnp.einsum(
        "shqk,sqhe->skhe", cross_low, grad_cross_heads, preferred_element_type=jnp.float32
    )
    cond_terms = jnp.stack(
        [
            grad_ck.reshape(seqs_here, cond_count, local_width),
            grad_cv.reshape(seqs_here, cond_count, local_width),
        ],
        axis=2,
    )
    cond_share = lax.psum_scatter(
        cond_terms.astype(jnp.bfloat16), "ctx", scatter_dimension=3, tiled=True
    )
    share_width = cond_share.shape[3]
    column_start = lax.axis_index("ctx") * share_width
    keyval_cols = lax.dynamic_slice_in_dim(cross_back[1], column_start, share_width, 2)
    cond_part = jnp.einsum(
        "sckj,ikj->sci", cond_share, keyval_cols, preferred_element_type=jnp.float32
    )
    cond_grad = total_of(cond_part.astype(jnp.bfloat16), ("ctx", "tp")).astype(jnp.float32)
    keyval_piece = jnp.einsum(
        "sci,sckj->ikj", context, cond_share, preferred_element_type=jnp.float32
    )
    grad_cross_keyval = lax.dynamic_update_slice_in_dim(
        jnp.zeros(cross_back[1].shape, jnp.float32), keyval_piece, column_start, 2
    )
    grad_normed_two = head_sum(
        jnp.einsum("sbe,de->sbd", grad_cq, cross_back[0], preferred_element_type=jnp.float32)
    )
    grad_cross_query = jnp.einsum(
        "sbd,sbe->de", normed_two, grad_cq, preferred_element_type=jnp.float32
    )
    grad_resid_norm, grad_gain_two = norm_back_two(grad_normed_two)
    grad_resid_one = grad_resid_two + grad_resid_norm
    cross_grads = reduce_grads((grad_gain_two, grad_cross_query, grad_cross_keyval, grad_cross_out))
    attn_back = gather_weights((self_proj, self_out))
    grad_attn = grad_resid_one.astype(jnp.bfloat16)
    grad_attended = jnp.einsum(
        "sbo,oi->sbi", grad_attn, attn_back[1], preferred_element_type=jnp.float32
    ).astype(jnp.bfloat16)
    grad_self_out = jnp.einsum(
        "sbo,sbi->oi", grad_attn, attended, preferred_element_type=jnp.float32
    )
    grad_heads = grad_attended.reshape(seqs_here, block_rows, local_heads, HD)
    scores_again = jnp.einsum(
        "sqhe,skhe->shqk", queries, all_keys, preferred_element_type=jnp.float32
    )
    probs_again = jnp.exp(jnp.where(key_valid, scores_again, masked_fill) - log_total)
    again_low = probs_again.astype(jnp.bfloat16)
    grad_probs = jnp.einsum(
        "sqhe,skhe->shqk", grad_heads, all_values, preferred_element_type=jnp.float32
    )
    grad_scores = softmax_back(probs_again, grad_probs).astype(jnp.bfloat16)
    grad_query = jnp.einsum(
        "shqk,skhe->sqhe", grad_scores, all_keys, preferred_element_type=jnp.float32
    )
    grad_key_all = jnp.einsum(
        "shqk,sqhe->skhe", grad_scores, queries, preferred_element_type=jnp.float32
    )
    grad_value_all = jnp.einsum(
        "shqk,sqhe->skhe", again_low, grad_heads, preferred_element_type=jnp.float32
    )
    grad_key, grad_value = (
        lax.psum_scatter(
            grad_key_all.astype(jnp.bfloat16), "ctx", scatter_dimension=1, tiled=True
        ).astype(jnp.float32),
        lax.psum_scatter(
            grad_value_all.astype(jnp.bfloat16), "ctx", scatter_dimension=1, tiled=True
        ).astype(jnp.float32),
    )
    rope_unused, back_scaled = jax.vjp(rope_scaled, query_raw)
    rope_unused, back_plain = jax.vjp(rope_plain, key_raw)
    grad_query_raw = back_scaled(grad_query)[0]
    grad_key_raw = back_plain(grad_key)[0]
    grad_qkv = jnp.stack([grad_query_raw, grad_key_raw, grad_value], axis=2).astype(jnp.bfloat16)
    grad_qkv = grad_qkv.reshape(seqs_here, block_rows, 3, local_width)
    grad_normed_one = head_sum(
        jnp.einsum("sbke,dke->sbd", grad_qkv, attn_back[0], preferred_element_type=jnp.float32)
    )
    grad_self_proj = jnp.einsum(
        "sbd,sbke->dke", normed_one, grad_qkv, preferred_element_type=jnp.float32
    )
    grad_input_norm, grad_gain_one = norm_back_one(grad_normed_one)
    in_grad = grad_resid_one + grad_input_norm
    attn_grads = reduce_grads((grad_gain_one, grad_self_proj, grad_self_out))
    return (
        output.astype(jnp.bfloat16),
        in_grad,
        cond_grad,
        layer_stats,
        attn_grads[0],
        attn_grads[1],
        attn_grads[2],
        cross_grads[0],
        cross_grads[1],
        cross_grads[2],
        cross_grads[3],
        feed_grads[0],
        feed_grads[1],
        feed_grads[2],
    )


def solution(mesh):
    return jax.shard_map(
        per_device,
        mesh=mesh,
        in_specs=(
            P("dp", "ctx", None),
            P("dp", None, None),
            P("dp"),
            P("dp", None),
            P("dp", "ctx", None),
            P("dp"),
            P("dp", None, "tp"),
            P("dp", "tp"),
            P("dp"),
            P("dp", "tp"),
            P("dp", None, "tp"),
            P("dp", "tp"),
            P("dp"),
            P("dp", None, "tp"),
            P("dp", "tp"),
        ),
        out_specs=(
            P("dp", "ctx", None),
            P("dp", "ctx", None),
            P("dp", None, None),
            P("dp", None),
            P("dp"),
            P("dp", None, "tp"),
            P("dp", "tp"),
            P("dp"),
            P("dp", "tp"),
            P("dp", None, "tp"),
            P("dp", "tp"),
            P("dp"),
            P("dp", None, "tp"),
            P("dp", "tp"),
        ),
        check_vma=False,
    )
```

profile of v0, /device:TPU:1, one launch (start us, length us, event | category | flops | bytes accessed | tf_op | source)
XLA Modules:
  0.0 2993.1 jit_solution(16238624054110774870)
XLA Ops:
  12.1 31.5 %all-reduce.21 = (bf16[1536]{0:T(1024)(128)(2,1)S(1)}, bf16[1536]{0:T(1024)(128)(2,1)S(1)}, bf16[1536]{0:T(1024)(128)(2,1)S(1)}) all-reduce(bf16[1536]{0:T(1024)(128)(2,1)S(1)} %dynamic-update-slice, bf16[1536]{0:T(1024)(128)(2,1)S(1)} %dynamic-update-slice.1, ...), channel_id=1, replica_groups=mesh['dp'=8,'ctx'=8,'tp'=2] {'dp'}, use_global_device_ids=true, to_apply=%add.9 | all-reduce | flops 4608 | bytes 18432
  44.4 113.4 %all-gather.12.cloned.1.call-done = bf16[1536,3,768]{2,0,1:T(8,128)(2,1)} async-done(((bf16[192,3,768]{2,0,1:T(8,128)(2,1)}), bf16[1536,3,768]{2,0,1:T(8,128)(2,1)}) %all-gather.12.cloned.1.call-update) | async-done | bytes 7077904 | tf_op jit(solution)/shard_map/all_gather | solution.py:90
  175.0 86.2 %all-gather.18.cloned.1.call-done = bf16[1536,2,768]{2,0,1:T(8,128)(2,1)} async-done(((bf16[192,2,768]{2,0,1:T(8,128)(2,1)}), bf16[1536,2,768]{2,0,1:T(8,128)(2,1)}) %all-gather.18.cloned.1.call-update) | async-done | bytes 4718608 | tf_op jit(solution)/shard_map/all_gather | solution.py:90
  267.5 63.6 %all-gather.14.cloned.1.call-done = bf16[2,1024,12,64]{1,3,2,0:T(8,128)(2,1)} async-done(((bf16[2,128,12,64]{1,3,2,0:T(8,128)(2,1)}), bf16[2,1024,12,64]{1,3,2,0:T(8,128)(2,1)}) %all-gather.14.cloned.1.call-update) | async-done | bytes 3145744 | tf_op jit(solution)/shard_map/all_gather | solution.py:162
  342.3 57.9 %all-gather.28.cloned.1.call-done = bf16[2,1024,1,12,64]{1,4,3,0,2:T(8,128)(2,1)} async-done(((bf16[2,128,1,12,64]{1,4,3,0,2:T(8,128)(2,1)}), bf16[2,1024,1,12,64]{1,4,3,0,2:T(8,128)(2,1)}) %all-gather.28.cloned.1.call-update) | async-done | bytes 3145744 | tf_op jit(solution)/shard_map/all_gather | solution.py:163
  400.2 8.5 fusion.86
  408.7 49.6 %all-gather.16.cloned.1.call-done = bf16[1536,768]{1,0:T(8,128)(2,1)} async-done(((bf16[192,768]{1,0:T(8,128)(2,1)}), bf16[1536,768]{1,0:T(8,128)(2,1)}) %all-gather.16.cloned.1.call-update) | async-done | bytes 2359312 | tf_op jit(solution)/shard_map/all_gather | solution.py:90
  461.3 7.9 all_to_all.30
  474.6 41.7 %all-gather.20.cloned.1.call-done = bf16[1536,768]{1,0:T(8,128)(2,1)} async-done(((bf16[192,768]{1,0:T(8,128)(2,1)}), bf16[1536,768]{1,0:T(8,128)(2,1)}) %all-gather.20.cloned.1.call-update) | async-done | bytes 2359312 | tf_op jit(solution)/shard_map/all_gather | solution.py:90
  523.6 50.7 %all-gather.22.cloned.1.call-done = bf16[1536,768]{1,0:T(8,128)(2,1)} async-done(((bf16[192,768]{1,0:T(8,128)(2,1)}), bf16[1536,768]{1,0:T(8,128)(2,1)}) %all-gather.22.cloned.1.call-update) | async-done | bytes 2359312 | tf_op jit(solution)/shard_map/all_gather | solution.py:90
  577.2 7.7 all_to_all.31
  592.4 348.5 %all-gather.24.cloned.1.call-done = bf16[1536,2,3072]{2,0,1:T(8,128)(2,1)} async-done(((bf16[192,2,3072]{2,0,1:T(8,128)(2,1)}), bf16[1536,2,3072]{2,0,1:T(8,128)(2,1)}) %all-gather.24.cloned.1.call-update) | async-done | bytes 18874384 | tf_op jit(solution)/shard_map/all_gather | solution.py:90
  940.9 13.5 fusion.4
  954.4 177.2 %all-gather.26.cloned.1.call-done = bf16[1536,3072]{1,0:T(8,128)(2,1)} async-done(((bf16[192,3072]{1,0:T(8,128)(2,1)}), bf16[1536,3072]{1,0:T(8,128)(2,1)}) %all-gather.26.cloned.1.call-update) | async-done | bytes 9437200 | tf_op jit(solution)/shard_map/all_gather | solution.py:90
  1131.6 11.2 fusion.67
  1147.5 6.1 all-to-all-start.2
  1153.6 10.8 fusion.35
  1199.4 7.5 all_to_all.32
  1235.8 12.5 multiply_reduce_fusion
  1249.3 6.6 multiply_convert_fusion
  1261.2 12.9 copy.274
  1274.0 11.4 reshape.335
  1285.5 9.0 convert_bitcast_fusion
  1294.5 12.9 copy.276
  1307.4 11.4 reshape.337
  1329.3 47.7 %dynamic_update_slice.3 = bf16[1536,2,768]{2,1,0:T(2,128)(2,1)} dynamic-update-slice(bf16[1536,2,768]{2,1,0:T(2,128)(2,1)} %broadcast_in_dim.144, bf16[1536,2,96]{2,1,0:T(2,128)(2,1)} %copy.238, s32[]{:T(128)} %constant.46.clone.1, s32[]{:T(128)} %constant.46.clone.1, s32[]{:T(128)S(6)} %select_n.31) | dynamic-update-slice | bytes 1179652 | tf_op jit(solution)/shard_map/dynamic_update_slice | solution.py:295
  1377.0 7.9 fusion.7
  1384.9 12.6 copy.280
  1409.3 6.1 fusion.75
  1423.9 49.6 %reduce-scatter.32.cloned.1.call-done = bf16[128,1536]{1,0:T(8,128)(2,1)} async-done(((bf16[1024,1536]{1,0:T(8,128)(2,1)}), bf16[128,1536]{1,0:T(8,128)(2,1)}) %reduce-scatter.32.cloned.1.call-update) | async-done | bytes 393232
  1478.1 6.3 bitcast_convert_fusion.2
  1485.2 11.0 bitcast_convert_fusion
  1497.1 289.7 %all-reduce.25.cloned.1.call-done = bf16[1536,2,768]{2,1,0:T(2,128)(2,1)} async-done(((bf16[1536,2,768]{2,1,0:T(2,128)(2,1)}), bf16[1536,2,768]{2,1,0:T(2,128)(2,1)}) %all-reduce.25.cloned.1.call-update) | async-done | bytes 4718608
  1789.0 189.3 %reduce-scatter.36.cloned.1.call-done = bf16[192,3072]{1,0:T(8,128)(2,1)} async-done(((bf16[1536,3072]{1,0:T(8,128)(2,1)}), bf16[192,3072]{1,0:T(8,128)(2,1)}) %reduce-scatter.36.cloned.1.call-update) | async-done | bytes 1179664
  1980.9 58.3 %reduce-scatter.24.cloned.1.call-done = bf16[192,768]{1,0:T(8,128)(2,1)} async-done(((bf16[1536,768]{1,0:T(8,128)(2,1)}), bf16[192,768]{1,0:T(8,128)(2,1)}) %reduce-scatter.24.cloned.1.call-update) | async-done | bytes 294928 | tf_op jit(solution)/shard_map/reduce_scatter | solution.py:102
  2039.1 59.2 %reduce-scatter.26.cloned.1.call-done = bf16[192,768]{1,0:T(8,128)(2,1)} async-done(((bf16[1536,768]{1,0:T(8,128)(2,1)}), bf16[192,768]{1,0:T(8,128)(2,1)}) %reduce-scatter.26.cloned.1.call-update) | async-done | bytes 294928 | tf_op jit(solution)/shard_map/reduce_scatter | solution.py:102
  2098.3 59.8 %reduce-scatter.22.cloned.1.call-done = bf16[192,768]{1,0:T(8,128)(2,1)} async-done(((bf16[1536,768]{1,0:T(8,128)(2,1)}), bf16[192,768]{1,0:T(8,128)(2,1)}) %reduce-scatter.22.cloned.1.call-update) | async-done | bytes 294928 | tf_op jit(solution)/shard_map/reduce_scatter | solution.py:102
  2158.1 146.6 %reduce-scatter.20.cloned.1.call-done = bf16[192,3,768]{2,0,1:T(8,128)(2,1)} async-done(((bf16[1536,3,768]{2,0,1:T(8,128)(2,1)}), bf16[192,3,768]{2,0,1:T(8,128)(2,1)}) %reduce-scatter.20.cloned.1.call-update) | async-done | bytes 884752 | tf_op jit(solution)/shard_map/reduce_scatter | solution.py:102
  2304.7 369.3 %reduce-scatter.28.cloned.1.call-done = bf16[192,2,3072]{2,0,1:T(8,128)(2,1)} async-done(((bf16[1536,2,3072]{2,0,1:T(8,128)(2,1)}), bf16[192,2,3072]{2,0,1:T(8,128)(2,1)}) %reduce-scatter.28.cloned.1.call-update) | async-done | bytes 2359312 | tf_op jit(solution)/shard_map/reduce_scatter | solution.py:102
  2677.1 66.2 %fusion = bf16[24,1536]{1,0:T(8,128)(2,1)S(1)} fusion(bf16[272,1536]{1,0:T(8,128)(2,1)S(1)} %pad.36), kind=kCustom, calls=%all-reduce-scatter | all-reduce-scatter fusion | flops 589825 | bytes 909824
  2750.5 10.2 collective-permute-start.2
  2768.7 42.5 %all-gather.1 = bf16[16,17,1536]{2,1,0:T(8,128)(2,1)S(1)} all-gather(bf16[1,17,1536]{2,1,0:T(8,128)(2,1)S(1)} %dynamic-slice_bitcast_fusion), channel_id=1, replica_groups=mesh['dp'=8,'ctx'=8,'tp'=2] {'ctx','tp'}, dimensions={0}, use_global_device_ids=true | all-gather | bytes 887808 | tf_op jit(solution)/shard_map/all_gather | solution.py:37
  2821.2 7.0 all_to_all.33
  2839.7 27.9 psum.77
  2867.6 41.7 %all-reduce.20 = (bf16[1536]{0:T(1024)(128)(2,1)S(1)}, bf16[1536]{0:T(1024)(128)(2,1)S(1)}, bf16[1536]{0:T(1024)(128)(2,1)S(1)}) all-reduce(bf16[1536]{0:T(1024)(128)(2,1)S(1)} %get-tuple-element.88, bf16[1536]{0:T(1024)(128)(2,1)S(1)} %copy-done.73, ...), channel_id=7, replica_groups=mesh['dp'=8,'ctx'=8,'tp'=2] {'dp'}, use_global_device_ids=true, to_apply=%region_35.36.clone | all-reduce | flops 4608 | bytes 18432
  2909.6 23.8 all-reduce.18
  2938.8 33.7 %all-reduce.27.cloned.1.call-done = (bf16[192,2,3072]{2,0,1:T(8,128)(2,1)}, bf16[192,3072]{0,1:T(8,128)(2,1)}, bf16[192,3,768]{2,0,1:T(8,128)(2,1)}, bf16[192,76...) async-done(((bf16[192,2,3072]{2,0,1:T(8,128)(2,1)}, bf16[192,3072]{0,1:T(8,128)(2,1)}, ...) | async-done | bytes 5898256 | tf_op jit(solution)/shard_map/psum | solution.py:105
  2972.5 6.4 copy.244
  (411 shorter events, 232.2 us)
Async XLA Ops:
  7.2 150.6 %all-gather.12.cloned.1.call-start = ((), (), s32[]{:S(2)}) async-start(), calls=%async_computation.15 | async-start | bytes 7962624 | tf_op jit(solution)/shard_map/all_gather | solution.py:90
  8.0 253.3 %all-gather.18.cloned.1.call-start = ((), (), s32[]{:S(2)}) async-start(), calls=%async_computation.18 | async-start | bytes 5308416 | tf_op jit(solution)/shard_map/all_gather | solution.py:90
  10.0 321.1 %all-gather.14.cloned.1.call-start = ((), (), s32[]{:S(2)}) async-start(), calls=%async_computation.16 | async-start | bytes 3538944 | tf_op jit(solution)/shard_map/all_gather | solution.py:162
  43.6 119.5 %copy-start.60 = (f32[1536]{0:T(1024)}, f32[1536]{0:T(1024)S(1)}, u32[]{:S(2)}) copy-start(f32[1536]{0:T(1024)S(1)} %convert_element_type.229) | copy-start | bytes 18436
  43.8 120.9 %copy-start.54 = (f32[128,32]{0,1:T(8,128)}, f32[128,32]{0,1:T(8,128)S(1)}, u32[]{:S(2)}) copy-start(f32[128,32]{0,1:T(8,128)S(1)} %get-tuple-element.143) | copy-start | bytes 49156
  43.8 120.9 %copy-start.56 = (f32[128,32]{0,1:T(8,128)}, f32[128,32]{0,1:T(8,128)S(1)}, u32[]{:S(2)}) copy-start(f32[128,32]{0,1:T(8,128)S(1)} %get-tuple-element.144) | copy-start | bytes 49156
  44.0 119.1 %copy-start.70 = (f32[2,128]{1,0:T(2,128)}, f32[2,128]{1,0:T(2,128)S(1)}, u32[]{:S(2)}) copy-start(f32[2,128]{1,0:T(2,128)S(1)} %broadcast_multiply_fusion.3) | copy-start | bytes 3076
  44.3 118.8 %copy-start.79 = (f32[2,128]{1,0:T(2,128)}, f32[2,128]{1,0:T(2,128)S(1)}, u32[]{:S(2)}) copy-start(f32[2,128]{1,0:T(2,128)S(1)} %fusion.62) | copy-start | bytes 3076
  44.4 118.8 %copy-start.77 = (f32[2,128]{1,0:T(2,128)}, f32[2,128]{1,0:T(2,128)S(1)}, u32[]{:S(2)}) copy-start(f32[2,128]{1,0:T(2,128)S(1)} %fusion.119) | copy-start | bytes 3076
  164.9 166.2 %copy-start.16 = (f32[2,128,12,32]{1,3,2,0:T(8,128)}, f32[2,128,12,32]{1,3,2,0:T(8,128)S(1)}, u32[]{:S(2)}) copy-start(f32[2,128,12,32]{1,3,2,0:T(8,128)S(1)} %get-tuple-element.129) | copy-start | bytes 1179652
  164.9 166.2 %copy-start.18 = (f32[2,128,12,32]{1,3,2,0:T(8,128)}, f32[2,128,12,32]{1,3,2,0:T(8,128)S(1)}, u32[]{:S(2)}) copy-start(f32[2,128,12,32]{1,3,2,0:T(8,128)S(1)} %get-tuple-element.130) | copy-start | bytes 1179652
  165.8 234.4 %all-gather.28.cloned.1.call-start = ((), (), s32[]{:S(2)}) async-start(), calls=%async_computation.28 | async-start | bytes 3538944 | tf_op jit(solution)/shard_map/all_gather | solution.py:163
  167.8 290.5 %all-gather.16.cloned.1.call-start = ((), (), s32[]{:S(2)}) async-start(), calls=%async_computation.17 | async-start | bytes 2654208 | tf_op jit(solution)/shard_map/all_gather | solution.py:90
  168.4 347.8 %all-gather.20.cloned.1.call-start = ((), (), s32[]{:S(2)}) async-start(), calls=%async_computation.19 | async-start | bytes 2654208 | tf_op jit(solution)/shard_map/all_gather | solution.py:90
  169.0 405.3 %all-gather.22.cloned.1.call-start = ((), (), s32[]{:S(2)}) async-start(), calls=%async_computation.20 | async-start | bytes 2654208 | tf_op jit(solution)/shard_map/all_gather | solution.py:90
  169.8 771.1 %all-gather.24.cloned.1.call-start = ((), (), s32[]{:S(2)}) async-start(), calls=%async_computation.21 | async-start | bytes 21233664 | tf_op jit(solution)/shard_map/all_gather | solution.py:90
  173.5 87.8 %copy-start.39 = (bf16[2,130,1536]{2,0,1:T(2,128)(2,1)S(1)}, bf16[2,130,1536]{2,0,1:T(2,128)(2,1)}, u32[]{:S(2)}) copy-start(bf16[2,130,1536]{2,0,1:T(2,128)(2,1)} %param.16) | copy-start | bytes 2396164
  173.5 958.1 %all-gather.26.cloned.1.call-start = ((), (), s32[]{:S(2)}) async-start(), calls=%async_computation.22 | async-start | bytes 10616832 | tf_op jit(solution)/shard_map/all_gather | solution.py:90
  174.3 342.0 %copy-start.51 = (f32[1536]{0:T(1024)}, f32[1536]{0:T(1024)S(1)}, u32[]{:S(2)}) copy-start(f32[1536]{0:T(1024)S(1)} %convert_element_type.239) | copy-start | bytes 18436
  334.9 65.3 %copy-start.58 = (f32[2,12,128]{2,1,0:T(8,128)}, f32[2,12,128]{2,1,0:T(8,128)S(1)}, u32[]{:S(2)}) copy-start(f32[2,12,128]{2,1,0:T(8,128)S(1)} %get-tuple-element.147) | copy-start | bytes 36868
  342.3 66.4 %copy-start.64 = (f32[2,12,128]{2,1,0:T(8,128)}, f32[2,12,128]{2,1,0:T(8,128)S(1)}, u32[]{:S(2)}) copy-start(f32[2,12,128]{2,1,0:T(8,128)S(1)} %fusion.6) | copy-start | bytes 36868
  590.3 594.2 %copy-start.62 = (f32[2,128]{1,0:T(2,128)}, f32[2,128]{1,0:T(2,128)S(1)}, u32[]{:S(2)}) copy-start(f32[2,128]{1,0:T(2,128)S(1)} %broadcast_multiply_fusion.1) | copy-start | bytes 3076
  1147.5 16.9 all-to-all-start.2
  1167.8 8.7 all-to-all-start.3
  1173.1 146.1 %reduce-scatter.34.cloned.1.call-start = ((), (), s32[]{:S(2)}) async-start(), calls=%async_computation.31 | async-start | bytes 1105920
  1235.6 179.9 %reduce-scatter.30.cloned.1.call-start = ((), (), s32[]{:S(2)}) async-start(), calls=%async_computation.29 | async-start | bytes 3538944
  1285.5 188.0 %reduce-scatter.32.cloned.1.call-start = ((), (), s32[]{:S(2)}) async-start(), calls=%async_computation.30 | async-start | bytes 3538944
  1318.8 467.9 %all-reduce.25.cloned.1.call-start = ((), (), s32[]{:S(2)}) async-start(), calls=%async_computation.33 | async-start | bytes 9437184
  1377.0 601.4 %reduce-scatter.36.cloned.1.call-start = ((), (), s32[]{:S(2)}) async-start(), calls=%async_computation.32 | async-start | bytes 10616832
  1397.6 641.5 %reduce-scatter.24.cloned.1.call-start = ((), (), s32[]{:S(2)}) async-start(), calls=%async_computation.25 | async-start | bytes 2654208 | tf_op jit(solution)/shard_map/reduce_scatter | solution.py:102
  1401.7 696.7 %reduce-scatter.26.cloned.1.call-start = ((), (), s32[]{:S(2)}) async-start(), calls=%async_computation.26 | async-start | bytes 2654208 | tf_op jit(solution)/shard_map/reduce_scatter | solution.py:102
  1405.1 752.9 %reduce-scatter.22.cloned.1.call-start = ((), (), s32[]{:S(2)}) async-start(), calls=%async_computation.24 | async-start | bytes 2654208 | tf_op jit(solution)/shard_map/reduce_scatter | solution.py:102
  1408.8 895.8 %reduce-scatter.20.cloned.1.call-start = ((), (), s32[]{:S(2)}) async-start(), calls=%async_computation.23 | async-start | bytes 7962624 | tf_op jit(solution)/shard_map/reduce_scatter | solution.py:102
  1423.9 54.2 %copy-start.61 = (f32[1536]{0:T(1024)S(1)}, f32[1536]{0:T(1024)}, u32[]{:S(2)}) copy-start(f32[1536]{0:T(1024)} %copy-done.60) | copy-start | bytes 18436
  1423.9 54.2 %copy-start.71 = (f32[2,128]{1,0:T(2,128)S(1)}, f32[2,128]{1,0:T(2,128)}, u32[]{:S(2)}) copy-start(f32[2,128]{1,0:T(2,128)} %copy-done.70) | copy-start | bytes 3076
  1423.9 54.2 %copy-start.78 = (f32[2,128]{1,0:T(2,128)S(1)}, f32[2,128]{1,0:T(2,128)}, u32[]{:S(2)}) copy-start(f32[2,128]{1,0:T(2,128)} %copy-done.77) | copy-start | bytes 3076
  1484.5 1189.5 %reduce-scatter.28.cloned.1.call-start = ((), (), s32[]{:S(2)}) async-start(), calls=%async_computation.27 | async-start | bytes 21233664 | tf_op jit(solution)/shard_map/reduce_scatter | solution.py:102
  1496.2 1476.3 %all-reduce.27.cloned.1.call-start = ((), (), s32[]{:S(2)}) async-start(), calls=%async_computation.34 | async-start | bytes 12582912 | tf_op jit(solution)/shard_map/psum | solution.py:105
  2677.0 89.3 %copy-start.91 = (s32[2]{0:T(128)S(1)}, s32[2]{0:T(128)}, u32[]{:S(2)}) copy-start(s32[2]{0:T(128)} %param.17) | copy-start | bytes 28
  2677.0 89.3 %copy-start.92 = (u32[128]{0:T(128)S(1)}, u32[128]{0:T(128)}, u32[]{:S(2)}) copy-start(u32[128]{0:T(128)} %constant.96) | copy-start | bytes 1540
  2677.0 90.5 %copy-start.89 = (f32[2]{0:T(128)S(1)}, f32[2]{0:T(128)}, u32[]{:S(2)}) copy-start(f32[2]{0:T(128)} %get-tuple-element.92) | copy-start | bytes 28
  2677.0 90.6 %copy-start.88 = (f32[2]{0:T(128)S(1)}, f32[2]{0:T(128)}, u32[]{:S(2)}) copy-start(f32[2]{0:T(128)} %get-tuple-element.93) | copy-start | bytes 28
  2743.3 24.4 collective-permute-start
  2749.2 18.5 collective-permute-start.1
  2750.5 17.2 collective-permute-start.2
  2760.7 7.0 collective-permute-start.3
  2762.4 5.4 collective-permute-start.4
  2835.7 100.0 %copy-start.7 = (f32[2,128,1536]{2,1,0:T(8,128)S(1)}, f32[2,128,1536]{2,1,0:T(8,128)}, u32[]{:S(2)}) copy-start(f32[2,128,1536]{2,1,0:T(8,128)} %copy-done.5) | copy-start | bytes 4718596
  (79 other events, 666.2 us)
Sparse Core Ops, SparseCore 0:
  9.7 148.0 all-gather.11
  160.0 101.1 all-gather.17
  264.0 66.9 all-gather.13
  333.7 66.4 all-gather.27
  401.7 56.6 all-gather.15
  459.9 56.3 all-gather.19
  517.9 56.3 all-gather.21
  576.5 364.3 all-gather.23
  942.5 189.0 all-gather.25
  1235.7 70.8 reduce-scatter.33
  1311.0 79.6 reduce-scatter.29
  1394.4 79.0 reduce-scatter.31
  1476.7 310.0 all-reduce.24
  1789.2 189.1 reduce-scatter.35
  1980.8 58.3 reduce-scatter.23
  2041.6 56.7 reduce-scatter.25
  2101.3 56.7 reduce-scatter.21
  2160.5 144.1 reduce-scatter.19
  2307.3 366.6 reduce-scatter.27
  2677.8 294.6 all-reduce.26
where the time goes:
time: 3010 us; the launch traced here: 2990 us
  waiting for transfers between devices  2250 us (75%)
  blocking collectives  264 us (9%)
  local copies, waits for them, and re-layouts  208 us (7%)
  matrix products  154 us (5%)
  other arithmetic  65.2 us (2%)
  starting transfers between devices  36.5 us (1%)
    all_gather x7, waiting for transfers between devices, gather_weights(): lax.all_gather(shortened(params), 'dp', axis=0, tiled=True)  867 us
    reduce_scatter x5, waiting for transfers between devices, reduce_grads(): lax.psum_scatter(shortened(gradients), 'dp', scatter_dimension=0, tiled=T...  693 us
    unnamed x30, waiting for transfers between devices  531 us
    unnamed x3, blocking collectives  139 us
    unnamed x236, local copies, waits for them, and re-layouts  128 us
    all_gather x1, waiting for transfers between devices, per_device(): lax.all_gather(rotated_keys, 'ctx', axis=1, tiled=True)  63.6 us
  transfers between devices with their start and end apart: 27, of which 18 were waited for; matrix products, arithmetic and copies ran while one was open for 13% of the time, Pallas kernels for 0%

commit v1 on v0

v1 whole, which is shorter than its diff:
```python
import jax
import jax.numpy as jnp
from jax import lax
from jax.experimental import pallas as pl
from jax.experimental.pallas import tpu as pltpu
from jax.sharding import Mesh
from jax.sharding import PartitionSpec as P

DP = ("z", "yl")
CTX = ("x", "yh")
PLANE = ("z", "yh", "yl")
SWAP = ((0, 0), (1, 2), (2, 1), (3, 3))

D = 1536
HD = 64
ROT = 32
HEADS = 3
WIDE = 256
ROWS = 128
SEQ = 1024
QB = 256
CROSS_KEYS = 144
norm_eps = 1e-05
masked_fill = -1e30
bf16 = jnp.bfloat16
f32 = jnp.float32


def permuted(v):
    parts = []
    for z in range(4):
        for piece in (0, 2, 1, 3):
            at = z * 384 + piece * 96
            parts.append(v[..., at : at + 96])
    return jnp.concatenate(parts, axis=-1)


def dot(a, b):
    return jnp.dot(a, b, preferred_element_type=f32)


def dot_nt(a, b):
    return lax.dot_general(a, b, (((1,), (1,)), ((), ())), preferred_element_type=f32)


def dot_tn(a, b):
    return lax.dot_general(a, b, (((0,), (0,)), ((), ())), preferred_element_type=f32)


def to_partner(v):
    return lax.ppermute(v, "tp", ((0, 1), (1, 0)))


def sent_to_all(v, axes, count):
    copies = jnp.broadcast_to(v[None], (count, *v.shape))
    return lax.all_to_all(copies, axes, split_axis=0, concat_axis=0, tiled=True)


def gather_rows(own):
    mine = sent_to_all(own, "x", 4).reshape(4 * ROWS, D)
    return jnp.concatenate([mine, to_partner(mine)], axis=0)


def scatter_rows(partial):
    half = 4 * ROWS
    got = to_partner(partial[half:].astype(bf16))
    mine = (partial[:half] + got.astype(f32)).astype(bf16)
    arrived = lax.all_to_all(mine.reshape(4, ROWS, D), "x", split_axis=0, concat_axis=0, tiled=True)
    return jnp.sum(arrived.astype(f32), axis=0)


def pair_rows(own):
    return jnp.concatenate([own, to_partner(own)], axis=0)


def pair_sum(partial):
    return partial[:ROWS] + to_partner(partial[ROWS:])


def gather_plane(shard):
    return lax.all_gather(shard, PLANE, axis=0, tiled=True)


def scatter_plane(grad):
    return lax.psum_scatter(grad, PLANE, scatter_dimension=0, tiled=True)


def unit_norm(v):
    centered = v - jnp.mean(v, axis=-1, keepdims=True)
    scale = lax.rsqrt(jnp.mean(centered * centered, axis=-1, keepdims=True) + norm_eps)
    return centered * scale, scale


def unit_norm_back(x_hat, scale, grad):
    along = jnp.mean(grad * x_hat, axis=-1, keepdims=True)
    return scale * (grad - jnp.mean(grad, axis=-1, keepdims=True) - x_hat * along)


def lane_masks(rows):
    lane = lax.broadcasted_iota(jnp.int32, (rows, WIDE), 1)
    heads = [(lane // HD == h).astype(f32).astype(bf16) for h in range(HEADS)]
    return lane, heads, (lane == HEADS * HD).astype(f32).astype(bf16)


def turned(v, cosine, sine, first):
    other = jnp.where(first, pltpu.roll(v, WIDE - ROT // 2, 1), pltpu.roll(v, ROT // 2, 1))
    return v * cosine, other * sine


def attn_forward_kernel(sc, qkv, cosine, sine, att, qs, ks, vs, lse, vt):
    lane, heads, extra = lane_masks(QB)
    first = lane % HD < ROT // 2
    wide_head = lax.broadcasted_iota(jnp.int32, (WIDE, QB), 0) // HD

    def prepare(block, carry):
        rows = pl.ds(block * QB, QB)
        c, s = cosine[rows, :], sine[rows, :]
        straight, crossed = turned(qkv[rows, 0:WIDE], c, s, first)
        query = ((straight + crossed) * HD ** (-0.5)).astype(bf16)
        qs[rows, :] = jnp.where(lane < HEADS * HD, query.astype(f32), jnp.where(lane == HEADS * HD, 1.0, 0.0)).astype(bf16)
        straight, crossed = turned(qkv[rows, WIDE : 2 * WIDE], c, s, first)
        row = lax.broadcasted_iota(jnp.int32, (QB, WIDE), 0) + block * QB
        side = jnp.where(row < SEQ // 2, sc[0], 1 - sc[0])
        within = row % (SEQ // 2)
        place = (within // ROWS * 2 + side) * ROWS + within % ROWS
        fill = jnp.where((lane == HEADS * HD) & (place >= sc[1]), masked_fill, 0.0)
        ks[rows, :] = jnp.where(lane < HEADS * HD, straight + crossed, fill).astype(bf16)
        value = qkv[rows, 2 * WIDE : 3 * WIDE]
        vs[rows, :] = value.astype(bf16)
        vt[:, rows] = value.T.astype(bf16)
        return carry

    for block in range(SEQ // QB):
        prepare(block, 0)

    def attend(block, carry):
        rows = pl.ds(pl.multiple_of(block * QB, QB), QB)
        query = qs[rows, :]
        total = jnp.zeros((WIDE, QB), f32)
        for h in range(HEADS):
            scores = dot_nt(ks[...], query * (heads[h] + extra))
            top = jnp.max(scores, axis=0, keepdims=True)
            weight = jnp.exp(scores - top)
            mass = jnp.sum(weight, axis=0, keepdims=True)
            out = dot(vt[...], weight.astype(bf16))
            total = jnp.where(wide_head == h, out / mass, total)
            lse[h : h + 1, rows] = top + jnp.log(mass)
        att[rows, :] = total.T.astype(bf16)
        return carry

    lse[...] = jnp.zeros(lse.shape, f32)
    lax.fori_loop(0, SEQ // QB, attend, 0)


def attn_forward(scalars, qkv, cosine, sine):
    wide = jax.ShapeDtypeStruct((SEQ, WIDE), bf16)
    return pl.pallas_call(
        attn_forward_kernel,
        in_specs=[pl.BlockSpec(memory_space=pltpu.SMEM)] + [pl.BlockSpec(memory_space=pltpu.VMEM)] * 3,
        out_shape=(wide, wide, wide, wide, jax.ShapeDtypeStruct((8, SEQ), f32)),
        scratch_shapes=[pltpu.VMEM((WIDE, SEQ), bf16)],
        cost_estimate=pl.CostEstimate(flops=4 * HEADS * SEQ * SEQ * WIDE, transcendentals=HEADS * SEQ * SEQ, bytes_accessed=8 << 20),
    )(scalars, qkv, cosine, sine)


def attn_backward_kernel(qs, ks, vs, grad, lse, cosine, sine, out, kt, dk, dv):
    lane, heads, extra = lane_masks(QB)
    first = lane % HD < ROT // 2
    wide_head = lax.broadcasted_iota(jnp.int32, (WIDE, QB), 0) // HD
    kept = lane < HEADS * HD
    kt[...] = ks[...].astype(f32).T.astype(bf16)
    dk[...] = jnp.zeros(dk.shape, f32)
    dv[...] = jnp.zeros(dv.shape, f32)

    def step(block, carry):
        rows = pl.ds(pl.multiple_of(block * QB, QB), QB)
        query, given = qs[rows, :], grad[rows, :]
        total = jnp.zeros((WIDE, QB), f32)
        for h in range(HEADS):
            own_query, own_grad = query * heads[h], given * heads[h]
            scores = dot_nt(ks[...], query * (heads[h] + extra))
            weight = jnp.exp(scores - lse[h : h + 1, rows])
            wanted = dot_nt(vs[...], own_grad)
            product = weight * wanted
            inner = jnp.sum(product, axis=0, keepdims=True)
            slope = (product - weight * inner).astype(bf16)
            dv[...] += dot(weight.astype(bf16), own_grad)
            dk[...] += dot(slope, own_query)
            total = jnp.where(wide_head == h, dot(kt[...], slope), total)
        straight, crossed = turned(total.T * HD ** (-0.5), cosine[rows, :], sine[rows, :], first)
        out[rows, 0:WIDE] = jnp.where(kept, straight - crossed, 0.0).astype(bf16)
        return carry

    lax.fori_loop(0, SEQ // QB, step, 0)
    for block in range(SEQ // QB):
        rows = pl.ds(block * QB, QB)
        straight, crossed = turned(dk[rows, :], cosine[rows, :], sine[rows, :], first)
        out[rows, WIDE : 2 * WIDE] = jnp.where(kept, straight - crossed, 0.0).astype(bf16)
        out[rows, 2 * WIDE : 3 * WIDE] = dv[rows, :].astype(bf16)


def attn_backward(qs, ks, vs, grad, lse, cosine, sine):
    return pl.pallas_call(
        attn_backward_kernel,
        in_specs=[pl.BlockSpec(memory_space=pltpu.VMEM)] * 7,
        out_shape=jax.ShapeDtypeStruct((SEQ, 3 * WIDE), bf16),
        scratch_shapes=[pltpu.VMEM((WIDE, SEQ), bf16), pltpu.VMEM((SEQ, WIDE), f32), pltpu.VMEM((SEQ, WIDE), f32)],
        cost_estimate=pl.CostEstimate(flops=10 * HEADS * SEQ * SEQ * WIDE, transcendentals=HEADS * SEQ * SEQ, bytes_accessed=8 << 20),
    )(qs, ks, vs, grad, lse, cosine, sine)


PAIR = 2 * HD


def cross_weights(query, keys, bias):
    scores = dot_nt(keys, query) + bias
    weight = jnp.exp(scores - jnp.max(scores, axis=0, keepdims=True))
    return weight / jnp.sum(weight, axis=0, keepdims=True)


def cross_forward_kernel(cq, ck, cv, bias, att):
    lane = lax.broadcasted_iota(jnp.int32, (2 * ROWS, PAIR), 1)
    row = lax.broadcasted_iota(jnp.int32, (PAIR, 2 * ROWS), 0)
    for group in range(cq.shape[1] // PAIR):
        at = pl.ds(group * PAIR, PAIR)
        query, keys = cq[:, at], ck[:, at]
        values = cv[:, at].astype(f32).T.astype(bf16)
        outs = []
        for h in range(2):
            mask = (lane // HD == h).astype(f32).astype(bf16)
            weight = cross_weights(query * mask, keys, bias[...])
            outs.append(dot(values, weight.astype(bf16)))
        att[:, at] = jnp.where(row < HD, outs[0], outs[1]).T.astype(bf16)


def cross_forward(cq, ck, cv, bias):
    return pl.pallas_call(
        cross_forward_kernel,
        in_specs=[pl.BlockSpec(memory_space=pltpu.VMEM)] * 4,
        out_shape=jax.ShapeDtypeStruct(cq.shape, bf16),
        cost_estimate=pl.CostEstimate(flops=4 * 12 * 256 * 144 * 128, transcendentals=12 * 256 * 144, bytes_accessed=2 << 20),
    )(cq, ck, cv, bias)


def cross_backward_kernel(cq, ck, cv, bias, grad, dq, dkv):
    lane = lax.broadcasted_iota(jnp.int32, (2 * ROWS, PAIR), 1)
    row = lax.broadcasted_iota(jnp.int32, (PAIR, 2 * ROWS), 0)
    width = cq.shape[1]
    for group in range(width // PAIR):
        at = pl.ds(group * PAIR, PAIR)
        query, keys, values, given = cq[:, at], ck[:, at], cv[:, at], grad[:, at]
        turned_keys = keys.astype(f32).T.astype(bf16)
        outs, key_grad, value_grad = [], 0.0, 0.0
        for h in range(2):
            mask = (lane // HD == h).astype(f32).astype(bf16)
            own_query, own_grad = query * mask, given * mask
            weight = cross_weights(own_query, keys, bias[...])
            product = weight * dot_nt(values, own_grad)
            slope = (product - weight * jnp.sum(product, axis=0, keepdims=True)).astype(bf16)
            outs.append(dot(turned_keys, slope))
            key_grad += dot(slope, own_query)
            value_grad += dot(weight.astype(bf16), own_grad)
        dq[:, at] = (jnp.where(row < HD, outs[0], outs[1]).T * HD ** (-0.5)).astype(bf16)
        dkv[:, at] = key_grad.astype(bf16)
        dkv[:, pl.ds(width + group * PAIR, PAIR)] = value_grad.astype(bf16)


def cross_backward(cq, ck, cv, bias, grad):
    return pl.pallas_call(
        cross_backward_kernel,
        in_specs=[pl.BlockSpec(memory_space=pltpu.VMEM)] * 5,
        out_shape=(jax.ShapeDtypeStruct(cq.shape, bf16), jax.ShapeDtypeStruct((CROSS_KEYS, 2 * cq.shape[1]), bf16)),
        cost_estimate=pl.CostEstimate(flops=10 * 12 * 256 * 144 * 128, transcendentals=12 * 256 * 144, bytes_accessed=3 << 20),
    )(cq, ck, cv, bias, grad)


def rotary_lanes(side):
    row = jnp.arange(SEQ, dtype=jnp.int32)
    within = row % (SEQ // 2)
    part = jnp.where(row < SEQ // 2, side, 1 - side)
    place = ((within // ROWS * 2 + part) * ROWS + within % ROWS).astype(f32)
    lane = jnp.arange(WIDE, dtype=jnp.int32) % HD
    exponent = (lane % (ROT // 2)).astype(f32) * (2.0 / ROT)
    angle = place[:, None] * jnp.power(jnp.float32(10000.0), -exponent)[None, :]
    inside = (lane < ROT)[None, :]
    sign = jnp.where(lane < ROT // 2, -1.0, 1.0)[None, :]
    return jnp.where(inside, jnp.cos(angle), 1.0), jnp.where(inside, jnp.sin(angle) * sign, 0.0)


def per_device(
    hidden_in,
    context,
    lengths,
    cond_mask,
    out_grad,
    gain_attn,
    self_proj,
    self_out,
    gain_cross,
    cross_query,
    cross_keyval,
    cross_out,
    gain_feed,
    feed_in,
    feed_out,
):
    x, yh, tp = lax.axis_index("x"), lax.axis_index("yh"), lax.axis_index("tp")
    cond_count = context.shape[1]
    own_rows = hidden_in.shape[1]
    half_rows = self_proj.shape[0] // 2
    quarter = self_proj.shape[2] // 4
    hidden_quarter = feed_in.shape[2] // 4
    local_width = self_proj.shape[2]

    def own_half(w):
        return lax.dynamic_slice_in_dim(w, yh * half_rows, half_rows, 0)

    def own_cols(w, count):
        return lax.dynamic_slice_in_dim(w, x * count, count, w.ndim - 1)

    def scaled(w, gain):
        g = own_half(gain).astype(f32)
        return (w.astype(f32) * g.reshape((-1,) + (1,) * (w.ndim - 1))).astype(bf16)

    x_own = lax.ppermute(lax.dynamic_index_in_dim(hidden_in, tp, 0, False), ("yh", "tp"), SWAP)
    u_own = lax.ppermute(lax.dynamic_index_in_dim(out_grad, tp, 0, False), ("yh", "tp"), SWAP)
    length = lax.dynamic_index_in_dim(lengths, yh, 0, False)
    own_mask = lax.dynamic_index_in_dim(cond_mask, yh, 0, False)
    own_context = permuted(lax.dynamic_index_in_dim(context, yh, 0, False))

    proj_cols = scaled(own_cols(own_half(self_proj), quarter), gain_attn)
    proj_cols = jnp.pad(proj_cols, ((0, 0), (0, 0), (0, WIDE - quarter))).reshape(half_rows, 3 * WIDE)
    out_cols = jnp.pad(own_cols(own_half(self_out), quarter), ((0, 0), (0, WIDE - quarter)))
    attn_set = gather_plane(jnp.concatenate([proj_cols, out_cols], axis=1))
    keyval_cols = own_cols(own_half(cross_keyval), quarter).reshape(half_rows, 2 * quarter)
    cross_set = gather_plane(
        jnp.concatenate([scaled(own_half(cross_query), gain_cross), own_half(cross_out), keyval_cols], axis=1)
    )
    feed_cols = scaled(own_cols(own_half(feed_in), hidden_quarter), gain_feed).reshape(half_rows, 2 * hidden_quarter)
    w_feed = gather_plane(feed_cols)
    w_down = gather_plane(own_cols(own_half(feed_out), hidden_quarter))
    w_proj, w_out = attn_set[:, : 3 * WIDE], attn_set[:, 3 * WIDE :]
    w_cq = cross_set[:, :local_width]
    w_co = cross_set[:, local_width : 2 * local_width]
    w_kv = cross_set[:, 2 * local_width :]

    tokens = permuted(x_own).astype(f32)
    norm_one, scale_one = unit_norm(tokens)
    full_one = gather_rows(norm_one.astype(bf16))
    cosine, sine = rotary_lanes(tp)
    scalars = jnp.stack([tp.astype(jnp.int32), length])
    attended, qs, ks, vs, lse = attn_forward(scalars, dot(full_one, w_proj), cosine, sine)
    attn_branch = scatter_rows(dot_nt(attended, w_out))
    resid_one = tokens + attn_branch

    cond_kv = dot(own_context, w_kv).astype(bf16)
    cond_kv = jnp.pad(cond_kv, ((0, CROSS_KEYS - cond_count), (0, 0)))
    cond_kv = sent_to_all(cond_kv, "x", 4).reshape(4, CROSS_KEYS, 2, quarter)
    cond_kv = cond_kv.transpose(2, 1, 0, 3).reshape(2, CROSS_KEYS, local_width)
    seen = jnp.pad(own_mask > 0, (0, CROSS_KEYS - cond_count))
    bias = jnp.broadcast_to(jnp.where(seen, 0.0, masked_fill)[:, None], (CROSS_KEYS, 2 * own_rows)).astype(f32)
    norm_two, scale_two = unit_norm(resid_one)
    pair_two = pair_rows(norm_two.astype(bf16))
    cross_q = (dot(pair_two, w_cq) * HD ** (-0.5)).astype(bf16)
    cross_att = cross_forward(cross_q, cond_kv[0], cond_kv[1], bias)
    cross_branch = pair_sum(dot_nt(cross_att, w_co))
    resid_two = resid_one + cross_branch

    norm_three, scale_three = unit_norm(resid_two)
    full_three = gather_rows(norm_three.astype(bf16))
    upstream = permuted(u_own)
    full_grad = gather_rows(upstream)
    gate_up = dot(full_three, w_feed)
    gate, upward = gate_up[:, :hidden_quarter], gate_up[:, hidden_quarter:]
    sig = jax.nn.sigmoid(gate)
    hidden = (gate * sig * upward).astype(bf16)
    grad_hidden = dot(full_grad, w_down)
    grad_gate = grad_hidden * upward * sig * (1.0 + gate * (1.0 - sig))
    grad_gate_up = jnp.concatenate([grad_gate.astype(bf16), (grad_hidden * gate * sig).astype(bf16)], axis=1)
    grad_three = scatter_rows(dot_nt(grad_gate_up, w_feed))
    feed_branch = scatter_rows(dot_nt(hidden, w_down))
    output = resid_two + feed_branch
    sum_feed = scatter_plane(dot_tn(full_three, grad_gate_up).astype(bf16))
    sum_down = scatter_plane(dot_tn(full_grad, hidden).astype(bf16))
    grad_resid_two = upstream.astype(f32) + unit_norm_back(norm_three, scale_three, grad_three)

    pair_grad = pair_rows(grad_resid_two.astype(bf16))
    grad_cross_att = dot(pair_grad, w_co).astype(bf16)
    grad_cq, grad_ckv = cross_backward(cross_q, cond_kv[0], cond_kv[1], bias, grad_cross_att)
    grad_two = pair_sum(dot_nt(grad_cq, w_cq))
    grad_resid_one = grad_resid_two + unit_norm_back(norm_two, scale_two, grad_two)
    sum_cross = scatter_plane(
        jnp.concatenate([dot_tn(pair_two, grad_cq).astype(bf16), dot_tn(pair_grad, cross_att).astype(bf16)], axis=1)
    )
    ckv_parts = grad_ckv.reshape(CROSS_KEYS, 2, 4, quarter).transpose(2, 0, 1, 3).reshape(4, CROSS_KEYS, 2 * quarter)
    ckv_parts = lax.all_to_all(ckv_parts, "x", split_axis=0, concat_axis=0, tiled=True)
    ckv_share = jnp.sum(ckv_parts.astype(f32), axis=0)[:cond_count].astype(bf16)
    grad_keyval = dot_tn(own_context, ckv_share).astype(bf16)
    cond_part = dot_nt(ckv_share, w_kv)
    cond_part = (cond_part + to_partner(cond_part)).astype(bf16)
    cond_rows = -(-cond_count // 4)
    cond_part = jnp.pad(cond_part, ((0, 4 * cond_rows - cond_count), (0, 0))).reshape(4, cond_rows, D)
    cond_part = lax.all_to_all(cond_part, "x", split_axis=0, concat_axis=0, tiled=True)
    cond_own = jnp.sum(cond_part.astype(f32), axis=0).astype(bf16)
    cond_all = sent_to_all(cond_own, CTX, 8).reshape(4, 2, cond_rows, D).transpose(1, 0, 2, 3)
    cond_grad = permuted(cond_all.reshape(2, 4 * cond_rows, D)[:, :cond_count]).astype(f32)

    full_back = gather_rows(grad_resid_one.astype(bf16))
    grad_att = dot(full_back, w_out).astype(bf16)
    sum_out = scatter_plane(jnp.concatenate([grad_keyval, dot_tn(full_back, attended).astype(bf16)], axis=1))
    grad_qkv = attn_backward(qs, ks, vs, grad_att, lse, cosine, sine)
    sum_proj = scatter_plane(dot_tn(full_one, grad_qkv).astype(bf16))
    grad_one = scatter_rows(dot_nt(grad_qkv, w_proj))
    in_grad = grad_resid_one + unit_norm_back(norm_one, scale_one, grad_one)

    def placed(rows):
        moved = lax.ppermute(permuted(rows.astype(bf16)), ("yh", "tp"), SWAP)
        return lax.all_gather(moved, "tp", axis=0, tiled=False)

    layer_out = placed(output)
    in_grad = placed(in_grad).astype(f32)

    row = jnp.arange(own_rows, dtype=jnp.int32)
    valid = ((2 * x + tp) * own_rows + row < length)[:, None]
    sums = jnp.stack(
        [jnp.sum(jnp.where(valid, v * v, 0.0)) for v in (tokens, attn_branch, cross_branch, feed_branch, output)]
    )
    sums = sent_to_all(jnp.pad(sums, (0, 123))[None], ("x", "yh", "tp"), 16).reshape(4, 2, 2, 128)
    sums = jnp.sum(sums, axis=(0, 2))[:, :5]
    layer_stats = jnp.sqrt(sums / (lengths.astype(f32)[:, None] * D))

    def collected(v):
        return sent_to_all(v, CTX, 8).reshape(4, 2, half_rows, v.shape[1]).transpose(1, 2, 0, 3).reshape(2 * half_rows, 4, v.shape[1])

    cross_parts = sum_cross.reshape(half_rows, 2, 4, quarter).transpose(2, 0, 1, 3).reshape(4, half_rows, 2 * quarter)
    cross_parts = lax.all_to_all(cross_parts, "x", split_axis=0, concat_axis=0, tiled=True)
    cross_share = jnp.sum(cross_parts.astype(f32), axis=0).astype(bf16)
    feed_all = collected(jnp.concatenate([sum_feed, sum_down], axis=1)).astype(f32)
    mid_all = collected(jnp.concatenate([cross_share, sum_out[:, : 3 * quarter]], axis=1)).astype(f32)
    proj_all = collected(jnp.concatenate([sum_proj[:, k * WIDE : k * WIDE + quarter] for k in range(3)], axis=1)).astype(f32)
    feed_all = feed_all.reshape(2 * half_rows, 4, 3, hidden_quarter).transpose(0, 2, 1, 3).reshape(2 * half_rows, 3, 4 * hidden_quarter)
    mid_all = mid_all.reshape(2 * half_rows, 4, 5, quarter).transpose(0, 2, 1, 3).reshape(2 * half_rows, 5, 4 * quarter)
    proj_all = proj_all.reshape(2 * half_rows, 4, 3, quarter).transpose(0, 2, 1, 3).reshape(2 * half_rows, 3, 4 * quarter)

    def gain_of(w, raw):
        return jnp.sum(w.astype(f32) * raw, axis=tuple(range(1, raw.ndim)))

    raw_feed, raw_cq = feed_all[:, :2], mid_all[:, 0]
    gains = jnp.stack([gain_of(self_proj, proj_all), gain_of(cross_query, raw_cq), gain_of(feed_in, raw_feed)])
    gains = gains + to_partner(gains)

    def by_gain(raw, gain):
        return raw * gain.astype(f32).reshape((-1,) + (1,) * (raw.ndim - 1))

    return (
        layer_out,
        in_grad,
        cond_grad,
        layer_stats,
        gains[0],
        by_gain(proj_all, gain_attn),
        mid_all[:, 4],
        gains[1],
        by_gain(raw_cq, gain_cross),
        mid_all[:, 2:4],
        mid_all[:, 1],
        gains[2],
        by_gain(raw_feed, gain_feed),
        feed_all[:, 2],
    )


def solution(mesh):
    fine = Mesh(mesh.devices.reshape(4, 2, 4, 2, 2), ("z", "yl", "x", "yh", "tp"))
    weights = (
        P(DP),
        P(DP, None, "tp"),
        P(DP, "tp"),
        P(DP),
        P(DP, "tp"),
        P(DP, None, "tp"),
        P(DP, "tp"),
        P(DP),
        P(DP, None, "tp"),
        P(DP, "tp"),
    )
    return jax.shard_map(
        per_device,
        mesh=fine,
        in_specs=(P(DP, CTX, None), P(DP, None, None), P(DP), P(DP, None), P(DP, CTX, None), *weights),
        out_specs=(P(DP, CTX, None), P(DP, CTX, None), P(DP, None, None), P(DP, None), *weights),
        check_vma=False,
    )
```

time: 3010 us -> 943 us (0.31)
  waiting for transfers between devices: 2250 us -> 399 us
  blocking collectives: 264 us -> 59.3 us
  starting transfers between devices: 36.5 us -> 105 us
  matrix products: 154 us -> 87.5 us
  local copies, waits for them, and re-layouts: 208 us -> 149 us
  Pallas kernels: 0 us -> 40.7 us
    all_gather x9 -> x4, waiting for transfers between devices: 989 us -> 19 us  [gather_plane(): return lax.all_gather(shard, PLANE, axis=0, tiled=True)]
    reduce_scatter x5 -> x3, waiting for transfers between devices: 693 us -> 95.2 us  [scatter_plane(): return lax.psum_scatter(grad, PLANE, scatter_dimension=0, tiled=True)]
    unnamed x30 -> x11, waiting for transfers between devices: 531 us -> 109 us
    unnamed x3 -> x0, blocking collectives: 139 us -> none
    all_to_all x2 -> x14, waiting for transfers between devices: 0.01 us -> 122 us  [the longest x4 70.8 us: scatter_rows(): lax.all_to_all(mine.reshape(4, ROWS, D), 'x', split_axis=0, concat_axis=0...]
    unnamed x236 -> x119, local copies, waits for them, and re-layouts: 128 us -> 27.7 us
    reshape x1 -> x19, local copies, waits for them, and re-layouts: 0.16 us -> 71.6 us  [the longest x3 32 us: per_device(): feed_all.reshape(2 * half_rows, 4, 3, hidden_quarter).transpose(0, 2, 1, 3)]
    dot_general x32 -> x21, matrix products: 152 us -> 87.5 us  [the longest x7 35.8 us: dot(): return jnp.dot(a, b, preferred_element_type=f32)]
  transfers between devices with their start and end apart: 27 -> 41, of which waited for: 18 -> 26; matrix products, arithmetic and copies ran while one was open for 13% -> 25% of each run, Pallas kernels for 0% -> 2%
where the time goes in v1:
time: 943 us; the launch traced here: 931 us
  waiting for transfers between devices  399 us (42%)
  local copies, waits for them, and re-layouts  149 us (16%)
  starting transfers between devices  105 us (11%)
  matrix products  87.5 us (9%)
  other arithmetic  74.7 us (8%)
  blocking collectives  59.3 us (6%)
  Pallas kernels  40.7 us (4%)
  between operations  15.5 us (2%)
    unnamed x11, waiting for transfers between devices  109 us
    reduce_scatter x3, waiting for transfers between devices, scatter_plane(): return lax.psum_scatter(grad, PLANE, scatter_dimension=0, tiled=True)  95.2 us
    all_to_all x4, waiting for transfers between devices, scatter_rows(): lax.all_to_all(mine.reshape(4, ROWS, D), 'x', split_axis=0, concat_axis=0...  70.8 us
    all_to_all x8, waiting for transfers between devices, sent_to_all(): return lax.all_to_all(copies, axes, split_axis=0, concat_axis=0, tiled=True)  46 us
    all_to_all x8, starting transfers between devices, sent_to_all(): return lax.all_to_all(copies, axes, split_axis=0, concat_axis=0, tiled=True)  39.6 us
    all_to_all x2, blocking collectives, sent_to_all(): return lax.all_to_all(copies, axes, split_axis=0, concat_axis=0, tiled=True)  39.3 us
    dot_general x7, matrix products, dot(): return jnp.dot(a, b, preferred_element_type=f32)  35.8 us
    reshape x3, local copies, waits for them, and re-layouts, per_device(): feed_all.reshape(2 * half_rows, 4, 3, hidden_quarter).transpose(0, 2, 1, 3)  32 us
  transfers between devices with their start and end apart: 41, of which 26 were waited for; matrix products, arithmetic and copies ran while one was open for 25% of the time, Pallas kernels for 2%

profile of v1, /device:TPU:1, one launch (start us, length us, event | category | flops | bytes accessed | tf_op | source)
XLA Modules:
  0.0 930.6 jit_solution(11345731502075814119)
XLA Ops:
  16.5 6.2 collective-permute-start
  22.7 5.8 collective-permute-done
  30.1 16.4 %all_to_all.85 = bf16[4,128,1536]{2,1,0:T(8,128)(2,1)S(1)} all-to-all(bf16[4,128,1536]{2,1,0:T(8,128)(2,1)S(1)} %broadcast_in_dim.155), channel_id=1, replica_groups=mesh['z'=4,'yl'=2,'x'=4,'yh'=2,'tp'=2] {'x'}, dimensions={0} | all-to-all | bytes 3145728 | tf_op jit(solution)/shard_map/all_to_all | solution.py:56
  51.2 5.6 fusion.32
  56.8 6.3 all-gather.7.cloned.1.call-done
  63.1 6.4 fusion.14.qkv
  69.5 13.6 %shard_map.254 = (bf16[1024,256]{1,0:T(8,128)(2,1)}, bf16[1024,256]{1,0:T(8,128)(2,1)}, bf16[1024,256]{1,0:T(8,128)(2,1)}, bf16[1024,256]{1,0:T(8,128)(2,1)}, f32[8,1024]{1,0:T(8,128)}) custom-call(s32[2]{0:T(128)} %pad_add_fusion.sc, f32[1024,768]{1,0:T(8,128)} %fusion.14.qkv, f32[1024,256]{1,0:T(8,128)} %get-tuple-element.243.cosine, ...), custom_call_target="tpu_custom_call" | custom-call | flops 3221225472 | bytes 8388608 | tf_op jit(solution)/shard_map/pallas_call | solution.py:157
  97.0 19.4 %all-to-all-done.1 = bf16[4,128,1536]{2,1,0:T(8,128)(2,1)} async-done(((bf16[4,128,1536]{2,1,0:T(8,128)(2,1)}), bf16[4,128,1536]{2,1,0:T(8,128)(2,1)}, u32[]{:S(2)}, u32[]{:S(2)}) %all-to-all-start.1) | async-done | bytes 1572896 | tf_op jit(solution)/shard_map/all_to_all | solution.py:68
  169.1 14.3 %collective-permute-done.8 = bf16[128,1536]{1,0:T(8,128)(2,1)S(1)} collective-permute-done((bf16[128,1536]{1,0:T(8,128)(2,1)S(1)}, bf16[128,1536]{1,0:T(8,128)(2,1)S(1)}, u32[]{:S(2)}, u32[]{:S(2)}) %collective-permute-start.8) | collective-permute-done | bytes 393248 | tf_op jit(solution)/shard_map/ppermute | solution.py:326
  191.1 21.2 %all-to-all-done.5 = bf16[4,128,1536]{2,1,0:T(8,128)(2,1)} async-done(((bf16[4,128,1536]{2,1,0:T(8,128)(2,1)}), bf16[4,128,1536]{2,1,0:T(8,128)(2,1)}, u32[]{:S(2)}, u32[]{:S(2)}) %all-to-all-start.5) | async-done | bytes 1572896 | tf_op jit(solution)/shard_map/all_to_all | solution.py:56
  213.1 9.6 %fusion.19 = f32[1024,1536]{1,0:T(8,128)} fusion(bf16[1536,1536]{1,0:T(8,128)(2,1)} %all-gather.11.cloned.1.call-done, bf16[512,1536]{1,0:T(8,128)(2,1)} %collective-permute-done.5, bf16[512,1536]{1,0:T(8,128)(2,1)} %bitcast.6), kind=kOutput, calls=%fused_computation.55 | convolution fusion | flops 4838129664 | bytes 14155776 | tf_op jit(solution)/shard_map/dot_general | solution.py:39
  222.7 9.4 %all-gather.13.cloned.1.call-done = bf16[1536,768]{1,0:T(8,128)(2,1)} async-done(((bf16[96,768]{1,0:T(8,128)(2,1)}), bf16[1536,768]{1,0:T(8,128)(2,1)}) %all-gather.13.cloned.1.call-update) | async-done | bytes 2359312 | tf_op jit(solution)/shard_map/all_gather | solution.py:81
  232.2 7.9 multiply_convert_fusion.1
  241.3 7.4 fusion.17
  266.0 16.3 %all-to-all-done.6 = bf16[4,128,1536]{2,1,0:T(8,128)(2,1)} async-done(((bf16[4,128,1536]{2,1,0:T(8,128)(2,1)}), bf16[4,128,1536]{2,1,0:T(8,128)(2,1)}, u32[]{:S(2)}, u32[]{:S(2)}) %all-to-all-start.6) | async-done | bytes 1572896 | tf_op jit(solution)/shard_map/all_to_all | solution.py:68
  290.3 15.7 %all-to-all-done.4 = bf16[4,128,1536]{2,1,0:T(8,128)(2,1)} async-done(((bf16[4,128,1536]{2,1,0:T(8,128)(2,1)}), bf16[4,128,1536]{2,1,0:T(8,128)(2,1)}, u32[]{:S(2)}, u32[]{:S(2)}) %all-to-all-start.4) | async-done | bytes 1572896 | tf_op jit(solution)/shard_map/all_to_all | solution.py:68
  318.9 5.8 shard_map.256
  331.4 22.9 %all_to_all.86 = bf16[4,128,1536]{2,1,0:T(8,128)(2,1)S(1)} all-to-all(bf16[4,128,1536]{2,1,0:T(8,128)(2,1)S(1)} %broadcast_in_dim.169), channel_id=1, replica_groups=mesh['z'=4,'yl'=2,'x'=4,'yh'=2,'tp'=2] {'x'}, dimensions={0} | all-to-all | bytes 3145728 | tf_op jit(solution)/shard_map/all_to_all | solution.py:56
  362.0 16.8 %shard_map.257 = bf16[1024,768]{1,0:T(8,128)(2,1)} custom-call(bf16[1024,256]{1,0:T(8,128)(2,1)} %get-tuple-element.23.qs, bf16[1024,256]{1,0:T(8,128)(2,1)} %get-tuple-element.24.ks, bf16[1024,256]{1,0:T(8,128)(2,1)} %get-tuple-element.25.vs, bf16[1024,256]{1,0:T(8,128)(2,1)} %fusion.20.grad, f32[8,1024]{1,0:T(8,128)} %get-tuple-element.26.lse, ...), custom_call_target="tpu_custom_call" | custom-call | flops 8053063680 | bytes 8388608 | tf_op jit(solution)/shard_map/pallas_call | solution.py:203
  378.8 6.0 convolution_convert_fusion.2
  384.9 6.5 convolution_convert_fusion.1
  391.9 8.9 convolution_convert_fusion
  403.1 10.4 %all_to_all.87 = bf16[4,144,384]{2,1,0:T(8,128)(2,1)S(1)} all-to-all(bf16[4,144,384]{2,1,0:T(8,128)(2,1)S(1)} %reshape.434), channel_id=1, replica_groups=mesh['z'=4,'yl'=2,'x'=4,'yh'=2,'tp'=2] {'x'}, dimensions={0} | all-to-all | bytes 884736 | tf_op jit(solution)/shard_map/all_to_all | solution.py:396
  428.1 6.6 copy.150
  464.5 19.4 %all-to-all-done.8 = bf16[4,128,1536]{2,1,0:T(8,128)(2,1)S(1)} async-done(((bf16[4,128,1536]{2,1,0:T(8,128)(2,1)}), bf16[4,128,1536]{2,1,0:T(8,128)(2,1)S(1)}, u32[]{:S(2)}, u32[]{:S(2)}) %all-to-all-start.8) | async-done | bytes 1572896 | tf_op jit(solution)/shard_map/all_to_all | solution.py:68
  496.0 7.1 all-to-all-done.11
  503.7 7.2 all-to-all-start.12
  511.0 6.8 all-to-all-done.12
  522.9 5.6 collective-permute-start.7
  531.2 15.1 %reduce-scatter.14.cloned.1.call-done = bf16[96,768]{1,0:T(8,128)(2,1)} async-done(((bf16[1536,768]{1,0:T(8,128)(2,1)}), bf16[96,768]{1,0:T(8,128)(2,1)}) %reduce-scatter.14.cloned.1.call-update) | async-done | bytes 147472 | tf_op jit(solution)/shard_map/reduce_scatter | solution.py:85
  546.2 80.1 %reduce-scatter.12.cloned.1.call-done = bf16[96,1536]{1,0:T(8,128)(2,1)} async-done(((bf16[1536,1536]{1,0:T(8,128)(2,1)}), bf16[96,1536]{1,0:T(8,128)(2,1)}) %reduce-scatter.12.cloned.1.call-update) | async-done | bytes 294928 | tf_op jit(solution)/shard_map/reduce_scatter | solution.py:85
  629.6 5.6 all-to-all-start.16
  635.2 7.0 all-gather
  652.3 6.6 concatenate.84
  661.3 22.6 %collective-permute-done.15 = bf16[128,1536]{1,0:T(8,128)(2,1)} collective-permute-done((bf16[128,1536]{1,0:T(8,128)(2,1)S(1)}, bf16[128,1536]{1,0:T(8,128)(2,1)}, u32[]{:S(2)}, u32[]{:S(2)}) %collective-permute-start.15) | collective-permute-done | bytes 393248 | tf_op jit(solution)/shard_map/ppermute | solution.py:417
  687.8 44.2 %reduce-scatter.18.cloned.1.call-done = bf16[96,640]{1,0:T(8,128)(2,1)} async-done(((bf16[1536,640]{1,0:T(8,128)(2,1)}), bf16[96,640]{1,0:T(8,128)(2,1)}) %reduce-scatter.18.cloned.1.call-update) | async-done | bytes 122896
  748.9 64.6 %reduce-scatter.16.cloned.1.call-done = bf16[96,1536]{1,0:T(8,128)(2,1)} async-done(((bf16[1536,1536]{1,0:T(8,128)(2,1)}), bf16[96,1536]{1,0:T(8,128)(2,1)}) %reduce-scatter.16.cloned.1.call-update) | async-done | bytes 294928
  820.3 5.5 convert_bitcast_fusion
  825.8 11.5 %reshape.461 = f32[192,4,3,768]{3,2,0,1:T(4,128)} reshape(f32[2,96,4,2304]{3,1,0,2:T(8,128)} %convert_bitcast_fusion) | data formatting | bytes 14155776 | tf_op jit(solution)/shard_map/reshape | solution.py:441
  837.3 11.1 %copy.144 = f32[192,3,4,768]{3,2,0,1:T(4,128)} copy(f32[192,3,4,768]{3,1,0,2:T(4,128)} %bitcast.107) | data formatting | bytes 14155776 | tf_op jit(solution)/shard_map/reshape | solution.py:441
  848.4 9.4 %reshape.452 = f32[192,3,3072]{2,0,1:T(8,128)} reshape(f32[192,3,4,768]{3,2,0,1:T(4,128)} %copy.144) | data formatting | bytes 14155776 | tf_op jit(solution)/shard_map/reshape | solution.py:441
  859.7 6.3 all-to-all-start.15
  870.2 5.8 copy.146
  879.3 6.9 all-to-all-done.15
  888.3 6.9 copy.141
  895.2 5.7 reshape.459
  900.8 6.4 copy.142
  907.2 5.4 reshape.450
  (348 shorter events, 276.8 us)
Async XLA Ops:
  7.2 88.7 %copy-start = (bf16[2,130,1536]{2,0,1:T(2,128)(2,1)S(1)}, bf16[2,130,1536]{2,0,1:T(2,128)(2,1)}, u32[]{:S(2)}) copy-start(bf16[2,130,1536]{2,0,1:T(2,128)(2,1)} %param.16) | copy-start | bytes 2396164
  7.2 55.9 %all-gather.7.cloned.1.call-start = ((), (), s32[]{:S(2)}) async-start(), calls=%async_computation.22 | async-start | bytes 3342336 | tf_op jit(solution)/shard_map/all_gather | solution.py:81
  11.7 112.8 %all-gather.9.cloned.1.call-start = ((), (), s32[]{:S(2)}) async-start(), calls=%async_computation.23 | async-start | bytes 6266880 | tf_op jit(solution)/shard_map/all_gather | solution.py:81
  16.4 196.7 %all-gather.11.cloned.1.call-start = ((), (), s32[]{:S(2)}) async-start(), calls=%async_computation.24 | async-start | bytes 5013504 | tf_op jit(solution)/shard_map/all_gather | solution.py:81
  16.5 12.0 %collective-permute-start = (bf16[128,1536]{1,0:T(8,128)(2,1)S(1)}, bf16[128,1536]{1,0:T(8,128)(2,1)S(1)}, u32[]{:S(2)}, u32[]{:S(2)}) collective-permute-start(bf16[128,1536]{1,0:T(8,128)(2,1)S(1)} %dynamic-slice_bitcast_fusion.1), channel_id=1, source_target_pairs={{0,0},{1,2},{2,1},{3,3},{4,4},{5,6},{6,5},{7,7},{8,8},{9,10},{10,9... | collective-permute-start | bytes 1179656 | tf_op jit(solution)/shard_map/ppermute | solution.py:325
  46.5 10.3 %collective-permute-start.1 = (bf16[512,1536]{1,0:T(8,128)(2,1)S(1)}, bf16[512,1536]{1,0:T(8,128)(2,1)}, u32[]{:S(2)}, u32[]{:S(2)}) collective-permute-start(bf16[512,1536]{1,0:T(8,128)(2,1)S(1)} %bitcast.123), channel_id=1, source_target_pairs={{0,1},{1,0},{2,3},{3,2},{4,5},{5,4},{6,7},{7,6},{8,9},{9,8},{10,11... | collective-permute-start | bytes 4718600 | tf_op jit(solution)/shard_map/ppermute | solution.py:51
  85.6 4.1 collective-permute-start.2
  91.3 25.1 %all-to-all-start.1 = ((bf16[4,128,1536]{2,1,0:T(8,128)(2,1)}), bf16[4,128,1536]{2,1,0:T(8,128)(2,1)}, u32[]{:S(2)}, u32[]{:S(2)}) async-start(bf16[4,128,1536]{2,1,0:T(8,128)(2,1)} %bitcast.3), calls=%async_computation.1 | async-start | bytes 3145728 | tf_op jit(solution)/shard_map/all_to_all | solution.py:68
  119.5 11.5 %collective-permute-start.3 = (bf16[128,1536]{1,0:T(8,128)(2,1)}, bf16[128,1536]{1,0:T(8,128)(2,1)}, u32[]{:S(2)}, u32[]{:S(2)}) collective-permute-start(bf16[128,1536]{1,0:T(8,128)(2,1)} %fusion.52), channel_id=1, source_target_pairs={{0,1},{1,0},{2,3},{3,2},{4,5},{5,4},{6,7},{7,6},{8,9},{9,8},{10,11... | collective-permute-start | bytes 1179656 | tf_op jit(solution)/shard_map/ppermute | solution.py:51
  127.0 11.4 %all-to-all-start.2 = ((bf16[4,144,384]{2,1,0:T(8,128)(2,1)}), bf16[4,144,384]{2,1,0:T(8,128)(2,1)S(1)}, u32[]{:S(2)}, u32[]{:S(2)}) async-start(bf16[4,144,384]{2,1,0:T(8,128)(2,1)} %broadcast_in_dim.163), calls=%async_computation.2 | async-start | bytes 884736 | tf_op jit(solution)/shard_map/all_to_all | solution.py:56
  131.0 101.2 %all-gather.13.cloned.1.call-start = ((), (), s32[]{:S(2)}) async-start(), calls=%async_computation.25 | async-start | bytes 2506752 | tf_op jit(solution)/shard_map/all_gather | solution.py:81
  151.3 4.1 collective-permute-start.4
  158.7 26.6 %all-to-all-start.3 = ((bf16[4,128,1536]{2,1,0:T(8,128)(2,1)}), bf16[4,128,1536]{2,1,0:T(8,128)(2,1)}, u32[]{:S(2)}, u32[]{:S(2)}) async-start(bf16[4,128,1536]{2,1,0:T(8,128)(2,1)} %broadcast_in_dim.167), calls=%async_computation.3 | async-start | bytes 3145728 | tf_op jit(solution)/shard_map/all_to_all | solution.py:56
  164.2 19.2 %collective-permute-start.8 = (bf16[128,1536]{1,0:T(8,128)(2,1)S(1)}, bf16[128,1536]{1,0:T(8,128)(2,1)S(1)}, u32[]{:S(2)}, u32[]{:S(2)}) collective-permute-start(bf16[128,1536]{1,0:T(8,128)(2,1)S(1)} %dynamic-slice_bitcast_fusion), channel_id=1, source_target_pairs={{0,0},{1,2},{2,1},{3,3},{4,4},{5,6},{6,5},{7,7},{8,8},{9,10},{10,9... | collective-permute-start | bytes 1179656 | tf_op jit(solution)/shard_map/ppermute | solution.py:326
  185.3 37.4 %copy-start.6 = (bf16[128,1536]{1,0:T(8,128)(2,1)}, bf16[128,1536]{1,0:T(8,128)(2,1)S(1)}, u32[]{:S(2)}) copy-start(bf16[128,1536]{1,0:T(8,128)(2,1)S(1)} %concatenate.78) | copy-start | bytes 1179652
  186.6 25.7 %all-to-all-start.5 = ((bf16[4,128,1536]{2,1,0:T(8,128)(2,1)}), bf16[4,128,1536]{2,1,0:T(8,128)(2,1)}, u32[]{:S(2)}, u32[]{:S(2)}) async-start(bf16[4,128,1536]{2,1,0:T(8,128)(2,1)} %broadcast_in_dim.168), calls=%async_computation.5 | async-start | bytes 3145728 | tf_op jit(solution)/shard_map/all_to_all | solution.py:56
  191.0 22.1 %collective-permute-start.5 = (bf16[512,1536]{1,0:T(8,128)(2,1)}, bf16[512,1536]{1,0:T(8,128)(2,1)}, u32[]{:S(2)}, u32[]{:S(2)}) collective-permute-start(bf16[512,1536]{1,0:T(8,128)(2,1)} %bitcast.6), channel_id=1, source_target_pairs={{0,1},{1,0},{2,3},{3,2},{4,5},{5,4},{6,7},{7,6},{8,9},{9,8},{10,11... | collective-permute-start | bytes 4718600 | tf_op jit(solution)/shard_map/ppermute | solution.py:51
  212.3 10.5 %collective-permute-start.9 = (bf16[512,1536]{1,0:T(8,128)(2,1)}, bf16[512,1536]{1,0:T(8,128)(2,1)}, u32[]{:S(2)}, u32[]{:S(2)}) collective-permute-start(bf16[512,1536]{1,0:T(8,128)(2,1)} %bitcast.10), channel_id=1, source_target_pairs={{0,1},{1,0},{2,3},{3,2},{4,5},{5,4},{6,7},{7,6},{8,9},{9,8},{10,11... | collective-permute-start | bytes 4718600 | tf_op jit(solution)/shard_map/ppermute | solution.py:51
  248.9 7.2 collective-permute-start.10
  254.7 7.4 collective-permute-start.6
  257.7 24.6 %all-to-all-start.6 = ((bf16[4,128,1536]{2,1,0:T(8,128)(2,1)}), bf16[4,128,1536]{2,1,0:T(8,128)(2,1)}, u32[]{:S(2)}, u32[]{:S(2)}) async-start(bf16[4,128,1536]{2,1,0:T(8,128)(2,1)} %bitcast.112), calls=%async_computation.6 | async-start | bytes 3145728 | tf_op jit(solution)/shard_map/all_to_all | solution.py:68
  282.3 23.7 %all-to-all-start.4 = ((bf16[4,128,1536]{2,1,0:T(8,128)(2,1)}), bf16[4,128,1536]{2,1,0:T(8,128)(2,1)}, u32[]{:S(2)}, u32[]{:S(2)}) async-start(bf16[4,128,1536]{2,1,0:T(8,128)(2,1)} %bitcast.110), calls=%async_computation.4 | async-start | bytes 3145728 | tf_op jit(solution)/shard_map/all_to_all | solution.py:68
  286.7 208.4 %reduce-scatter.10.cloned.1.call-start = ((), (), s32[]{:S(2)}) async-start(), calls=%async_computation.26 | async-start | bytes 2506752 | tf_op jit(solution)/shard_map/reduce_scatter | solution.py:85
  311.5 4.0 collective-permute-start.11
  327.3 2.4 collective-permute-start.12
  354.3 4.2 collective-permute-start.13
  384.8 161.4 %reduce-scatter.14.cloned.1.call-start = ((), (), s32[]{:S(2)}) async-start(), calls=%async_computation.28 | async-start | bytes 2506752 | tf_op jit(solution)/shard_map/reduce_scatter | solution.py:85
  391.4 234.9 %reduce-scatter.12.cloned.1.call-start = ((), (), s32[]{:S(2)}) async-start(), calls=%async_computation.27 | async-start | bytes 5013504 | tf_op jit(solution)/shard_map/reduce_scatter | solution.py:85
  400.8 331.2 %reduce-scatter.18.cloned.1.call-start = ((), (), s32[]{:S(2)}) async-start(), calls=%async_computation.30 | async-start | bytes 2088960
  422.7 390.9 %reduce-scatter.16.cloned.1.call-start = ((), (), s32[]{:S(2)}) async-start(), calls=%async_computation.29 | async-start | bytes 5013504
  440.6 11.1 %collective-permute-start.14 = (bf16[512,1536]{1,0:T(8,128)(2,1)S(1)}, bf16[512,1536]{1,0:T(8,128)(2,1)}, u32[]{:S(2)}, u32[]{:S(2)}) collective-permute-start(bf16[512,1536]{1,0:T(8,128)(2,1)S(1)} %slice.705), channel_id=1, source_target_pairs={{0,1},{1,0},{2,3},{3,2},{4,5},{5,4},{6,7},{7,6},{8,9},{9,8},{10,11... | collective-permute-start | bytes 4718600 | tf_op jit(solution)/shard_map/ppermute | solution.py:51
  444.4 2.7 collective-permute-start.16
  448.2 12.3 %all-to-all-start.10 = ((bf16[4,33,1536]{2,1,0:T(8,128)(2,1)}), bf16[4,33,1536]{2,1,0:T(8,128)(2,1)S(1)}, u32[]{:S(2)}, u32[]{:S(2)}) async-start(bf16[4,33,1536]{2,1,0:T(8,128)(2,1)} %reshape.435), calls=%async_computation.10 | async-start | bytes 983040 | tf_op jit(solution)/shard_map/all_to_all | solution.py:403
  460.5 23.4 %all-to-all-start.8 = ((bf16[4,128,1536]{2,1,0:T(8,128)(2,1)}), bf16[4,128,1536]{2,1,0:T(8,128)(2,1)S(1)}, u32[]{:S(2)}, u32[]{:S(2)}) async-start(bf16[4,128,1536]{2,1,0:T(8,128)(2,1)} %bitcast.113), calls=%async_computation.8 | async-start | bytes 3145728 | tf_op jit(solution)/shard_map/all_to_all | solution.py:68
  484.9 18.2 %all-to-all-start.11 = ((bf16[8,33,1536]{2,1,0:T(8,128)(2,1)}), bf16[8,33,1536]{2,1,0:T(8,128)(2,1)}, u32[]{:S(2)}, u32[]{:S(2)}) async-start(bf16[8,33,1536]{2,1,0:T(8,128)(2,1)} %broadcast_in_dim.170), calls=%async_computation.11 | async-start | bytes 1966080 | tf_op jit(solution)/shard_map/all_to_all | solution.py:56
  490.9 31.7 %copy-start.30 = (bf16[128,96]{1,0:T(8,128)(2,1)S(1)}, bf16[128,96]{1,0:T(8,128)(2,1)}, u32[]{:S(2)}) copy-start(bf16[128,96]{1,0:T(8,128)(2,1)} %get-tuple-element.219) | copy-start | bytes 73732
  490.9 31.7 %copy-start.31 = (bf16[128,96]{1,0:T(8,128)(2,1)S(1)}, bf16[128,96]{1,0:T(8,128)(2,1)}, u32[]{:S(2)}) copy-start(bf16[128,96]{1,0:T(8,128)(2,1)} %get-tuple-element.220) | copy-start | bytes 73732
  490.9 31.7 %copy-start.32 = (bf16[128,96]{1,0:T(8,128)(2,1)S(1)}, bf16[128,96]{1,0:T(8,128)(2,1)}, u32[]{:S(2)}) copy-start(bf16[128,96]{1,0:T(8,128)(2,1)} %get-tuple-element.221) | copy-start | bytes 73732
  490.9 31.7 %copy-start.33 = (bf16[128,96]{1,0:T(8,128)(2,1)S(1)}, bf16[128,96]{1,0:T(8,128)(2,1)}, u32[]{:S(2)}) copy-start(bf16[128,96]{1,0:T(8,128)(2,1)} %get-tuple-element.222) | copy-start | bytes 73732
  503.7 14.1 %all-to-all-start.12 = ((f32[16,1,128]{2,1,0:T(1,128)}), f32[16,1,128]{2,1,0:T(1,128)S(1)}, u32[]{:S(2)}, u32[]{:S(2)}) async-start(f32[16,1,128]{2,1,0:T(1,128)} %broadcast_in_dim.173), calls=%async_computation.12 | async-start | bytes 16384 | tf_op jit(solution)/shard_map/all_to_all | solution.py:56
  518.8 108.6 %all-to-all-start.13 = ((bf16[8,96,576]{2,1,0:T(8,128)(2,1)}), bf16[8,96,576]{2,1,0:T(8,128)(2,1)S(1)}, u32[]{:S(2)}, u32[]{:S(2)}) async-start(bf16[8,96,576]{2,1,0:T(8,128)(2,1)} %broadcast_in_dim.174), calls=%async_computation.14 | async-start | bytes 1966080 | tf_op jit(solution)/shard_map/all_to_all | solution.py:56
  522.9 112.3 %collective-permute-start.7 = (bf16[128,1536]{1,0:T(8,128)(2,1)S(1)}, bf16[128,1536]{1,0:T(8,128)(2,1)}, u32[]{:S(2)}, u32[]{:S(2)}) collective-permute-start(bf16[128,1536]{1,0:T(8,128)(2,1)S(1)} %concatenate.77), channel_id=1, source_target_pairs={{0,0},{1,2},{2,1},{3,3},{4,4},{5,6},{6,5},{7,7},{8,8},{9,10},{10,9... | collective-permute-start | bytes 1179656 | tf_op jit(solution)/shard_map/ppermute | solution.py:417
  629.6 186.5 %all-to-all-start.16 = ((bf16[8,96,2304]{2,1,0:T(8,128)(2,1)}), bf16[8,96,2304]{2,1,0:T(8,128)(2,1)}, u32[]{:S(2)}, u32[]{:S(2)}) async-start(bf16[8,96,2304]{2,1,0:T(8,128)(2,1)} %broadcast_in_dim.176), calls=%async_computation.19 | async-start | bytes 7077888 | tf_op jit(solution)/shard_map/all_to_all | solution.py:56
  646.5 37.5 %collective-permute-start.15 = (bf16[128,1536]{1,0:T(8,128)(2,1)S(1)}, bf16[128,1536]{1,0:T(8,128)(2,1)}, u32[]{:S(2)}, u32[]{:S(2)}) collective-permute-start(bf16[128,1536]{1,0:T(8,128)(2,1)S(1)} %concatenate.83), channel_id=1, source_target_pairs={{0,0},{1,2},{2,1},{3,3},{4,4},{5,6},{6,5},{7,7},{8,8},{9,10},{10,9... | collective-permute-start | bytes 1179656 | tf_op jit(solution)/shard_map/ppermute | solution.py:417
  659.0 74.1 %copy-start.3 = (bf16[8,96,576]{2,1,0:T(8,128)(2,1)S(1)}, bf16[8,96,576]{2,1,0:T(8,128)(2,1)}, u32[]{:S(2)}) copy-start(bf16[8,96,576]{2,1,0:T(8,128)(2,1)} %copy-done.2) | copy-start | bytes 2654212
  816.1 41.7 %all-to-all-start.14 = ((bf16[4,96,384]{2,1,0:T(8,128)(2,1)}), bf16[4,96,384]{2,1,0:T(8,128)(2,1)S(1)}, u32[]{:S(2)}, u32[]{:S(2)}) async-start(bf16[4,96,384]{2,1,0:T(8,128)(2,1)} %reshape.442), calls=%async_computation.15 | async-start | bytes 589824 | tf_op jit(solution)/shard_map/all_to_all | solution.py:436
  859.7 26.6 %all-to-all-start.15 = ((bf16[8,96,960]{2,1,0:T(8,128)(2,1)}), bf16[8,96,960]{2,1,0:T(8,128)(2,1)S(1)}, u32[]{:S(2)}, u32[]{:S(2)}) async-start(bf16[8,96,960]{2,1,0:T(8,128)(2,1)} %broadcast_in_dim.175), calls=%async_computation.16 | async-start | bytes 3145728 | tf_op jit(solution)/shard_map/all_to_all | solution.py:56
  914.8 7.3 collective-permute-start.17
  (48 other events, 447.7 us)
Sparse Core Ops, SparseCore 0:
  11.8 51.2 all-gather.6
  65.8 58.6 all-gather.8
  127.2 57.6 all-gather.10
  187.5 44.6 all-gather.12
  384.9 70.6 reduce-scatter.9
  459.4 86.8 reduce-scatter.13
  550.2 76.1 reduce-scatter.11
  629.6 102.3 reduce-scatter.17
  735.8 77.7 reduce-scatter.15

commit v2 on v1

v2 whole, which is shorter than its diff:
```python
import jax
import jax.numpy as jnp
from jax import lax
from jax.experimental import pallas as pl
from jax.experimental.pallas import tpu as pltpu
from jax.sharding import Mesh
from jax.sharding import PartitionSpec as P

DP = ("z", "yl")
CTX = ("x", "yh")
PLANE = ("z", "yh", "yl")
SWAP = ((0, 0), (1, 2), (2, 1), (3, 3))

D = 1536
HD = 64
ROT = 32
HEADS = 3
WIDE = 256
V_AT, K_AT, O_AT, QVK = 128, 384, 512, 640
ROWS = 128
SEQ = 1024
QB = 256
CROSS_KEYS = 144
norm_eps = 1e-05
masked_fill = -1e30
bf16 = jnp.bfloat16
f32 = jnp.float32


def permuted(v):
    parts = []
    for z in range(v.shape[-1] // 384):
        for piece in (0, 2, 1, 3):
            at = z * 384 + piece * 96
            parts.append(v[..., at : at + 96])
    return jnp.concatenate(parts, axis=-1)


def dot(a, b):
    return jnp.dot(a, b, preferred_element_type=f32)


def dot_nt(a, b):
    return lax.dot_general(a, b, (((1,), (1,)), ((), ())), preferred_element_type=f32)


def dot_tn(a, b):
    return lax.dot_general(a, b, (((0,), (0,)), ((), ())), preferred_element_type=f32)


def to_partner(v):
    return lax.ppermute(v, "tp", ((0, 1), (1, 0)))


def exchanged(v, axes):
    return lax.all_to_all(v, axes, split_axis=0, concat_axis=0, tiled=True)


def sent_to_all(v, axes, count):
    return exchanged(jnp.broadcast_to(v[None], (count, *v.shape)), axes)


def after(values, *others):
    return lax.optimization_barrier((values, others))[0]


def both(first, *others):
    return lax.optimization_barrier((first, *others))


def along_x(v, step):
    return lax.ppermute(v, "x", [(i, (i + step) % 4) for i in range(4)])


def gather_x(own):
    return [own] + [along_x(own, step) for step in (1, 2, 3)]


def scatter_x(blocks):
    return [blocks[0]] + [along_x(blocks[step], -step) for step in (1, 2, 3)]


def swapped_x(blocks):
    return [blocks[0]] + [along_x(blocks[step], step) for step in (1, 2, 3)]


def summed(blocks):
    return sum(block.astype(f32) for block in blocks[1:]) + blocks[0].astype(f32)


def gather_half(own):
    return jnp.concatenate(gather_x(own), axis=0)


def to_far(v):
    return lax.ppermute(v, "yh", ((0, 1), (1, 0)))


def with_partner(mine):
    return jnp.concatenate([mine, to_partner(mine)], axis=0)


def scatter_half(partial):
    half = 4 * ROWS
    got = to_partner(partial[half:].astype(bf16))
    mine = (partial[:half].astype(f32) + got.astype(f32)).astype(bf16)
    return [mine[k * ROWS : (k + 1) * ROWS] for k in range(4)]


def plane_parts(grad):
    return exchanged(grad.astype(bf16).reshape(16, grad.shape[0] // 16, grad.shape[1]), PLANE)


def total(parts):
    return jnp.sum(parts.astype(f32), axis=0)


def pair_rows(own):
    return jnp.concatenate([own, to_partner(own)], axis=0)


def pair_sum(partial):
    return partial[:ROWS] + to_partner(partial[ROWS:])


def gather_plane(shard):
    return lax.all_gather(shard, PLANE, axis=0, tiled=True)


def scatter_plane(grad):
    return lax.psum_scatter(grad, PLANE, scatter_dimension=0, tiled=True)


def unit_norm(v):
    centered = v - jnp.mean(v, axis=-1, keepdims=True)
    scale = lax.rsqrt(jnp.mean(centered * centered, axis=-1, keepdims=True) + norm_eps)
    return centered * scale, scale


def unit_norm_back(x_hat, scale, grad):
    along = jnp.mean(grad * x_hat, axis=-1, keepdims=True)
    return scale * (grad - jnp.mean(grad, axis=-1, keepdims=True) - x_hat * along)


def lane_masks(rows):
    lane = lax.broadcasted_iota(jnp.int32, (rows, WIDE), 1)
    heads = [(lane // HD == h).astype(f32).astype(bf16) for h in range(HEADS + 1)]
    return lane, heads, (lane == HEADS * HD).astype(f32).astype(bf16)


def turned(v, cosine, sine, first):
    other = jnp.where(first, pltpu.roll(v, WIDE - ROT // 2, 1), pltpu.roll(v, ROT // 2, 1))
    cosine, sine = (jnp.concatenate([table, table], axis=1) for table in (cosine, sine))
    return v * cosine, other * sine


def attn_forward_kernel(sc, qkv, cosine, sine, att, qs, ks, vs, lse, vt):
    lane, heads, extra = lane_masks(QB)
    first = lane % HD < ROT // 2
    value_head = lax.broadcasted_iota(jnp.int32, (WIDE, QB), 0) // HD - 1

    def prepare(block, carry):
        rows = pl.ds(block * QB, QB)
        c, s = cosine[rows, :], sine[rows, :]
        straight, crossed = turned(qkv[rows, 0:WIDE], c, s, first)
        query = ((straight + crossed) * HD ** (-0.5)).astype(bf16)
        qs[rows, :] = jnp.where(lane < HEADS * HD, query.astype(f32), jnp.where(lane == HEADS * HD, 1.0, 0.0)).astype(bf16)
        straight, crossed = turned(qkv[rows, K_AT : K_AT + WIDE], c, s, first)
        row = lax.broadcasted_iota(jnp.int32, (QB, WIDE), 0) + block * QB
        side = jnp.where(row < SEQ // 2, sc[0], 1 - sc[0])
        within = row % (SEQ // 2)
        place = ((sc[2] + 4 - within // ROWS) % 4 * 2 + side) * ROWS + within % ROWS
        fill = jnp.where((lane == HEADS * HD) & (place >= sc[1]), masked_fill, 0.0)
        ks[rows, :] = jnp.where(lane < HEADS * HD, straight + crossed, fill).astype(bf16)
        value = qkv[rows, V_AT : V_AT + WIDE]
        vs[rows, :] = value.astype(bf16)
        vt[:, rows] = value.T.astype(bf16)
        return carry

    for block in range(SEQ // QB):
        prepare(block, 0)

    def attend(block, carry):
        rows = pl.ds(pl.multiple_of(block * QB, QB), QB)
        query = qs[rows, :]
        total = jnp.zeros((WIDE, QB), f32)
        for h in range(HEADS):
            scores = dot_nt(ks[...], query * (heads[h] + extra))
            top = jnp.max(scores, axis=0, keepdims=True)
            weight = jnp.exp(scores - top)
            mass = jnp.sum(weight, axis=0, keepdims=True)
            out = dot(vt[...], weight.astype(bf16))
            total = jnp.where(value_head == h, out / mass, total)
            lse[h : h + 1, rows] = top + jnp.log(mass)
        att[rows, :] = total.T.astype(bf16)
        return carry

    lse[...] = jnp.zeros(lse.shape, f32)
    lax.fori_loop(0, SEQ // QB, attend, 0)


def attn_forward(scalars, qkv, cosine, sine):
    wide = jax.ShapeDtypeStruct((SEQ, WIDE), bf16)
    return pl.pallas_call(
        attn_forward_kernel,
        in_specs=[pl.BlockSpec(memory_space=pltpu.SMEM)] + [pl.BlockSpec(memory_space=pltpu.VMEM)] * 3,
        out_shape=(wide, wide, wide, wide, jax.ShapeDtypeStruct((8, SEQ), f32)),
        scratch_shapes=[pltpu.VMEM((WIDE, SEQ), bf16)],
        cost_estimate=pl.CostEstimate(flops=4 * HEADS * SEQ * SEQ * WIDE, transcendentals=HEADS * SEQ * SEQ, bytes_accessed=8 << 20),
    )(scalars, qkv, cosine, sine)


def attn_backward_kernel(qs, ks, vs, grad, lse, cosine, sine, out, kt, dq, dk, dv):
    lane, heads, extra = lane_masks(QB)
    first = lane % HD < ROT // 2
    wide_head = lax.broadcasted_iota(jnp.int32, (WIDE, QB), 0) // HD
    kept = lane < HEADS * HD
    kt[...] = ks[...].astype(f32).T.astype(bf16)
    dk[...] = jnp.zeros(dk.shape, f32)
    dv[...] = jnp.zeros(dv.shape, f32)

    def step(block, carry):
        rows = pl.ds(pl.multiple_of(block * QB, QB), QB)
        query, given = qs[rows, :], grad[rows, :]
        total = jnp.zeros((WIDE, QB), f32)
        for h in range(HEADS):
            own_query, own_grad = query * heads[h], given * heads[h + 1]
            scores = dot_nt(ks[...], query * (heads[h] + extra))
            weight = jnp.exp(scores - lse[h : h + 1, rows])
            wanted = dot_nt(vs[...], own_grad)
            product = weight * wanted
            inner = jnp.sum(product, axis=0, keepdims=True)
            slope = (product - weight * inner).astype(bf16)
            dv[...] += dot(weight.astype(bf16), own_grad)
            dk[...] += dot(slope, own_query)
            total = jnp.where(wide_head == h, dot(kt[...], slope), total)
        straight, crossed = turned(total.T * HD ** (-0.5), cosine[rows, :], sine[rows, :], first)
        turned_back = straight - crossed
        out[rows, 0:128] = turned_back[:, :128].astype(bf16)
        dq[rows, :] = turned_back[:, 128:]
        return carry

    lax.fori_loop(0, SEQ // QB, step, 0)
    for block in range(SEQ // QB):
        rows = pl.ds(block * QB, QB)
        value = dv[rows, :]
        out[rows, V_AT : V_AT + 128] = jnp.where(lane[:, :128] < HD, dq[rows, :], value[:, :128]).astype(bf16)
        out[rows, V_AT + 128 : V_AT + 256] = value[:, 128:].astype(bf16)
        straight, crossed = turned(dk[rows, :], cosine[rows, :], sine[rows, :], first)
        out[rows, K_AT : K_AT + WIDE] = jnp.where(kept, straight - crossed, 0.0).astype(bf16)


def attn_backward(qs, ks, vs, grad, lse, cosine, sine):
    return pl.pallas_call(
        attn_backward_kernel,
        in_specs=[pl.BlockSpec(memory_space=pltpu.VMEM)] * 7,
        out_shape=jax.ShapeDtypeStruct((SEQ, QVK), bf16),
        scratch_shapes=[pltpu.VMEM((WIDE, SEQ), bf16), pltpu.VMEM((SEQ, 128), f32), pltpu.VMEM((SEQ, WIDE), f32), pltpu.VMEM((SEQ, WIDE), f32)],
        cost_estimate=pl.CostEstimate(flops=10 * HEADS * SEQ * SEQ * WIDE, transcendentals=HEADS * SEQ * SEQ, bytes_accessed=8 << 20),
    )(qs, ks, vs, grad, lse, cosine, sine)


PAIR = 2 * HD
QUARTER = HEADS * HD


def pair_of(sc, kv, group, kind):
    lanes = []
    for head in (2 * group, 2 * group + 1):
        at = kind * QUARTER + head % HEADS * HD
        lanes.append(kv[(sc[2] + 4 - head // HEADS) % 4, :, at : at + HD])
    return jnp.concatenate(lanes, axis=1)


def cross_weights(query, keys, bias):
    scores = dot_nt(keys, query) + bias
    weight = jnp.exp(scores - jnp.max(scores, axis=0, keepdims=True))
    return weight / jnp.sum(weight, axis=0, keepdims=True)


def store_quarters(sc, out, group, value):
    for h in range(2):
        head = 2 * group + h
        at = head % HEADS * HD
        for side in range(2):
            piece = value[side * ROWS : (side + 1) * ROWS, h * HD : (h + 1) * HD]
            out[(head // HEADS + 4 - sc[2]) % 4, 0:ROWS, side * QUARTER + at : side * QUARTER + at + HD] = piece


def cross_forward_kernel(sc, cq, kv, bias, att, quarters):
    lane = lax.broadcasted_iota(jnp.int32, (2 * ROWS, PAIR), 1)
    row = lax.broadcasted_iota(jnp.int32, (PAIR, 2 * ROWS), 0)
    for group in range(cq.shape[1] // PAIR):
        at = pl.ds(group * PAIR, PAIR)
        query, keys = cq[:, at], pair_of(sc, kv, group, 0)
        values = pair_of(sc, kv, group, 1).astype(f32).T.astype(bf16)
        outs = []
        for h in range(2):
            mask = (lane // HD == h).astype(f32).astype(bf16)
            weight = cross_weights(query * mask, keys, bias[...])
            outs.append(dot(values, weight.astype(bf16)))
        value = jnp.where(row < HD, outs[0], outs[1]).T.astype(bf16)
        att[:, at] = value
        store_quarters(sc, quarters, group, value)


def cross_forward(scalars, cq, kv, bias):
    return pl.pallas_call(
        cross_forward_kernel,
        in_specs=[pl.BlockSpec(memory_space=pltpu.SMEM)] + [pl.BlockSpec(memory_space=pltpu.VMEM)] * 3,
        out_shape=(jax.ShapeDtypeStruct(cq.shape, bf16), jax.ShapeDtypeStruct((4, ROWS, 2 * QUARTER), bf16)),
        cost_estimate=pl.CostEstimate(flops=4 * 12 * 256 * 144 * 128, transcendentals=12 * 256 * 144, bytes_accessed=2 << 20),
    )(scalars, cq, kv, bias)


def cross_backward_kernel(sc, cq, kv, bias, grad, dq, quarters):
    lane = lax.broadcasted_iota(jnp.int32, (2 * ROWS, PAIR), 1)
    row = lax.broadcasted_iota(jnp.int32, (PAIR, 2 * ROWS), 0)
    for group in range(cq.shape[1] // PAIR):
        at = pl.ds(group * PAIR, PAIR)
        query, given = cq[:, at], grad[:, at]
        keys, values = pair_of(sc, kv, group, 0), pair_of(sc, kv, group, 1)
        turned_keys = keys.astype(f32).T.astype(bf16)
        outs, grads = [], [0.0, 0.0]
        for h in range(2):
            mask = (lane // HD == h).astype(f32).astype(bf16)
            own_query, own_grad = query * mask, given * mask
            weight = cross_weights(own_query, keys, bias[...])
            product = weight * dot_nt(values, own_grad)
            slope = (product - weight * jnp.sum(product, axis=0, keepdims=True)).astype(bf16)
            outs.append(dot(turned_keys, slope))
            grads[0] += dot(slope, own_query)
            grads[1] += dot(weight.astype(bf16), own_grad)
        value = (jnp.where(row < HD, outs[0], outs[1]).T * HD ** (-0.5)).astype(bf16)
        dq[:, at] = value
        store_quarters(sc, quarters, group, value)
        for h in range(2):
            head = 2 * group + h
            for kind in range(2):
                place = kind * QUARTER + head % HEADS * HD
                piece = grads[kind][:, h * HD : (h + 1) * HD].astype(bf16)
                quarters[(head // HEADS + 4 - sc[2]) % 4, ROWS:, place : place + HD] = piece


def cross_backward(scalars, cq, kv, bias, grad):
    return pl.pallas_call(
        cross_backward_kernel,
        in_specs=[pl.BlockSpec(memory_space=pltpu.SMEM)] + [pl.BlockSpec(memory_space=pltpu.VMEM)] * 4,
        out_shape=(
            jax.ShapeDtypeStruct(cq.shape, bf16),
            jax.ShapeDtypeStruct((4, ROWS + kv.shape[1], 2 * QUARTER), bf16),
        ),
        cost_estimate=pl.CostEstimate(flops=10 * 12 * 256 * 144 * 128, transcendentals=12 * 256 * 144, bytes_accessed=3 << 20),
    )(scalars, cq, kv, bias, grad)


def rotary_lanes(side, x):
    row = jnp.arange(SEQ, dtype=jnp.int32)
    within = row % (SEQ // 2)
    part = jnp.where(row < SEQ // 2, side, 1 - side)
    place = (((x + 4 - within // ROWS) % 4 * 2 + part) * ROWS + within % ROWS).astype(f32)
    lane = jnp.arange(128, dtype=jnp.int32) % HD
    exponent = (lane % (ROT // 2)).astype(f32) * (2.0 / ROT)
    angle = place[:, None] * jnp.power(jnp.float32(10000.0), -exponent)[None, :]
    inside = (lane < ROT)[None, :]
    sign = jnp.where(lane < ROT // 2, -1.0, 1.0)[None, :]
    return jnp.where(inside, jnp.cos(angle), 1.0), jnp.where(inside, jnp.sin(angle) * sign, 0.0)


def products_kernel(count, *refs):
    out, at = refs[-1], 0
    for k in range(count):
        left, right = refs[2 * k], refs[2 * k + 1]
        width = right.shape[1]
        out[:, at : at + width] = dot_tn(left[...], right[...]).astype(bf16)
        at += width


def products(*pairs):
    tile, total_width = 256, sum(right.shape[1] for _, right in pairs)
    flat, specs = [], []
    for left, right in pairs:
        flat += [left, right]
        specs += [pl.BlockSpec((left.shape[0], tile), lambda i: (0, i)), pl.BlockSpec(right.shape, lambda i: (0, 0))]
    work = sum(left.shape[0] * right.shape[1] for left, right in pairs)
    return pl.pallas_call(
        lambda *refs: products_kernel(len(pairs), *refs),
        grid=(D // tile,),
        in_specs=specs,
        out_specs=pl.BlockSpec((tile, total_width), lambda i: (i, 0)),
        out_shape=jax.ShapeDtypeStruct((D, total_width), bf16),
        cost_estimate=pl.CostEstimate(flops=2 * D * work, transcendentals=0, bytes_accessed=10 << 20),
    )(*flat)


def by_rows(blocks):
    return jnp.concatenate([b[:ROWS, k * QUARTER : (k + 1) * QUARTER] for k in range(2) for b in blocks], axis=0)


def attn_products_kernel(one, grad, back, att, context, share, two, three, *rest):
    cq, catt, out = rest[:4], rest[4:8], rest[8]
    proj, across = dot_tn(one[...], grad[...]), dot_tn(back[...], att[...])
    out[:, :O_AT] = proj[:, :O_AT].astype(bf16)
    out[:, O_AT:QVK] = (proj[:, O_AT:] + across[:, : QVK - O_AT]).astype(bf16)
    out[:, QVK : O_AT + WIDE] = across[:, QVK - O_AT :].astype(bf16)
    at = O_AT + WIDE
    out[:, at : at + 2 * QUARTER] = dot_tn(context[...], share[...]).astype(bf16)
    at += 2 * QUARTER
    pieces = [dot_tn(left[...], by_rows(right)).astype(bf16) for left, right in ((two, cq), (three, catt))]
    out[:, at:] = jnp.concatenate(pieces, axis=1)


def attn_products(one, grad, back, att, context, share, two, three, cq, catt):
    tile, width = 256, O_AT + WIDE + 4 * QUARTER

    def whole(v):
        return pl.BlockSpec(v.shape, lambda i: (0, 0))

    def piece(v):
        return pl.BlockSpec((v.shape[0], tile), lambda i: (0, i))

    specs = [piece(one), whole(grad), piece(back), whole(att), piece(context), whole(share), piece(two), piece(three)]
    return pl.pallas_call(
        attn_products_kernel,
        grid=(D // tile,),
        in_specs=specs + [whole(v) for v in (*cq, *catt)],
        out_specs=pl.BlockSpec((tile, width), lambda i: (i, 0)),
        out_shape=jax.ShapeDtypeStruct((D, width), bf16),
        cost_estimate=pl.CostEstimate(flops=2 * D * SEQ * width, transcendentals=0, bytes_accessed=16 << 20),
    )(one, grad, back, att, context, share, two, three, *cq, *catt)


def finish_feed_kernel(at, parts, gain, grad_in, grad_down):
    width = grad_down.shape[1]
    for kind in range(2):
        grad_in[kind] = parts[0, :, kind * width : (kind + 1) * width].astype(f32) * gain[...]
    grad_down[...] = parts[0, :, 2 * width :].astype(f32)


def held_at(h, q, at):
    return (at[0] + 4 - q) % 4 * 2 + jnp.where(h == at[1], 0, 1)


def finish_feed(at, parts, gain):
    rows, width = parts.shape[1], parts.shape[2] // 3
    return pl.pallas_call(
        finish_feed_kernel,
        grid_spec=pltpu.PrefetchScalarGridSpec(
            num_scalar_prefetch=1,
            grid=(2, 4),
            in_specs=[
                pl.BlockSpec((1, rows, 3 * width), lambda h, q, at: (held_at(h, q, at), 0, 0)),
                pl.BlockSpec((rows, 1), lambda h, q, at: (h, 0)),
            ],
            out_specs=(
                pl.BlockSpec((2, rows, width), lambda h, q, at: (0, h, q)),
                pl.BlockSpec((rows, width), lambda h, q, at: (h, q)),
            ),
        ),
        out_shape=(
            jax.ShapeDtypeStruct((2, 2 * rows, 4 * width), f32),
            jax.ShapeDtypeStruct((2 * rows, 4 * width), f32),
        ),
        cost_estimate=pl.CostEstimate(flops=1 << 22, transcendentals=0, bytes_accessed=11 << 20),
    )(at, parts, gain)


def finish_cond_kernel(at, parts, out):
    width = parts.shape[2]
    for h in range(2):
        for q in range(4):
            out[h, :, q * width : (q + 1) * width] = parts[held_at(h, q, at)].astype(f32)


def finish_cond(at, parts):
    count, width = parts.shape[1:]
    return pl.pallas_call(
        finish_cond_kernel,
        in_specs=[pl.BlockSpec(memory_space=pltpu.SMEM), pl.BlockSpec(memory_space=pltpu.VMEM)],
        out_shape=jax.ShapeDtypeStruct((2, count, 4 * width), f32),
        cost_estimate=pl.CostEstimate(flops=1 << 20, transcendentals=0, bytes_accessed=3 << 20),
    )(at, parts)


def finish_columns(places, parts, gain, other_gain):
    rows, quarter = parts.shape[1], parts.shape[2] // 8
    width = 4 * quarter

    def kernel(places, parts, gain, other_gain, proj, out, keyval, query, cross):
        h = pl.program_id(0)

        def kind_of(kind):
            row = [parts[places[4 * h + q], :, kind * quarter : (kind + 1) * quarter].astype(f32) for q in range(4)]
            return jnp.concatenate(row, axis=1)

        for place, kind in enumerate((0, 2, 1)):
            proj[place] = kind_of(kind) * gain[...]
        out[...] = kind_of(3)
        keyval[0] = kind_of(4)
        keyval[1] = kind_of(5)
        query[...] = kind_of(6) * other_gain[...]
        cross[...] = kind_of(7)

    def stacked(count):
        return pl.BlockSpec((count, rows, width), lambda h, places: (0, h, 0)), jax.ShapeDtypeStruct((count, 2 * rows, width), f32)

    plain = pl.BlockSpec((rows, width), lambda h, places: (h, 0)), jax.ShapeDtypeStruct((2 * rows, width), f32)
    outs = [stacked(3), plain, stacked(2), plain, plain]
    return pl.pallas_call(
        kernel,
        grid_spec=pltpu.PrefetchScalarGridSpec(
            num_scalar_prefetch=1,
            grid=(2,),
            in_specs=[
                pl.BlockSpec(parts.shape, lambda h, places: (0, 0, 0)),
                pl.BlockSpec((rows, 1), lambda h, places: (h, 0)),
                pl.BlockSpec((rows, 1), lambda h, places: (h, 0)),
            ],
            out_specs=[spec for spec, _ in outs],
        ),
        out_shape=[shape for _, shape in outs],
        cost_estimate=pl.CostEstimate(flops=1 << 20, transcendentals=0, bytes_accessed=4 << 20),
    )(places, parts, gain, other_gain)


def per_device(
    hidden_in,
    context,
    lengths,
    cond_mask,
    out_grad,
    gain_attn,
    self_proj,
    self_out,
    gain_cross,
    cross_query,
    cross_keyval,
    cross_out,
    gain_feed,
    feed_in,
    feed_out,
):
    x, yh, tp = lax.axis_index("x"), lax.axis_index("yh"), lax.axis_index("tp")
    cond_count = context.shape[1]
    own_rows = hidden_in.shape[1]
    half_rows = self_proj.shape[0] // 2
    quarter = self_proj.shape[2] // 4
    hidden_quarter = feed_in.shape[2] // 4
    local_width = self_proj.shape[2]

    def own_half(w):
        return lax.dynamic_slice_in_dim(w, yh * half_rows, half_rows, 0)

    def own_cols(w, count):
        return lax.dynamic_slice_in_dim(w, x * count, count, w.ndim - 1)

    def scaled(w, gain):
        return (w.astype(f32) * own_half(gain).astype(f32)[:, None]).astype(bf16)

    x_own = lax.ppermute(lax.dynamic_index_in_dim(hidden_in, tp, 0, False), ("yh", "tp"), SWAP)
    u_own = lax.ppermute(lax.dynamic_index_in_dim(out_grad, tp, 0, False), ("yh", "tp"), SWAP)
    length = lax.dynamic_index_in_dim(lengths, yh, 0, False)
    own_mask = lax.dynamic_index_in_dim(cond_mask, yh, 0, False)
    tokens = permuted(x_own).astype(f32)
    norm_one, scale_one = unit_norm(tokens)

    qkv_cols = own_cols(own_half(self_proj), quarter)
    qvk_cols = jnp.concatenate([qkv_cols[:, 0], qkv_cols[:, 2], qkv_cols[:, 1]], axis=1)
    out_cols = own_cols(own_half(self_out), quarter)
    keyval_cols = own_cols(own_half(cross_keyval), quarter).reshape(half_rows, 2 * quarter)
    cq_half = own_half(cross_query)
    first_set = gather_plane(
        jnp.concatenate([scaled(qvk_cols, gain_attn), out_cols, keyval_cols, scaled(cq_half, gain_cross), own_half(cross_out)], axis=1)
    )
    sent_one = norm_one.astype(bf16)
    sent_one, feed_in, feed_out, context = both(sent_one, feed_in, feed_out, context)
    feed_cols = own_cols(own_half(feed_in), hidden_quarter).reshape(half_rows, 2 * hidden_quarter)
    down_cols = own_cols(own_half(feed_out), hidden_quarter)
    feed_set = gather_plane(jnp.concatenate([scaled(feed_cols, gain_feed), down_cols], axis=1))
    w_qvk, w_out = first_set[:, :QVK], first_set[:, O_AT : O_AT + WIDE]
    cq_at = O_AT + WIDE + 2 * quarter
    w_kv, w_cq, w_co = first_set[:, O_AT + WIDE : cq_at], first_set[:, cq_at : cq_at + local_width], first_set[:, cq_at + local_width :]
    w_feed, w_down = feed_set[:, : 2 * hidden_quarter], feed_set[:, 2 * hidden_quarter :]

    scalars = jnp.stack([tp.astype(jnp.int32), length, x.astype(jnp.int32)])
    own_context = jnp.pad(lax.dynamic_index_in_dim(context, yh, 0, False), ((0, CROSS_KEYS - cond_count), (0, 0)))
    mine_one, u_own, cosine, sine, own_context = both(
        gather_half(sent_one), u_own, *rotary_lanes(tp, x), permuted(own_context)
    )
    upstream = permuted(u_own)
    full_one, mine_grad = both(with_partner(mine_one), gather_half(upstream))
    qvk, keyval, full_grad = both(dot(full_one, w_qvk), dot(own_context, w_kv).astype(bf16), with_partner(mine_grad))
    attended, qs, ks, vs, lse = attn_forward(scalars, qvk, cosine, sine)
    attended, keyval = both(attended, gather_x(keyval))
    cond_kv = jnp.stack(keyval)
    blocks = both(*scatter_half(dot_nt(attended, w_out)))
    attn_branch = summed(both(*scatter_x(blocks)))
    resid_one = tokens + attn_branch

    seen = jnp.pad(own_mask > 0, (0, CROSS_KEYS - cond_count))
    bias = jnp.broadcast_to(jnp.where(seen, 0.0, masked_fill)[:, None], (CROSS_KEYS, 2 * own_rows)).astype(f32)
    norm_two, scale_two = unit_norm(resid_one)
    sent_two = norm_two.astype(bf16)
    pair_two = pair_rows(sent_two)
    cross_q = (dot(pair_two, w_cq) * HD ** (-0.5)).astype(bf16)
    cross_att, att_quarters = cross_forward(scalars, cross_q, cond_kv, bias)
    cross_branch = pair_sum(dot_nt(cross_att, w_co))
    resid_two = resid_one + cross_branch
    norm_three, scale_three = unit_norm(resid_two)

    sent_three, full_grad, sent_two, att_quarters = both(norm_three.astype(bf16), full_grad, sent_two, att_quarters)
    mine_three, grad_hidden = both(gather_half(sent_three), dot(full_grad, w_down))
    full_three, sent_two, att_quarters = both(with_partner(mine_three), sent_two, att_quarters)
    carried = [jnp.concatenate([sent_two, att_quarters[k]], axis=1) for k in range(4)]
    carried = swapped_x(carried)
    gate_up = dot(full_three, w_feed)
    gate, upward = gate_up[:, :hidden_quarter], gate_up[:, hidden_quarter:]
    sig = jax.nn.sigmoid(gate)
    hidden = (gate * sig * upward).astype(bf16)
    grad_gate = grad_hidden * upward * sig * (1.0 + gate * (1.0 - sig))
    grad_gate_up = jnp.concatenate([grad_gate.astype(bf16), (grad_hidden * gate * sig).astype(bf16)], axis=1)
    partial, carried = both(dot_nt(grad_gate_up, w_feed), carried)
    blocks, carried, grad_gate_up, hidden = both(scatter_half(partial), carried, grad_gate_up, hidden)
    mine_two = jnp.concatenate([block[:, :D] for block in carried], axis=0)
    att_quarter = carried
    grad_three, grad_feed, feed_part, full_two = both(
        scatter_x(blocks),
        products((full_three, grad_gate_up), (full_grad, hidden)),
        dot_nt(hidden, w_down).astype(bf16),
        with_partner(mine_two),
    )
    sum_feed = scatter_plane(grad_feed)
    grad_resid_two = upstream.astype(f32) + unit_norm_back(norm_three, scale_three, summed(grad_three))

    sent_two, feed_part = both(grad_resid_two.astype(bf16), feed_part)
    mine_two = gather_half(sent_two)
    pair_grad = pair_rows(sent_two)
    grad_cross_att = dot(pair_grad, w_co).astype(bf16)
    grad_cq, quarters = cross_backward(scalars, cross_q, cond_kv, bias, grad_cross_att)
    grad_cq, mine_two, feed_part = both(grad_cq, mine_two, feed_part)
    grad_two = pair_sum(dot_nt(grad_cq, w_cq))
    grad_resid_one = grad_resid_two + unit_norm_back(norm_two, scale_two, grad_two)

    sent_back, mine_two, quarters, feed_part, att_quarter = both(
        grad_resid_one.astype(bf16), mine_two, quarters, feed_part, att_quarter
    )
    mine_back, grad_two_all, feed_half, att_quarter = both(
        gather_half(sent_back), with_partner(mine_two), scatter_half(feed_part), [block[:, D:] for block in att_quarter]
    )
    full_back, quarters, feed_half = both(with_partner(mine_back), quarters, feed_half)
    grad_att, quarters, feed_half = both(dot(full_back, w_out).astype(bf16), quarters, feed_half)
    quarter_parts = swapped_x([quarters[k] for k in range(4)])
    feed_parts = scatter_x(feed_half)
    grad_qvk = attn_backward(qs, ks, vs, grad_att, lse, cosine, sine)
    grad_qvk, quarter_parts, sum_feed = both(grad_qvk, quarter_parts, sum_feed)
    ckv_share = summed([part[ROWS:] for part in quarter_parts]).astype(bf16)
    grad_attn = attn_products(
        full_one, grad_qvk, full_back, attended, own_context, ckv_share, full_two, grad_two_all, quarter_parts, att_quarter
    )
    grad_attn, grad_qvk, ckv_share, feed_parts, sum_feed_far = both(grad_attn, grad_qvk, ckv_share, feed_parts, to_far(sum_feed))
    parts_attn = plane_parts(grad_attn)
    blocks, ckv_share, feed_parts = both(scatter_half(dot_nt(grad_qvk, w_qvk)), ckv_share, feed_parts)
    cond_part = dot_nt(ckv_share, w_kv)[:cond_count]
    cond_part = (cond_part + to_partner(cond_part)).astype(bf16)
    feed_branch = summed(feed_parts)
    output = resid_two + feed_branch
    grad_one, cond_part, sent_out, sum_feed, sum_feed_far = both(
        scatter_x(blocks), cond_part, permuted(output.astype(bf16)), sum_feed, sum_feed_far
    )
    in_grad = grad_resid_one + unit_norm_back(norm_one, scale_one, summed(grad_one))

    def columns_of(back):
        return lax.dynamic_slice_in_dim(cond_part, (x + 4 - back) % 4 * (D // 4), D // 4, 1)

    cond_parts = scatter_x([columns_of(back) for back in range(4)])
    cond_own = permuted(summed(cond_parts).astype(bf16))
    feed_all = gather_x(jnp.stack([sum_feed, sum_feed_far]))

    def row_sums(w, grad):
        sums = jnp.sum(w.astype(f32) * grad.astype(f32), axis=1)
        return jnp.pad(sums, (0, 128 - half_rows))

    row = jnp.arange(own_rows, dtype=jnp.int32)
    valid = ((2 * x + tp) * own_rows + row < length)[:, None]
    squares = [jnp.sum(jnp.where(valid, v * v, 0.0)) for v in (tokens, attn_branch, cross_branch, feed_branch, output)]
    small = jnp.concatenate([row_sums(feed_cols, sum_feed[:, : 2 * hidden_quarter]), jnp.pad(jnp.stack(squares), (0, 123))])

    moved_in = lax.ppermute(permuted(in_grad.astype(bf16)), ("yh", "tp"), SWAP)
    moved_out = lax.ppermute(sent_out, ("yh", "tp"), SWAP)
    parts_attn, moved_in, moved_out, feed_all, small, cond_own = both(parts_attn, moved_in, moved_out, feed_all, small, cond_own)
    sum_attn = total(parts_attn)
    attn_own = sum_attn.astype(bf16)
    attn_far, cond_far = both(to_far(attn_own), to_far(cond_own))
    attn_all = gather_x(jnp.stack([attn_own, attn_far]))
    cond_all = gather_x(jnp.stack([cond_own, cond_far]))
    more = [row_sums(qvk_cols, sum_attn[:, : 3 * quarter])]
    more += [row_sums(own_cols(cq_half, quarter), sum_attn[:, 6 * quarter : 7 * quarter])]
    small = jnp.concatenate([*more, small]).reshape(4, 128)
    small_blocks = gather_x(small + to_partner(small))
    in_grad = lax.all_gather(moved_in, "tp", axis=0, tiled=False).astype(f32)
    layer_out = lax.all_gather(moved_out, "tp", axis=0, tiled=False)
    at = jnp.stack([x, yh]).astype(jnp.int32)

    def laid(blocks):
        stacked = jnp.stack(blocks)
        return stacked.reshape(8, *stacked.shape[2:])

    def column(gain):
        return gain.astype(f32)[:, None]

    grad_feed_in, grad_feed_out = finish_feed(at, laid(feed_all), column(gain_feed))
    grad_feed_in = grad_feed_in.transpose(1, 0, 2)
    attn_all, small_blocks, cond_all, grad_feed_in, grad_feed_out, in_grad, layer_out = both(
        attn_all, small_blocks, cond_all, grad_feed_in, grad_feed_out, in_grad, layer_out
    )
    cond_grad = finish_cond(at, laid(cond_all))

    block = jnp.arange(8, dtype=jnp.int32)
    places = (x + 4 - block % 4) % 4 * 2 + jnp.where(block // 4 == yh, 0, 1)
    proj, out, keyval, query, cross = finish_columns(places, laid(attn_all), column(gain_attn), column(gain_cross))
    small = jnp.stack(small_blocks)
    small = sum(lax.dynamic_index_in_dim(small, (x + 4 - q) % 4, 0, False) for q in range(4))
    other = lax.ppermute(small, "yh", ((0, 1), (1, 0)))
    small = jnp.where(yh == 0, jnp.stack([small, other]), jnp.stack([other, small]))
    layer_stats = jnp.sqrt(small[:, 3, :5] / (lengths.astype(f32)[:, None] * D))
    gains = [small[:, k, :half_rows].reshape(2 * half_rows) for k in range(3)]

    return (
        layer_out,
        in_grad,
        cond_grad,
        layer_stats,
        gains[0],
        proj.transpose(1, 0, 2),
        out,
        gains[1],
        query,
        keyval.transpose(1, 0, 2),
        cross,
        gains[2],
        grad_feed_in,
        grad_feed_out,
    )


def solution(mesh):
    fine = Mesh(mesh.devices.reshape(4, 2, 4, 2, 2), ("z", "yl", "x", "yh", "tp"))
    weights = (
        P(DP),
        P(DP, None, "tp"),
        P(DP, "tp"),
        P(DP),
        P(DP, "tp"),
        P(DP, None, "tp"),
        P(DP, "tp"),
        P(DP),
        P(DP, None, "tp"),
        P(DP, "tp"),
    )
    return jax.shard_map(
        per_device,
        mesh=fine,
        in_specs=(P(DP, CTX, None), P(DP, None, None), P(DP), P(DP, None), P(DP, CTX, None), *weights),
        out_specs=(P(DP, CTX, None), P(DP, CTX, None), P(DP, None, None), P(DP, None), *weights),
        check_vma=False,
    )
```

time: 943 us -> 592 us (0.63)
  waiting for transfers between devices: 399 us -> 177 us
  local copies, waits for them, and re-layouts: 149 us -> 67 us
  blocking collectives: 59.3 us -> 6.77 us
  Pallas kernels: 40.7 us -> 80.4 us
  matrix products: 87.5 us -> 54.6 us
    ppermute x2 -> x57, waiting for transfers between devices: 22.6 us -> 157 us  [the longest x51 149 us: along_x(): return lax.ppermute(v, 'x', [(i, (i + step) % 4) for i in range(4)])]
    all_to_all x14 -> x1, waiting for transfers between devices: 122 us -> 0.01 us  [exchanged(): return lax.all_to_all(v, axes, split_axis=0, concat_axis=0, tiled=True)]
    unnamed x11 -> x3, waiting for transfers between devices: 109 us -> 0.05 us
    reduce_scatter x3 -> x1, waiting for transfers between devices: 95.2 us -> 0.02 us  [scatter_plane(): return lax.psum_scatter(grad, PLANE, scatter_dimension=0, tiled=True)]
    reshape x18 -> x0, local copies, waits for them, and re-layouts: 71.5 us -> none  [the longest x3 32 us: per_device(): feed_all.reshape(2 * half_rows, 4, 3, hidden_quarter).transpose(0, 2, 1, 3)]
    ppermute x2 -> x57, starting transfers between devices: 10.8 us -> 82 us  [the longest x51 66.6 us: along_x(): return lax.ppermute(v, 'x', [(i, (i + step) % 4) for i in range(4)])]
    all_to_all x14 -> x1, starting transfers between devices: 64.4 us -> 4.56 us  [exchanged(): return lax.all_to_all(v, axes, split_axis=0, concat_axis=0, tiled=True)]
    all_to_all x3 -> x0, blocking collectives: 49.7 us -> none  [the longest x2 39.3 us: sent_to_all(): return lax.all_to_all(copies, axes, split_axis=0, concat_axis=0, tiled=True)]
  transfers between devices with their start and end apart: 41 -> 79, of which waited for: 26 -> 28; matrix products, arithmetic and copies ran while one was open for 25% -> 27% of each run, Pallas kernels for 2% -> 14%
where the time goes in v2:
time: 592 us; the launch traced here: 581 us
  waiting for transfers between devices  177 us (30%)
  starting transfers between devices  111 us (19%)
  Pallas kernels  80.4 us (14%)
  other arithmetic  69.8 us (12%)
  local copies, waits for them, and re-layouts  67 us (11%)
  matrix products  54.6 us (9%)
  between operations  15.5 us (3%)
  blocking collectives  6.77 us (1%)
    ppermute x51, waiting for transfers between devices, along_x(): return lax.ppermute(v, 'x', [(i, (i + step) % 4) for i in range(4)])  149 us
    ppermute x51, starting transfers between devices, along_x(): return lax.ppermute(v, 'x', [(i, (i + step) % 4) for i in range(4)])  66.6 us
    dot_general x7, matrix products, dot(): return jnp.dot(a, b, preferred_element_type=f32)  28.7 us
    dot_general x7, matrix products, dot_nt(): lax.dot_general(a, b, (((1,), (1,)), ((), ())), preferred_element_type=f32)  25.9 us
    unnamed x111, local copies, waits for them, and re-layouts  20.2 us
    ppermute x16, waiting for transfers between devices, to_partner(): return lax.ppermute(v, 'tp', ((0, 1), (1, 0)))  16.3 us
    pallas_call x1, Pallas kernels, attn_backward(): pl.pallas_call(attn_backward_kernel, in_specs=[pl.BlockSpec(memory_space=...  16.2 us
    ppermute x16, starting transfers between devices, to_partner(): return lax.ppermute(v, 'tp', ((0, 1), (1, 0)))  15.8 us
  transfers between devices with their start and end apart: 79, of which 28 were waited for; matrix products, arithmetic and copies ran while one was open for 27% of the time, Pallas kernels for 14%

profile of v2, /device:TPU:1, one launch (start us, length us, event | category | flops | bytes accessed | tf_op | source)
XLA Modules:
  0.0 581.5 jit_solution(3986837692648026031)
XLA Ops:
  14.6 6.2 %collective-permute-start = (bf16[128,1536]{1,0:T(8,128)(2,1)S(1)}, bf16[128,1536]{1,0:T(8,128)(2,1)S(1)}, u32[]{:S(2)}, u32[]{:S(2)}) collective-permute-start(bf16[128,1536]{1,0:T(8,128)(2,1)S(1)} %dynamic-slice_bitcast_fusion.2), channel_id=1, source_target_pairs={{0,0},{1,2},{2,1},{3,3},{4,4},{5,6},{6,5},{7,7},{8,8},{9,10},{10,9... | collective-permute-start | bytes 1179656 | tf_op jit(solution)/shard_map/ppermute | solution.py:560
  23.7 3.1 fusion.59
  39.6 8.9 %collective-permute-done.2 = bf16[128,1536]{1,0:T(8,128)(2,1)} collective-permute-done((bf16[128,1536]{1,0:T(8,128)(2,1)S(1)}, bf16[128,1536]{1,0:T(8,128)(2,1)}, u32[]{:S(2)}, u32[]{:S(2)}) %collective-permute-start.2) | collective-permute-done | bytes 393248 | tf_op jit(solution)/shard_map/ppermute | solution.py:72
  59.9 7.7 %collective-permute-done.6 = bf16[128,1536]{1,0:T(8,128)(2,1)S(1)} collective-permute-done((bf16[128,1536]{1,0:T(8,128)(2,1)S(1)}, bf16[128,1536]{1,0:T(8,128)(2,1)S(1)}, u32[]{:S(2)}, u32[]{:S(2)}) %collective-permute-start.6) | collective-permute-done | bytes 393248 | tf_op jit(solution)/shard_map/ppermute | solution.py:72
  67.6 9.5 %collective-permute-done.7 = bf16[128,1536]{1,0:T(8,128)(2,1)S(1)} collective-permute-done((bf16[128,1536]{1,0:T(8,128)(2,1)S(1)}, bf16[128,1536]{1,0:T(8,128)(2,1)S(1)}, u32[]{:S(2)}, u32[]{:S(2)}) %collective-permute-start.7) | collective-permute-done | bytes 393248 | tf_op jit(solution)/shard_map/ppermute | solution.py:72
  77.2 3.3 pad_maximum_fusion.1.one
  86.2 3.1 all-gather.5.cloned.1.call-done
  91.1 6.6 %fusion.19.qkv = f32[1024,640]{1,0:T(8,128)} fusion(bf16[1024,1536]{1,0:T(8,128)(2,1)} %pad_maximum_fusion.1.one, bf16[1536,2688]{1,0:T(8,128)(2,1)} %all-gather.5.cloned.1.call-done), kind=kOutput, calls=%fused_computation.40 | convolution fusion | flops 2013265920 | bytes 7733248 | tf_op jit(solution)/shard_map/dot_general | solution.py:40
  102.9 13.2 %shard_map.254 = (bf16[1024,256]{1,0:T(8,128)(2,1)}, bf16[1024,256]{1,0:T(8,128)(2,1)}, bf16[1024,256]{1,0:T(8,128)(2,1)}, bf16[1024,256]{1,0:T(8,128)(2,1)}, f32[8,1024]{1,0:T(8,128)}) custom-call(s32[3]{0:T(128)} %pad_add_fusion.sc, f32[1024,640]{1,0:T(8,128)} %fusion.19.qkv, f32[1024,128]{1,0:T(8,128)} %get-tuple-element.189.cosine, ...), custom_call_target="tpu_custom_call" | custom-call | flops 3221225472 | bytes 8388608 | tf_op jit(solution)/shard_map/pallas_call | solution.py:204
  126.8 7.7 %collective-permute-done.14 = bf16[128,1536]{1,0:T(8,128)(2,1)S(1)} collective-permute-done((bf16[128,1536]{1,0:T(8,128)(2,1)S(1)}, bf16[128,1536]{1,0:T(8,128)(2,1)S(1)}, u32[]{:S(2)}, u32[]{:S(2)}) %collective-permute-start.14) | collective-permute-done | bytes 393248 | tf_op jit(solution)/shard_map/ppermute | solution.py:72
  136.0 9.2 %collective-permute-done.16 = bf16[128,1536]{1,0:T(8,128)(2,1)} collective-permute-done((bf16[128,1536]{1,0:T(8,128)(2,1)S(1)}, bf16[128,1536]{1,0:T(8,128)(2,1)}, u32[]{:S(2)}, u32[]{:S(2)}) %collective-permute-start.16) | collective-permute-done | bytes 393248 | tf_op jit(solution)/shard_map/ppermute | solution.py:72
  150.5 3.2 fusion.24.cq
  154.4 4.6 shard_map.255
  168.6 5.2 fusion.7
  173.9 11.4 %collective-permute-done.19 = bf16[128,1536]{1,0:T(8,128)(2,1)} collective-permute-done((bf16[128,1536]{1,0:T(8,128)(2,1)S(1)}, bf16[128,1536]{1,0:T(8,128)(2,1)}, u32[]{:S(2)}, u32[]{:S(2)}) %collective-permute-start.19) | collective-permute-done | bytes 393248 | tf_op jit(solution)/shard_map/ppermute | solution.py:72
  195.6 5.0 fusion.2
  203.6 5.1 fusion
  208.7 8.2 %collective-permute-done.24 = bf16[128,1920]{1,0:T(8,128)(2,1)S(1)} collective-permute-done((bf16[128,1920]{1,0:T(8,128)(2,1)S(1)}, bf16[128,1920]{1,0:T(8,128)(2,1)S(1)}, u32[]{:S(2)}, u32[]{:S(2)}) %collective-permute-start.24) | collective-permute-done | bytes 491552 | tf_op jit(solution)/shard_map/ppermute | solution.py:72
  230.7 12.9 %shard_map.256 = bf16[1536,2304]{1,0:T(8,128)(2,1)} custom-call(bf16[1024,1536]{1,0:T(8,128)(2,1)} %copy-done.5, bf16[1024,1536]{1,0:T(8,128)(2,1)} %pad_maximum_fusion.4.refs_1_, bf16[1024,1536]{1,0:T(8,128)(2,1)} %pad_maximum_fusion.2.refs_2_, bf16[1024,768]{1,0:T(8,128)(2,1)} %get-tuple-element.233.refs_3_), custom_call_target="tpu_custom_call" | custom-call | flops 7247757312 | bytes 10485760 | tf_op jit(solution)/shard_map/pallas_call | solution.py:386
  243.6 6.4 %convolution_convert_fusion = bf16[1024,1536]{1,0:T(8,128)(2,1)} fusion(bf16[1024,768]{1,0:T(8,128)(2,1)} %get-tuple-element.233.refs_3_, bf16[1536,2304]{1,0:T(8,128)(2,1)} %all-gather.7.cloned.1.call-done), kind=kOutput, calls=%fused_computation.5 | convolution fusion | flops 2417491968 | bytes 7077888 | tf_op jit(solution)/shard_map/dot_general | solution.py:44
  262.9 3.3 fusion.27.grad
  266.3 5.9 %shard_map.257 = (bf16[256,768]{1,0:T(8,128)(2,1)}, bf16[4,272,384]{2,1,0:T(8,128)(2,1)}) custom-call(s32[3]{0:T(128)} %pad_add_fusion.sc, bf16[256,768]{1,0:T(8,128)(2,1)} %fusion.24.cq, bf16[4,144,384]{2,1,0:T(8,128)(2,1)} %pad_maximum_fusion.21.kv, f32[144,256]{1,0:T(8,128)} %broadcast_in_dim.127.bias, bf16[256,768]{1,0:T(8,128)(2,1)} %fusion.27.grad), custom_call_target="tpu_custom_call" | custom-call | flops 566231040 | bytes 3145728 | tf_op jit(solution)/shard_map/pallas_call | solution.py:346
  272.2 7.3 %collective-permute-done.33 = bf16[128,1536]{1,0:T(8,128)(2,1)S(1)} collective-permute-done((bf16[128,1536]{1,0:T(8,128)(2,1)}, bf16[128,1536]{1,0:T(8,128)(2,1)S(1)}, u32[]{:S(2)}, u32[]{:S(2)}) %collective-permute-start.33) | collective-permute-done | bytes 393248 | tf_op jit(solution)/shard_map/ppermute | solution.py:72
  300.1 8.8 %collective-permute-done.37 = bf16[128,1536]{1,0:T(8,128)(2,1)S(1)} collective-permute-done((bf16[128,1536]{1,0:T(8,128)(2,1)S(1)}, bf16[128,1536]{1,0:T(8,128)(2,1)S(1)}, u32[]{:S(2)}, u32[]{:S(2)}) %collective-permute-start.37) | collective-permute-done | bytes 393248 | tf_op jit(solution)/shard_map/ppermute | solution.py:72
  317.1 3.6 convolution_convert_fusion.1.grad
  328.5 16.2 %shard_map.258.grad = bf16[1024,640]{1,0:T(8,128)(2,1)} custom-call(bf16[1024,256]{1,0:T(8,128)(2,1)} %get-tuple-element.191.qs, bf16[1024,256]{1,0:T(8,128)(2,1)} %get-tuple-element.192.ks, bf16[1024,256]{1,0:T(8,128)(2,1)} %get-tuple-element.193.vs, bf16[1024,256]{1,0:T(8,128)(2,1)} %convolution_convert_fusion.1.grad, f32[8,1024]{1,0:T(8,128)} %get-tuple-element.270.lse, ...), custom_call_target="tpu_custom_call" | custom-call | flops 8053063680 | bytes 8388608 | tf_op jit(solution)/shard_map/pallas_call | solution.py:254
  349.3 12.4 %shard_map.259 = bf16[1536,1536]{1,0:T(8,128)(2,1)} custom-call(bf16[1024,1536]{1,0:T(8,128)(2,1)} %pad_maximum_fusion.1.one, bf16[1024,640]{1,0:T(8,128)(2,1)} %shard_map.258.grad, bf16[1024,1536]{1,0:T(8,128)(2,1)} %copy-done.2, bf16[1024,256]{1,0:T(8,128)(2,1)} %get-tuple-element.196.att, bf16[144,1536]{1,0:T(8,128)(2,1)} %copy-done.12, ...), custom_call_target="tpu_custom_call" | custom-call | flops 4831838208 | bytes 16777216 | tf_op jit(solution)/shard_map/pallas_call | solution.py:423
  361.8 4.9 fusion.17
  376.2 4.6 all-to-all-start
  395.9 10.5 %collective-permute-done.50 = bf16[128,1536]{1,0:T(8,128)(2,1)} collective-permute-done((bf16[128,1536]{1,0:T(8,128)(2,1)}, bf16[128,1536]{1,0:T(8,128)(2,1)}, u32[]{:S(2)}, u32[]{:S(2)}) %collective-permute-start.50) | collective-permute-done | bytes 393248 | tf_op jit(solution)/shard_map/ppermute | solution.py:72
  406.4 4.0 collective-permute-done.52
  422.9 3.3 stack.163
  426.6 28.6 %collective-permute-done.59 = bf16[130,384]{1,0:T(8,128)(2,1)S(1)} collective-permute-done((bf16[130,384]{1,0:T(8,128)(2,1)}, bf16[130,384]{1,0:T(8,128)(2,1)S(1)}, u32[]{:S(2)}, u32[]{:S(2)}) %collective-permute-start.59) | collective-permute-done | bytes 99872 | tf_op jit(solution)/shard_map/ppermute | solution.py:72
  457.7 5.5 collective-permute-start.54
  463.2 5.8 collective-permute-start.55
  470.3 4.2 collective-permute-done.55
  479.7 3.7 collective-permute-start.67
  488.0 3.9 collective-permute-done.63
  492.2 3.5 collective-permute-start.65
  497.2 3.3 pad_maximum_fusion
  501.2 23.1 %collective-permute-done.71 = bf16[2,130,384]{2,1,0:T(8,128)(2,1)S(1)} collective-permute-done((bf16[2,130,384]{2,1,0:T(8,128)(2,1)S(1)}, bf16[2,130,384]{2,1,0:T(8,128)(2,1)S(1)}, u32[]{:S(2)}, u32[]{:S(2)}) %collective-permute-start.71) | collective-permute-done | bytes 199712 | tf_op jit(solution)/shard_map/ppermute | solution.py:72
  526.2 4.3 all-gather
  531.8 7.8 %shard_map.260 = (f32[2,192,3072]{2,1,0:T(8,128)}, f32[192,3072]{1,0:T(8,128)}) custom-call(s32[2]{0:T(128)} %pad_add_fusion.1.at, bf16[8,96,2304]{2,1,0:T(8,128)(2,1)} %bitcast.114, f32[192,1]{1,0:T(8,128)} %copy.36.gain), custom_call_target="tpu_custom_call" | custom-call | flops 4194304 | bytes 11534336 | tf_op jit(solution)/shard_map/pallas_call | solution.py:446
  543.3 3.1 pad_maximum_fusion.7
  548.4 4.9 shard_map.262
  553.3 3.2 copy.43
  559.0 3.8 copy.42
  562.8 8.2 %copy.44 = f32[192,2,3072]{2,1,0:T(2,128)} copy(f32[192,2,3072]{2,0,1:T(8,128)} %bitcast.118) | data formatting | bytes 9437184
  (401 shorter events, 223.6 us)
Async XLA Ops:
  7.2 82.2 %all-gather.5.cloned.1.call-start = ((), (), s32[]{:S(2)}) async-start(), calls=%async_computation.2 | async-start | bytes 8773632 | tf_op jit(solution)/shard_map/all_gather | solution.py:127
  14.5 154.2 %all-gather.7.cloned.1.call-start = ((), (), s32[]{:S(2)}) async-start(), calls=%async_computation.3 | async-start | bytes 7520256 | tf_op jit(solution)/shard_map/all_gather | solution.py:127
  21.6 28.2 %collective-permute-start.4 = (bf16[128,1536]{1,0:T(8,128)(2,1)}, bf16[128,1536]{1,0:T(8,128)(2,1)}, u32[]{:S(2)}, u32[]{:S(2)}) collective-permute-start(bf16[128,1536]{1,0:T(8,128)(2,1)} %dynamic-slice_bitcast_fusion.1), channel_id=1, source_target_pairs={{0,0},{1,2},{2,1},{3,3},{4,4},{5,6},{6,5},{7,7},{8,8},{9,10},{10,9... | collective-permute-start | bytes 1179656 | tf_op jit(solution)/shard_map/ppermute | solution.py:561
  29.3 19.1 %collective-permute-start.2 = (bf16[128,1536]{1,0:T(8,128)(2,1)S(1)}, bf16[128,1536]{1,0:T(8,128)(2,1)}, u32[]{:S(2)}, u32[]{:S(2)}) collective-permute-start(bf16[128,1536]{1,0:T(8,128)(2,1)S(1)} %fusion.37), channel_id=1, source_target_pairs={{0,8},{4,12},{8,0},{12,4},{1,9},{5,13},{9,1},{13,5},{2,10},{6,14},... | collective-permute-start | bytes 1179656 | tf_op jit(solution)/shard_map/ppermute | solution.py:72
  37.9 306.8 %reduce-scatter.2.cloned.1.call-start = ((), (), s32[]{:S(2)}) async-start(), calls=%async_computation.4 | async-start | bytes 7520256 | tf_op jit(solution)/shard_map/reduce_scatter | solution.py:131
  49.8 27.4 %collective-permute-start.5 = (bf16[512,1536]{1,0:T(8,128)(2,1)S(1)}, bf16[512,1536]{1,0:T(8,128)(2,1)}, u32[]{:S(2)}, u32[]{:S(2)}) collective-permute-start(bf16[512,1536]{1,0:T(8,128)(2,1)S(1)} %pad_maximum_fusion.8), channel_id=1, source_target_pairs={{0,1},{1,0},{2,3},{3,2},{4,5},{5,4},{6,7},{7,6},{8,9},{9,8},{10,11... | collective-permute-start | bytes 4718600 | tf_op jit(solution)/shard_map/ppermute | solution.py:52
  57.1 19.9 %collective-permute-start.7 = (bf16[128,1536]{1,0:T(8,128)(2,1)S(1)}, bf16[128,1536]{1,0:T(8,128)(2,1)S(1)}, u32[]{:S(2)}, u32[]{:S(2)}) collective-permute-start(bf16[128,1536]{1,0:T(8,128)(2,1)S(1)} %concatenate.100), channel_id=1, source_target_pairs={{0,8},{4,12},{8,0},{12,4},{1,9},{5,13},{9,1},{13,5},{2,10},{6,14},... | collective-permute-start | bytes 1179656 | tf_op jit(solution)/shard_map/ppermute | solution.py:72
  59.4 17.6 %collective-permute-start.8 = (bf16[128,1536]{1,0:T(8,128)(2,1)S(1)}, bf16[128,1536]{1,0:T(8,128)(2,1)S(1)}, u32[]{:S(2)}, u32[]{:S(2)}) collective-permute-start(bf16[128,1536]{1,0:T(8,128)(2,1)S(1)} %concatenate.100), channel_id=1, source_target_pairs={{0,12},{4,0},{8,4},{12,8},{1,13},{5,1},{9,5},{13,9},{2,14},{6,2},{... | collective-permute-start | bytes 1179656 | tf_op jit(solution)/shard_map/ppermute | solution.py:72
  97.7 18.4 %collective-permute-start.10 = (bf16[144,384]{1,0:T(8,128)(2,1)S(1)}, bf16[144,384]{1,0:T(8,128)(2,1)S(1)}, u32[]{:S(2)}, u32[]{:S(2)}) collective-permute-start(bf16[144,384]{1,0:T(8,128)(2,1)S(1)} %convolution_convert_fusion.2), channel_id=1, source_target_pairs={{0,4},{4,8},{8,12},{12,0},{1,5},{5,9},{9,13},{13,1},{2,6},{6,10},{... | collective-permute-start | bytes 331784 | tf_op jit(solution)/shard_map/ppermute | solution.py:72
  98.9 17.3 %collective-permute-start.11 = (bf16[144,384]{1,0:T(8,128)(2,1)S(1)}, bf16[144,384]{1,0:T(8,128)(2,1)S(1)}, u32[]{:S(2)}, u32[]{:S(2)}) collective-permute-start(bf16[144,384]{1,0:T(8,128)(2,1)S(1)} %convolution_convert_fusion.2), channel_id=1, source_target_pairs={{0,8},{4,12},{8,0},{12,4},{1,9},{5,13},{9,1},{13,5},{2,10},{6,14},... | collective-permute-start | bytes 331784 | tf_op jit(solution)/shard_map/ppermute | solution.py:72
  126.2 19.1 %collective-permute-start.16 = (bf16[128,1536]{1,0:T(8,128)(2,1)S(1)}, bf16[128,1536]{1,0:T(8,128)(2,1)}, u32[]{:S(2)}, u32[]{:S(2)}) collective-permute-start(bf16[128,1536]{1,0:T(8,128)(2,1)S(1)} %get-tuple-element.200), channel_id=1, source_target_pairs={{0,4},{4,8},{8,12},{12,0},{1,5},{5,9},{9,13},{13,1},{2,6},{6,10},{... | collective-permute-start | bytes 1179656 | tf_op jit(solution)/shard_map/ppermute | solution.py:72
  165.0 20.3 %collective-permute-start.19 = (bf16[128,1536]{1,0:T(8,128)(2,1)S(1)}, bf16[128,1536]{1,0:T(8,128)(2,1)}, u32[]{:S(2)}, u32[]{:S(2)}) collective-permute-start(bf16[128,1536]{1,0:T(8,128)(2,1)S(1)} %fusion.56), channel_id=1, source_target_pairs={{0,4},{4,8},{8,12},{12,0},{1,5},{5,9},{9,13},{13,1},{2,6},{6,10},{... | collective-permute-start | bytes 1179656 | tf_op jit(solution)/shard_map/ppermute | solution.py:72
  165.5 19.8 %collective-permute-start.20 = (bf16[128,1536]{1,0:T(8,128)(2,1)S(1)}, bf16[128,1536]{1,0:T(8,128)(2,1)}, u32[]{:S(2)}, u32[]{:S(2)}) collective-permute-start(bf16[128,1536]{1,0:T(8,128)(2,1)S(1)} %fusion.56), channel_id=1, source_target_pairs={{0,8},{4,12},{8,0},{12,4},{1,9},{5,13},{9,1},{13,5},{2,10},{6,14},... | collective-permute-start | bytes 1179656 | tf_op jit(solution)/shard_map/ppermute | solution.py:72
  166.9 18.6 %collective-permute-start.21 = (bf16[128,1536]{1,0:T(8,128)(2,1)S(1)}, bf16[128,1536]{1,0:T(8,128)(2,1)}, u32[]{:S(2)}, u32[]{:S(2)}) collective-permute-start(bf16[128,1536]{1,0:T(8,128)(2,1)S(1)} %fusion.56), channel_id=1, source_target_pairs={{0,12},{4,0},{8,4},{12,8},{1,13},{5,1},{9,5},{13,9},{2,14},{6,2},{... | collective-permute-start | bytes 1179656 | tf_op jit(solution)/shard_map/ppermute | solution.py:72
  192.7 24.2 %collective-permute-start.24 = (bf16[128,1920]{1,0:T(8,128)(2,1)S(1)}, bf16[128,1920]{1,0:T(8,128)(2,1)S(1)}, u32[]{:S(2)}, u32[]{:S(2)}) collective-permute-start(bf16[128,1920]{1,0:T(8,128)(2,1)S(1)} %get-tuple-element.474), channel_id=1, source_target_pairs={{0,8},{4,12},{8,0},{12,4},{1,9},{5,13},{9,1},{13,5},{2,10},{6,14},... | collective-permute-start | bytes 1474568 | tf_op jit(solution)/shard_map/ppermute | solution.py:72
  195.4 21.5 %collective-permute-start.25 = (bf16[128,1920]{1,0:T(8,128)(2,1)S(1)}, bf16[128,1920]{1,0:T(8,128)(2,1)S(1)}, u32[]{:S(2)}, u32[]{:S(2)}) collective-permute-start(bf16[128,1920]{1,0:T(8,128)(2,1)S(1)} %get-tuple-element.472), channel_id=1, source_target_pairs={{0,12},{4,0},{8,4},{12,8},{1,13},{5,1},{9,5},{13,9},{2,14},{6,2},{... | collective-permute-start | bytes 1474568 | tf_op jit(solution)/shard_map/ppermute | solution.py:72
  227.6 22.4 %collective-permute-start.30 = (bf16[512,1536]{1,0:T(8,128)(2,1)}, bf16[512,1536]{1,0:T(8,128)(2,1)}, u32[]{:S(2)}, u32[]{:S(2)}) collective-permute-start(bf16[512,1536]{1,0:T(8,128)(2,1)} %pad_maximum_fusion.11), channel_id=1, source_target_pairs={{0,1},{1,0},{2,3},{3,2},{4,5},{5,4},{6,7},{7,6},{8,9},{9,8},{10,11... | collective-permute-start | bytes 4718600 | tf_op jit(solution)/shard_map/ppermute | solution.py:52
  228.0 24.7 %collective-permute-start.27 = (bf16[128,1536]{1,0:T(8,128)(2,1)}, bf16[128,1536]{1,0:T(8,128)(2,1)}, u32[]{:S(2)}, u32[]{:S(2)}) collective-permute-start(bf16[128,1536]{1,0:T(8,128)(2,1)} %get-tuple-element.229), channel_id=1, source_target_pairs={{0,12},{4,0},{8,4},{12,8},{1,13},{5,1},{9,5},{13,9},{2,14},{6,2},{... | collective-permute-start | bytes 1179656 | tf_op jit(solution)/shard_map/ppermute | solution.py:72
  230.1 22.6 %collective-permute-start.28 = (bf16[128,1536]{1,0:T(8,128)(2,1)}, bf16[128,1536]{1,0:T(8,128)(2,1)}, u32[]{:S(2)}, u32[]{:S(2)}) collective-permute-start(bf16[128,1536]{1,0:T(8,128)(2,1)} %get-tuple-element.230), channel_id=1, source_target_pairs={{0,8},{4,12},{8,0},{12,4},{1,9},{5,13},{9,1},{13,5},{2,10},{6,14},... | collective-permute-start | bytes 1179656 | tf_op jit(solution)/shard_map/ppermute | solution.py:72
  230.4 22.3 %collective-permute-start.29 = (bf16[128,1536]{1,0:T(8,128)(2,1)}, bf16[128,1536]{1,0:T(8,128)(2,1)}, u32[]{:S(2)}, u32[]{:S(2)}) collective-permute-start(bf16[128,1536]{1,0:T(8,128)(2,1)} %get-tuple-element.231), channel_id=1, source_target_pairs={{0,4},{4,8},{8,12},{12,0},{1,5},{5,9},{9,13},{13,1},{2,6},{6,10},{... | collective-permute-start | bytes 1179656 | tf_op jit(solution)/shard_map/ppermute | solution.py:72
  260.1 19.4 %collective-permute-start.33 = (bf16[128,1536]{1,0:T(8,128)(2,1)}, bf16[128,1536]{1,0:T(8,128)(2,1)S(1)}, u32[]{:S(2)}, u32[]{:S(2)}) collective-permute-start(bf16[128,1536]{1,0:T(8,128)(2,1)} %get-tuple-element.243), channel_id=1, source_target_pairs={{0,8},{4,12},{8,0},{12,4},{1,9},{5,13},{9,1},{13,5},{2,10},{6,14},... | collective-permute-start | bytes 1179656 | tf_op jit(solution)/shard_map/ppermute | solution.py:72
  261.6 17.9 %collective-permute-start.34 = (bf16[128,1536]{1,0:T(8,128)(2,1)}, bf16[128,1536]{1,0:T(8,128)(2,1)}, u32[]{:S(2)}, u32[]{:S(2)}) collective-permute-start(bf16[128,1536]{1,0:T(8,128)(2,1)} %get-tuple-element.243), channel_id=1, source_target_pairs={{0,12},{4,0},{8,4},{12,8},{1,13},{5,1},{9,5},{13,9},{2,14},{6,2},{... | collective-permute-start | bytes 1179656 | tf_op jit(solution)/shard_map/ppermute | solution.py:72
  287.8 21.2 %collective-permute-start.39 = (bf16[512,1536]{1,0:T(8,128)(2,1)S(1)}, bf16[512,1536]{1,0:T(8,128)(2,1)S(1)}, u32[]{:S(2)}, u32[]{:S(2)}) collective-permute-start(bf16[512,1536]{1,0:T(8,128)(2,1)S(1)} %pad_maximum_fusion.12), channel_id=1, source_target_pairs={{0,1},{1,0},{2,3},{3,2},{4,5},{5,4},{6,7},{7,6},{8,9},{9,8},{10,11... | collective-permute-start | bytes 4718600 | tf_op jit(solution)/shard_map/ppermute | solution.py:52
  288.3 22.6 %collective-permute-start.40 = (bf16[512,1536]{1,0:T(8,128)(2,1)S(1)}, bf16[512,1536]{1,0:T(8,128)(2,1)S(1)}, u32[]{:S(2)}, u32[]{:S(2)}) collective-permute-start(bf16[512,1536]{1,0:T(8,128)(2,1)S(1)} %slice.520), channel_id=1, source_target_pairs={{0,1},{1,0},{2,3},{3,2},{4,5},{5,4},{6,7},{7,6},{8,9},{9,8},{10,11... | collective-permute-start | bytes 4718600 | tf_op jit(solution)/shard_map/ppermute | solution.py:52
  290.1 18.8 %collective-permute-start.37 = (bf16[128,1536]{1,0:T(8,128)(2,1)S(1)}, bf16[128,1536]{1,0:T(8,128)(2,1)S(1)}, u32[]{:S(2)}, u32[]{:S(2)}) collective-permute-start(bf16[128,1536]{1,0:T(8,128)(2,1)S(1)} %get-tuple-element.250), channel_id=1, source_target_pairs={{0,8},{4,12},{8,0},{12,4},{1,9},{5,13},{9,1},{13,5},{2,10},{6,14},... | collective-permute-start | bytes 1179656 | tf_op jit(solution)/shard_map/ppermute | solution.py:72
  291.6 17.3 %collective-permute-start.38 = (bf16[128,1536]{1,0:T(8,128)(2,1)S(1)}, bf16[128,1536]{1,0:T(8,128)(2,1)S(1)}, u32[]{:S(2)}, u32[]{:S(2)}) collective-permute-start(bf16[128,1536]{1,0:T(8,128)(2,1)S(1)} %get-tuple-element.250), channel_id=1, source_target_pairs={{0,12},{4,0},{8,4},{12,8},{1,13},{5,1},{9,5},{13,9},{2,14},{6,2},{... | collective-permute-start | bytes 1179656 | tf_op jit(solution)/shard_map/ppermute | solution.py:72
  321.6 23.1 %collective-permute-start.42 = (bf16[272,384]{1,0:T(8,128)(2,1)S(1)}, bf16[272,384]{1,0:T(8,128)(2,1)}, u32[]{:S(2)}, u32[]{:S(2)}) collective-permute-start(bf16[272,384]{1,0:T(8,128)(2,1)S(1)} %get-tuple-element.421), channel_id=1, source_target_pairs={{0,4},{4,8},{8,12},{12,0},{1,5},{5,9},{9,13},{13,1},{2,6},{6,10},{... | collective-permute-start | bytes 626696 | tf_op jit(solution)/shard_map/ppermute | solution.py:72
  323.0 21.7 %collective-permute-start.43 = (bf16[272,384]{1,0:T(8,128)(2,1)}, bf16[272,384]{1,0:T(8,128)(2,1)}, u32[]{:S(2)}, u32[]{:S(2)}) collective-permute-start(bf16[272,384]{1,0:T(8,128)(2,1)} %get-tuple-element.420), channel_id=1, source_target_pairs={{0,8},{4,12},{8,0},{12,4},{1,9},{5,13},{9,1},{13,5},{2,10},{6,14},... | collective-permute-start | bytes 626696 | tf_op jit(solution)/shard_map/ppermute | solution.py:72
  325.1 19.6 %collective-permute-start.44 = (bf16[272,384]{1,0:T(8,128)(2,1)}, bf16[272,384]{1,0:T(8,128)(2,1)}, u32[]{:S(2)}, u32[]{:S(2)}) collective-permute-start(bf16[272,384]{1,0:T(8,128)(2,1)} %get-tuple-element.419), channel_id=1, source_target_pairs={{0,12},{4,0},{8,4},{12,8},{1,13},{5,1},{9,5},{13,9},{2,14},{6,2},{... | collective-permute-start | bytes 626696 | tf_op jit(solution)/shard_map/ppermute | solution.py:72
  325.9 35.8 %collective-permute-start.45 = (bf16[128,1536]{1,0:T(8,128)(2,1)}, bf16[128,1536]{1,0:T(8,128)(2,1)S(1)}, u32[]{:S(2)}, u32[]{:S(2)}) collective-permute-start(bf16[128,1536]{1,0:T(8,128)(2,1)} %get-tuple-element.285), channel_id=1, source_target_pairs={{0,12},{4,0},{8,4},{12,8},{1,13},{5,1},{9,5},{13,9},{2,14},{6,2},{... | collective-permute-start | bytes 1179656 | tf_op jit(solution)/shard_map/ppermute | solution.py:72
  326.2 35.5 %collective-permute-start.46 = (bf16[128,1536]{1,0:T(8,128)(2,1)}, bf16[128,1536]{1,0:T(8,128)(2,1)S(1)}, u32[]{:S(2)}, u32[]{:S(2)}) collective-permute-start(bf16[128,1536]{1,0:T(8,128)(2,1)} %get-tuple-element.286), channel_id=1, source_target_pairs={{0,8},{4,12},{8,0},{12,4},{1,9},{5,13},{9,1},{13,5},{2,10},{6,14},... | collective-permute-start | bytes 1179656 | tf_op jit(solution)/shard_map/ppermute | solution.py:72
  344.7 17.1 %collective-permute-start.47 = (bf16[128,1536]{1,0:T(8,128)(2,1)}, bf16[128,1536]{1,0:T(8,128)(2,1)S(1)}, u32[]{:S(2)}, u32[]{:S(2)}) collective-permute-start(bf16[128,1536]{1,0:T(8,128)(2,1)} %get-tuple-element.287), channel_id=1, source_target_pairs={{0,4},{4,8},{8,12},{12,0},{1,5},{5,9},{9,13},{13,1},{2,6},{6,10},{... | collective-permute-start | bytes 1179656 | tf_op jit(solution)/shard_map/ppermute | solution.py:72
  344.7 17.1 %collective-permute-start.48 = (bf16[96,2304]{1,0:T(8,128)(2,1)}, bf16[96,2304]{1,0:T(8,128)(2,1)}, u32[]{:S(2)}, u32[]{:S(2)}) collective-permute-start(bf16[96,2304]{1,0:T(8,128)(2,1)} %reduce-scatter.2.cloned.1.call-done), channel_id=1, source_target_pairs={{0,2},{2,0},{1,3},{3,1},{4,6},{6,4},{5,7},{7,5},{8,10},{10,8},{9,1... | collective-permute-start | bytes 1327112 | tf_op jit(solution)/shard_map/ppermute | solution.py:96
  376.2 98.9 %all-to-all-start = ((bf16[16,96,1536]{2,1,0:T(8,128)(2,1)}), bf16[16,96,1536]{2,1,0:T(8,128)(2,1)}, u32[]{:S(2)}, u32[]{:S(2)}) async-start(bf16[16,96,1536]{2,1,0:T(8,128)(2,1)} %bitcast.113), calls=%async_computation.1 | async-start | bytes 9437184 | tf_op jit(solution)/shard_map/all_to_all | solution.py:56
  386.7 19.7 %collective-permute-start.50 = (bf16[128,1536]{1,0:T(8,128)(2,1)}, bf16[128,1536]{1,0:T(8,128)(2,1)}, u32[]{:S(2)}, u32[]{:S(2)}) collective-permute-start(bf16[128,1536]{1,0:T(8,128)(2,1)} %get-tuple-element.297), channel_id=1, source_target_pairs={{0,12},{4,0},{8,4},{12,8},{1,13},{5,1},{9,5},{13,9},{2,14},{6,2},{... | collective-permute-start | bytes 1179656 | tf_op jit(solution)/shard_map/ppermute | solution.py:72
  389.7 20.7 %collective-permute-start.52 = (bf16[128,1536]{1,0:T(8,128)(2,1)}, bf16[128,1536]{1,0:T(8,128)(2,1)}, u32[]{:S(2)}, u32[]{:S(2)}) collective-permute-start(bf16[128,1536]{1,0:T(8,128)(2,1)} %get-tuple-element.299), channel_id=1, source_target_pairs={{0,4},{4,8},{8,12},{12,0},{1,5},{5,9},{9,13},{13,1},{2,6},{6,10},{... | collective-permute-start | bytes 1179656 | tf_op jit(solution)/shard_map/ppermute | solution.py:72
  411.7 62.8 %collective-permute-start.56 = (bf16[2,96,2304]{2,1,0:T(8,128)(2,1)S(1)}, bf16[2,96,2304]{2,1,0:T(8,128)(2,1)}, u32[]{:S(2)}, u32[]{:S(2)}) collective-permute-start(bf16[2,96,2304]{2,1,0:T(8,128)(2,1)S(1)} %pad_maximum_fusion.14), channel_id=1, source_target_pairs={{0,4},{4,8},{8,12},{12,0},{1,5},{5,9},{9,13},{13,1},{2,6},{6,10},{... | collective-permute-start | bytes 2654216 | tf_op jit(solution)/shard_map/ppermute | solution.py:72
  412.0 62.5 %collective-permute-start.57 = (bf16[2,96,2304]{2,1,0:T(8,128)(2,1)S(1)}, bf16[2,96,2304]{2,1,0:T(8,128)(2,1)}, u32[]{:S(2)}, u32[]{:S(2)}) collective-permute-start(bf16[2,96,2304]{2,1,0:T(8,128)(2,1)S(1)} %pad_maximum_fusion.14), channel_id=1, source_target_pairs={{0,8},{4,12},{8,0},{12,4},{1,9},{5,13},{9,1},{13,5},{2,10},{6,14},... | collective-permute-start | bytes 2654216 | tf_op jit(solution)/shard_map/ppermute | solution.py:72
  413.0 61.5 %collective-permute-start.58 = (bf16[2,96,2304]{2,1,0:T(8,128)(2,1)S(1)}, bf16[2,96,2304]{2,1,0:T(8,128)(2,1)}, u32[]{:S(2)}, u32[]{:S(2)}) collective-permute-start(bf16[2,96,2304]{2,1,0:T(8,128)(2,1)S(1)} %pad_maximum_fusion.14), channel_id=1, source_target_pairs={{0,12},{4,0},{8,4},{12,8},{1,13},{5,1},{9,5},{13,9},{2,14},{6,2},{... | collective-permute-start | bytes 2654216 | tf_op jit(solution)/shard_map/ppermute | solution.py:72
  420.5 34.7 %collective-permute-start.59 = (bf16[130,384]{1,0:T(8,128)(2,1)}, bf16[130,384]{1,0:T(8,128)(2,1)S(1)}, u32[]{:S(2)}, u32[]{:S(2)}) collective-permute-start(bf16[130,384]{1,0:T(8,128)(2,1)} %get-tuple-element.431), channel_id=1, source_target_pairs={{0,12},{4,0},{8,4},{12,8},{1,13},{5,1},{9,5},{13,9},{2,14},{6,2},{... | collective-permute-start | bytes 299528 | tf_op jit(solution)/shard_map/ppermute | solution.py:72
  421.2 36.5 %collective-permute-start.60 = (bf16[130,384]{1,0:T(8,128)(2,1)}, bf16[130,384]{1,0:T(8,128)(2,1)}, u32[]{:S(2)}, u32[]{:S(2)}) collective-permute-start(bf16[130,384]{1,0:T(8,128)(2,1)} %get-tuple-element.433), channel_id=1, source_target_pairs={{0,8},{4,12},{8,0},{12,4},{1,9},{5,13},{9,1},{13,5},{2,10},{6,14},... | collective-permute-start | bytes 299528 | tf_op jit(solution)/shard_map/ppermute | solution.py:72
  492.0 50.1 %collective-permute-start.64 = (bf16[2,96,1536]{2,1,0:T(8,128)(2,1)S(1)}, bf16[2,96,1536]{2,1,0:T(8,128)(2,1)}, u32[]{:S(2)}, u32[]{:S(2)}) collective-permute-start(bf16[2,96,1536]{2,1,0:T(8,128)(2,1)S(1)} %pad_maximum_fusion.16), channel_id=1, source_target_pairs={{0,4},{4,8},{8,12},{12,0},{1,5},{5,9},{9,13},{13,1},{2,6},{6,10},{... | collective-permute-start | bytes 1769480 | tf_op jit(solution)/shard_map/ppermute | solution.py:72
  492.2 49.9 %collective-permute-start.65 = (bf16[2,96,1536]{2,1,0:T(8,128)(2,1)S(1)}, bf16[2,96,1536]{2,1,0:T(8,128)(2,1)}, u32[]{:S(2)}, u32[]{:S(2)}) collective-permute-start(bf16[2,96,1536]{2,1,0:T(8,128)(2,1)S(1)} %pad_maximum_fusion.16), channel_id=1, source_target_pairs={{0,8},{4,12},{8,0},{12,4},{1,9},{5,13},{9,1},{13,5},{2,10},{6,14},... | collective-permute-start | bytes 1769480 | tf_op jit(solution)/shard_map/ppermute | solution.py:72
  495.7 46.4 %collective-permute-start.66 = (bf16[2,96,1536]{2,1,0:T(8,128)(2,1)S(1)}, bf16[2,96,1536]{2,1,0:T(8,128)(2,1)}, u32[]{:S(2)}, u32[]{:S(2)}) collective-permute-start(bf16[2,96,1536]{2,1,0:T(8,128)(2,1)S(1)} %pad_maximum_fusion.16), channel_id=1, source_target_pairs={{0,12},{4,0},{8,4},{12,8},{1,13},{5,1},{9,5},{13,9},{2,14},{6,2},{... | collective-permute-start | bytes 1769480 | tf_op jit(solution)/shard_map/ppermute | solution.py:72
  496.7 27.6 %collective-permute-start.71 = (bf16[2,130,384]{2,1,0:T(8,128)(2,1)S(1)}, bf16[2,130,384]{2,1,0:T(8,128)(2,1)S(1)}, u32[]{:S(2)}, u32[]{:S(2)}) collective-permute-start(bf16[2,130,384]{2,1,0:T(8,128)(2,1)S(1)} %pad_maximum_fusion.23), channel_id=1, source_target_pairs={{0,4},{4,8},{8,12},{12,0},{1,5},{5,9},{9,13},{13,1},{2,6},{6,10},{... | collective-permute-start | bytes 599048 | tf_op jit(solution)/shard_map/ppermute | solution.py:72
  500.5 41.5 %collective-permute-start.72 = (bf16[2,130,384]{2,1,0:T(8,128)(2,1)S(1)}, bf16[2,130,384]{2,1,0:T(8,128)(2,1)S(1)}, u32[]{:S(2)}, u32[]{:S(2)}) collective-permute-start(bf16[2,130,384]{2,1,0:T(8,128)(2,1)S(1)} %pad_maximum_fusion.23), channel_id=1, source_target_pairs={{0,8},{4,12},{8,0},{12,4},{1,9},{5,13},{9,1},{13,5},{2,10},{6,14},... | collective-permute-start | bytes 599048 | tf_op jit(solution)/shard_map/ppermute | solution.py:72
  524.3 17.7 %collective-permute-start.73 = (bf16[2,130,384]{2,1,0:T(8,128)(2,1)S(1)}, bf16[2,130,384]{2,1,0:T(8,128)(2,1)}, u32[]{:S(2)}, u32[]{:S(2)}) collective-permute-start(bf16[2,130,384]{2,1,0:T(8,128)(2,1)S(1)} %pad_maximum_fusion.23), channel_id=1, source_target_pairs={{0,12},{4,0},{8,4},{12,8},{1,13},{5,1},{9,5},{13,9},{2,14},{6,2},{... | collective-permute-start | bytes 599048 | tf_op jit(solution)/shard_map/ppermute | solution.py:72
  542.1 28.9 %collective-permute-start.74 = (f32[4,128]{1,0:T(4,128)S(1)}, f32[4,128]{1,0:T(4,128)S(1)}, u32[]{:S(2)}, u32[]{:S(2)}) collective-permute-start(f32[4,128]{1,0:T(4,128)S(1)} %bitcast.137), channel_id=1, source_target_pairs={{0,2},{2,0},{1,3},{3,1},{4,6},{6,4},{5,7},{7,5},{8,10},{10,8},{9,1... | collective-permute-start | bytes 6152 | tf_op jit(solution)/shard_map/ppermute | solution.py:723
  (84 other events, 824.4 us)
Sparse Core Ops, SparseCore 0:
  14.6 74.7 all-gather.4
  92.1 64.5 all-gather.6
  252.8 81.5 reduce-scatter.1

commit v3 on v2

--- a/solution.py
+++ b/solution.py
@@ -393,8 +393,9 @@
     )(*flat)
 
 
-def by_rows(blocks):
-    return jnp.concatenate([b[:ROWS, k * QUARTER : (k + 1) * QUARTER] for k in range(2) for b in blocks], axis=0)
+def by_rows(blocks, at):
+    starts = (at, at + QUARTER)
+    return jnp.concatenate([b[:ROWS, k : k + QUARTER] for k in starts for b in blocks], axis=0)
 
 
 def attn_products_kernel(one, grad, back, att, context, share, two, three, *rest):
@@ -406,7 +407,7 @@
     at = O_AT + WIDE
     out[:, at : at + 2 * QUARTER] = dot_tn(context[...], share[...]).astype(bf16)
     at += 2 * QUARTER
-    pieces = [dot_tn(left[...], by_rows(right)).astype(bf16) for left, right in ((two, cq), (three, catt))]
+    pieces = [dot_tn(two[...], by_rows(cq, 0)).astype(bf16), dot_tn(three[...], by_rows(catt, D)).astype(bf16)]
     out[:, at:] = jnp.concatenate(pieces, axis=1)
 
 
@@ -430,97 +431,95 @@
     )(one, grad, back, att, context, share, two, three, *cq, *catt)
 
 
-def finish_feed_kernel(at, parts, gain, grad_in, grad_down):
-    width = grad_down.shape[1]
-    for kind in range(2):
-        grad_in[kind] = parts[0, :, kind * width : (kind + 1) * width].astype(f32) * gain[...]
-    grad_down[...] = parts[0, :, 2 * width :].astype(f32)
-
-
-def held_at(h, q, at):
-    return (at[0] + 4 - q) % 4 * 2 + jnp.where(h == at[1], 0, 1)
-
-
-def finish_feed(at, parts, gain):
-    rows, width = parts.shape[1], parts.shape[2] // 3
+def held_at(q, x):
+    return (x + 4 - q) % 4
+
+
+def finish_feed_kernel(at, b0, b1, b2, b3, gain, grad_in, grad_down, held):
+    rows, width = b0.shape[1], grad_down.shape[1] // 4
+    for k, block in enumerate((b0, b1, b2, b3)):
+        held[k] = block[...]
+    for h in range(2):
+        scale = gain[h * rows : (h + 1) * rows, :]
+        for q in range(4):
+            part = held[held_at(q, at[0]), (at[1] + h) % 2]
+            to = pl.ds(q * width, width)
+            for kind in range(2):
+                grad_in[kind, h * rows : (h + 1) * rows, to] = part[:, kind * width : (kind + 1) * width].astype(f32) * scale
+            grad_down[h * rows : (h + 1) * rows, to] = part[:, 2 * width :].astype(f32)
+
+
+def finish_feed(at, blocks, gain):
+    _, rows, columns = blocks[0].shape
+    width = columns // 3
     return pl.pallas_call(
         finish_feed_kernel,
-        grid_spec=pltpu.PrefetchScalarGridSpec(
-            num_scalar_prefetch=1,
-            grid=(2, 4),
-            in_specs=[
-                pl.BlockSpec((1, rows, 3 * width), lambda h, q, at: (held_at(h, q, at), 0, 0)),
-                pl.BlockSpec((rows, 1), lambda h, q, at: (h, 0)),
-            ],
-            out_specs=(
-                pl.BlockSpec((2, rows, width), lambda h, q, at: (0, h, q)),
-                pl.BlockSpec((rows, width), lambda h, q, at: (h, q)),
-            ),
-        ),
+        in_specs=[pl.BlockSpec(memory_space=pltpu.SMEM)] + [pl.BlockSpec(memory_space=pltpu.VMEM)] * 5,
         out_shape=(
             jax.ShapeDtypeStruct((2, 2 * rows, 4 * width), f32),
             jax.ShapeDtypeStruct((2 * rows, 4 * width), f32),
         ),
+        scratch_shapes=[pltpu.VMEM((4, 2, rows, columns), bf16)],
         cost_estimate=pl.CostEstimate(flops=1 << 22, transcendentals=0, bytes_accessed=11 << 20),
-    )(at, parts, gain)
-
-
-def finish_cond_kernel(at, parts, out):
-    width = parts.shape[2]
-    for h in range(2):
-        for q in range(4):
-            out[h, :, q * width : (q + 1) * width] = parts[held_at(h, q, at)].astype(f32)
-
-
-def finish_cond(at, parts):
-    count, width = parts.shape[1:]
+    )(at, *blocks, gain)
+
+
+def finish_cond_kernel(at, near, far, out):
+    width = near.shape[2]
+    for q in range(4):
+        place = held_at(q, at[0])
+        out[at[1], :, q * width : (q + 1) * width] = near[place].astype(f32)
+        out[1 - at[1], :, q * width : (q + 1) * width] = far[place].astype(f32)
+
+
+def finish_cond(at, near, far):
+    _, count, width = near.shape
     return pl.pallas_call(
         finish_cond_kernel,
-        in_specs=[pl.BlockSpec(memory_space=pltpu.SMEM), pl.BlockSpec(memory_space=pltpu.VMEM)],
+        in_specs=[pl.BlockSpec(memory_space=pltpu.SMEM)] + [pl.BlockSpec(memory_space=pltpu.VMEM)] * 2,
         out_shape=jax.ShapeDtypeStruct((2, count, 4 * width), f32),
         cost_estimate=pl.CostEstimate(flops=1 << 20, transcendentals=0, bytes_accessed=3 << 20),
-    )(at, parts)
-
-
-def finish_columns(places, parts, gain, other_gain):
-    rows, quarter = parts.shape[1], parts.shape[2] // 8
-    width = 4 * quarter
-
-    def kernel(places, parts, gain, other_gain, proj, out, keyval, query, cross):
-        h = pl.program_id(0)
+    )(at, near, far)
+
+
+def finish_columns_kernel(at, b0, b1, b2, b3, gain, other_gain, proj, out, keyval, query, cross, held):
+    rows = b0.shape[1]
+    for k, block in enumerate((b0, b1, b2, b3)):
+        held[k] = block[...]
+    for h in range(2):
+        to = pl.ds(h * rows, rows)
+        parts = [held[held_at(q, at[0]), (at[1] + h) % 2] for q in range(4)]
 
         def kind_of(kind):
-            row = [parts[places[4 * h + q], :, kind * quarter : (kind + 1) * quarter].astype(f32) for q in range(4)]
+            row = [part[:, kind * QUARTER : (kind + 1) * QUARTER].astype(f32) for part in parts]
             return jnp.concatenate(row, axis=1)
 
         for place, kind in enumerate((0, 2, 1)):
-            proj[place] = kind_of(kind) * gain[...]
-        out[...] = kind_of(3)
-        keyval[0] = kind_of(4)
-        keyval[1] = kind_of(5)
-        query[...] = kind_of(6) * other_gain[...]
-        cross[...] = kind_of(7)
-
-    def stacked(count):
-        return pl.BlockSpec((count, rows, width), lambda h, places: (0, h, 0)), jax.ShapeDtypeStruct((count, 2 * rows, width), f32)
-
-    plain = pl.BlockSpec((rows, width), lambda h, places: (h, 0)), jax.ShapeDtypeStruct((2 * rows, width), f32)
-    outs = [stacked(3), plain, stacked(2), plain, plain]
-    return pl.pallas_call(
-        kernel,
-        grid_spec=pltpu.PrefetchScalarGridSpec(
-            num_scalar_prefetch=1,
-            grid=(2,),
-            in_specs=[
-                pl.BlockSpec(parts.shape, lambda h, places: (0, 0, 0)),
-                pl.BlockSpec((rows, 1), lambda h, places: (h, 0)),
-                pl.BlockSpec((rows, 1), lambda h, places: (h, 0)),
-            ],
-            out_specs=[spec for spec, _ in outs],
+            proj[place, to, :] = kind_of(kind) * gain[to, :]
+        out[to, :] = kind_of(3)
+        keyval[0, to, :] = kind_of(4)
+        keyval[1, to, :] = kind_of(5)
+        query[to, :] = kind_of(6) * other_gain[to, :]
+        cross[to, :] = kind_of(7)
+
+
+def finish_columns(at, blocks, gain, other_gain):
+    _, rows, columns = blocks[0].shape
+    width = columns // 2
+    plain = jax.ShapeDtypeStruct((2 * rows, width), f32)
+    return pl.pallas_call(
+        finish_columns_kernel,
+        in_specs=[pl.BlockSpec(memory_space=pltpu.SMEM)] + [pl.BlockSpec(memory_space=pltpu.VMEM)] * 6,
+        out_shape=(
+            jax.ShapeDtypeStruct((3, 2 * rows, width), f32),
+            plain,
+            jax.ShapeDtypeStruct((2, 2 * rows, width), f32),
+            plain,
+            plain,
         ),
-        out_shape=[shape for _, shape in outs],
+        scratch_shapes=[pltpu.VMEM((4, 2, rows, columns), bf16)],
         cost_estimate=pl.CostEstimate(flops=1 << 20, transcendentals=0, bytes_accessed=4 << 20),
-    )(places, parts, gain, other_gain)
+    )(at, *blocks, gain, other_gain)
 
 
 def per_device(
@@ -623,29 +622,24 @@
     blocks, carried, grad_gate_up, hidden = both(scatter_half(partial), carried, grad_gate_up, hidden)
     mine_two = jnp.concatenate([block[:, :D] for block in carried], axis=0)
     att_quarter = carried
-    grad_three, grad_feed, feed_part, full_two = both(
-        scatter_x(blocks),
-        products((full_three, grad_gate_up), (full_grad, hidden)),
-        dot_nt(hidden, w_down).astype(bf16),
-        with_partner(mine_two),
+    grad_three, grad_feed, full_two = both(
+        scatter_x(blocks), products((full_three, grad_gate_up), (full_grad, hidden)), with_partner(mine_two)
     )
     sum_feed = scatter_plane(grad_feed)
     grad_resid_two = upstream.astype(f32) + unit_norm_back(norm_three, scale_three, summed(grad_three))
 
-    sent_two, feed_part = both(grad_resid_two.astype(bf16), feed_part)
+    sent_two = grad_resid_two.astype(bf16)
     mine_two = gather_half(sent_two)
     pair_grad = pair_rows(sent_two)
     grad_cross_att = dot(pair_grad, w_co).astype(bf16)
     grad_cq, quarters = cross_backward(scalars, cross_q, cond_kv, bias, grad_cross_att)
-    grad_cq, mine_two, feed_part = both(grad_cq, mine_two, feed_part)
+    grad_cq, mine_two = both(grad_cq, mine_two)
     grad_two = pair_sum(dot_nt(grad_cq, w_cq))
     grad_resid_one = grad_resid_two + unit_norm_back(norm_two, scale_two, grad_two)
 
-    sent_back, mine_two, quarters, feed_part, att_quarter = both(
-        grad_resid_one.astype(bf16), mine_two, quarters, feed_part, att_quarter
-    )
-    mine_back, grad_two_all, feed_half, att_quarter = both(
-        gather_half(sent_back), with_partner(mine_two), scatter_half(feed_part), [block[:, D:] for block in att_quarter]
+    sent_back, mine_two, quarters, hidden = both(grad_resid_one.astype(bf16), mine_two, quarters, hidden)
+    mine_back, grad_two_all, feed_half = both(
+        gather_half(sent_back), with_partner(mine_two), scatter_half(dot_nt(hidden, w_down))
     )
     full_back, quarters, feed_half = both(with_partner(mine_back), quarters, feed_half)
     grad_att, quarters, feed_half = both(dot(full_back, w_out).astype(bf16), quarters, feed_half)
@@ -654,27 +648,34 @@
     grad_qvk = attn_backward(qs, ks, vs, grad_att, lse, cosine, sine)
     grad_qvk, quarter_parts, sum_feed = both(grad_qvk, quarter_parts, sum_feed)
     ckv_share = summed([part[ROWS:] for part in quarter_parts]).astype(bf16)
+    partial, grad_qvk, ckv_share, sum_feed = both(dot_nt(grad_qvk, w_qvk), grad_qvk, ckv_share, sum_feed)
     grad_attn = attn_products(
         full_one, grad_qvk, full_back, attended, own_context, ckv_share, full_two, grad_two_all, quarter_parts, att_quarter
     )
-    grad_attn, grad_qvk, ckv_share, feed_parts, sum_feed_far = both(grad_attn, grad_qvk, ckv_share, feed_parts, to_far(sum_feed))
+    blocks, grad_attn, ckv_share, feed_parts, sum_feed_far = both(
+        scatter_half(partial), grad_attn, ckv_share, feed_parts, to_far(sum_feed)
+    )
     parts_attn = plane_parts(grad_attn)
-    blocks, ckv_share, feed_parts = both(scatter_half(dot_nt(grad_qvk, w_qvk)), ckv_share, feed_parts)
+    feed_all = gather_x(jnp.stack([sum_feed, sum_feed_far]))
     cond_part = dot_nt(ckv_share, w_kv)[:cond_count]
     cond_part = (cond_part + to_partner(cond_part)).astype(bf16)
     feed_branch = summed(feed_parts)
     output = resid_two + feed_branch
-    grad_one, cond_part, sent_out, sum_feed, sum_feed_far = both(
-        scatter_x(blocks), cond_part, permuted(output.astype(bf16)), sum_feed, sum_feed_far
-    )
+    grad_one, cond_part, sent_out = both(scatter_x(blocks), cond_part, permuted(output.astype(bf16)))
     in_grad = grad_resid_one + unit_norm_back(norm_one, scale_one, summed(grad_one))
 
     def columns_of(back):
         return lax.dynamic_slice_in_dim(cond_part, (x + 4 - back) % 4 * (D // 4), D // 4, 1)
 
     cond_parts = scatter_x([columns_of(back) for back in range(4)])
-    cond_own = permuted(summed(cond_parts).astype(bf16))
-    feed_all = gather_x(jnp.stack([sum_feed, sum_feed_far]))
+    cond_near = jnp.stack(gather_x(permuted(summed(cond_parts).astype(bf16))))
+    at = jnp.stack([x, yh]).astype(jnp.int32)
+
+    def column(gain):
+        return gain.astype(f32)[:, None]
+
+    grad_feed_in, grad_feed_out = finish_feed(at, feed_all, column(gain_feed))
+    grad_feed_in = grad_feed_in.transpose(1, 0, 2)
 
     def row_sums(w, grad):
         sums = jnp.sum(w.astype(f32) * grad.astype(f32), axis=1)
@@ -687,37 +688,22 @@
 
     moved_in = lax.ppermute(permuted(in_grad.astype(bf16)), ("yh", "tp"), SWAP)
     moved_out = lax.ppermute(sent_out, ("yh", "tp"), SWAP)
-    parts_attn, moved_in, moved_out, feed_all, small, cond_own = both(parts_attn, moved_in, moved_out, feed_all, small, cond_own)
+    parts_attn, moved_in, moved_out, small, cond_near, grad_feed_in, grad_feed_out = both(
+        parts_attn, moved_in, moved_out, small, cond_near, grad_feed_in, grad_feed_out
+    )
     sum_attn = total(parts_attn)
-    attn_own = sum_attn.astype(bf16)
-    attn_far, cond_far = both(to_far(attn_own), to_far(cond_own))
+    attn_own, cond_near = both(sum_attn.astype(bf16), cond_near)
+    attn_far = to_far(attn_own)
     attn_all = gather_x(jnp.stack([attn_own, attn_far]))
-    cond_all = gather_x(jnp.stack([cond_own, cond_far]))
     more = [row_sums(qvk_cols, sum_attn[:, : 3 * quarter])]
     more += [row_sums(own_cols(cq_half, quarter), sum_attn[:, 6 * quarter : 7 * quarter])]
     small = jnp.concatenate([*more, small]).reshape(4, 128)
     small_blocks = gather_x(small + to_partner(small))
     in_grad = lax.all_gather(moved_in, "tp", axis=0, tiled=False).astype(f32)
     layer_out = lax.all_gather(moved_out, "tp", axis=0, tiled=False)
-    at = jnp.stack([x, yh]).astype(jnp.int32)
-
-    def laid(blocks):
-        stacked = jnp.stack(blocks)
-        return stacked.reshape(8, *stacked.shape[2:])
-
-    def column(gain):
-        return gain.astype(f32)[:, None]
-
-    grad_feed_in, grad_feed_out = finish_feed(at, laid(feed_all), column(gain_feed))
-    grad_feed_in = grad_feed_in.transpose(1, 0, 2)
-    attn_all, small_blocks, cond_all, grad_feed_in, grad_feed_out, in_grad, layer_out = both(
-        attn_all, small_blocks, cond_all, grad_feed_in, grad_feed_out, in_grad, layer_out
-    )
-    cond_grad = finish_cond(at, laid(cond_all))
-
-    block = jnp.arange(8, dtype=jnp.int32)
-    places = (x + 4 - block % 4) % 4 * 2 + jnp.where(block // 4 == yh, 0, 1)
-    proj, out, keyval, query, cross = finish_columns(places, laid(attn_all), column(gain_attn), column(gain_cross))
+    cond_grad = finish_cond(at, cond_near, to_far(cond_near))
+    attn_all, small_blocks, cond_grad, in_grad, layer_out = both(attn_all, small_blocks, cond_grad, in_grad, layer_out)
+    proj, out, keyval, query, cross = finish_columns(at, attn_all, column(gain_attn), column(gain_cross))
     small = jnp.stack(small_blocks)
     small = sum(lax.dynamic_index_in_dim(small, (x + 4 - q) % 4, 0, False) for q in range(4))
     other = lax.ppermute(small, "yh", ((0, 1), (1, 0)))

time: 592 us -> 568 us (0.959)
  starting transfers between devices: 111 us -> 97.4 us
  local copies, waits for them, and re-layouts: 67 us -> 59.3 us
  other arithmetic: 69.8 us -> 62.5 us
    ppermute x51, starting transfers between devices: 66.6 us -> 57.3 us  [along_x(): return lax.ppermute(v, 'x', [(i, (i + step) % 4) for i in range(4)])]
    another operation x4 -> x2, other arithmetic: 8.43 us -> 0.19 us  [per_device(): cond_near = jnp.stack(gather_x(permuted(summed(cond_parts).astype(bf16))))]
    ppermute x1, waiting for transfers between devices: 0.01 us -> 6.67 us  [per_device(): lax.ppermute(lax.dynamic_index_in_dim(hidden_in, tp, 0, False), ('yh', 't...]
    slice x4 -> x0, local copies, waits for them, and re-layouts: 6.17 us -> none  [per_device(): block[:, D:]]
    unnamed x111 -> x121, local copies, waits for them, and re-layouts: 20.2 us -> 19 us
  transfers between devices with their start and end apart: 79 -> 79, of which waited for: 28 -> 33; matrix products, arithmetic and copies ran while one was open for 27% -> 25% of each run, Pallas kernels for 14% -> 14%
where the time goes in v3:
time: 568 us; the launch traced here: 557 us
  waiting for transfers between devices  177 us (31%)
  starting transfers between devices  97.4 us (17%)
  Pallas kernels  79 us (14%)
  other arithmetic  62.5 us (11%)
  local copies, waits for them, and re-layouts  59.3 us (10%)
  matrix products  55.9 us (10%)
  between operations  15.3 us (3%)
  blocking collectives  10.8 us (2%)
    ppermute x51, waiting for transfers between devices, along_x(): return lax.ppermute(v, 'x', [(i, (i + step) % 4) for i in range(4)])  148 us
    ppermute x51, starting transfers between devices, along_x(): return lax.ppermute(v, 'x', [(i, (i + step) % 4) for i in range(4)])  57.3 us
    dot_general x7, matrix products, dot(): return jnp.dot(a, b, preferred_element_type=f32)  29 us
    dot_general x7, matrix products, dot_nt(): lax.dot_general(a, b, (((1,), (1,)), ((), ())), preferred_element_type=f32)  26.9 us
    unnamed x121, local copies, waits for them, and re-layouts  19 us
    pallas_call x1, Pallas kernels, attn_backward(): pl.pallas_call(attn_backward_kernel, in_specs=[pl.BlockSpec(memory_space=...  16.2 us
    ppermute x16, waiting for transfers between devices, to_partner(): return lax.ppermute(v, 'tp', ((0, 1), (1, 0)))  15.7 us
    ppermute x16, starting transfers between devices, to_partner(): return lax.ppermute(v, 'tp', ((0, 1), (1, 0)))  14.9 us
  transfers between devices with their start and end apart: 79, of which 33 were waited for; matrix products, arithmetic and copies ran while one was open for 25% of the time, Pallas kernels for 14%

profile of v3, /device:TPU:1, one launch (start us, length us, event | category | flops | bytes accessed | tf_op | source)
XLA Modules:
  0.0 557.5 jit_solution(11026838006772090752)
XLA Ops:
  15.3 6.2 %collective-permute-start.4 = (bf16[128,1536]{1,0:T(8,128)(2,1)}, bf16[128,1536]{1,0:T(8,128)(2,1)}, u32[]{:S(2)}, u32[]{:S(2)}) collective-permute-start(bf16[128,1536]{1,0:T(8,128)(2,1)} %dynamic-slice_bitcast_fusion.1), channel_id=1, source_target_pairs={{0,0},{1,2},{2,1},{3,3},{4,4},{5,6},{6,5},{7,7},{8,8},{9,10},{10,9... | collective-permute-start | bytes 1179656 | tf_op jit(solution)/shard_map/ppermute | solution.py:560
  23.7 3.1 fusion.60
  26.8 6.7 %collective-permute-done = bf16[128,1536]{1,0:T(8,128)(2,1)S(1)} collective-permute-done((bf16[128,1536]{1,0:T(8,128)(2,1)S(1)}, bf16[128,1536]{1,0:T(8,128)(2,1)S(1)}, u32[]{:S(2)}, u32[]{:S(2)}) %collective-permute-start) | collective-permute-done | bytes 393248 | tf_op jit(solution)/shard_map/ppermute | solution.py:559
  46.7 3.8 collective-permute-done.1
  58.7 8.7 %collective-permute-done.8 = bf16[128,1536]{1,0:T(8,128)(2,1)S(1)} collective-permute-done((bf16[128,1536]{1,0:T(8,128)(2,1)S(1)}, bf16[128,1536]{1,0:T(8,128)(2,1)S(1)}, u32[]{:S(2)}, u32[]{:S(2)}) %collective-permute-start.8) | collective-permute-done | bytes 393248 | tf_op jit(solution)/shard_map/ppermute | solution.py:72
  68.7 9.8 %collective-permute-done.6 = bf16[128,1536]{1,0:T(8,128)(2,1)S(1)} collective-permute-done((bf16[128,1536]{1,0:T(8,128)(2,1)S(1)}, bf16[128,1536]{1,0:T(8,128)(2,1)S(1)}, u32[]{:S(2)}, u32[]{:S(2)}) %collective-permute-start.6) | collective-permute-done | bytes 393248 | tf_op jit(solution)/shard_map/ppermute | solution.py:72
  78.6 3.4 pad_maximum_fusion.one
  90.8 6.7 %fusion.20.qkv = f32[1024,640]{1,0:T(8,128)} fusion(bf16[1024,1536]{1,0:T(8,128)(2,1)} %pad_maximum_fusion.one, bf16[1536,2688]{1,0:T(8,128)(2,1)} %all-gather.5.cloned.1.call-done), kind=kOutput, calls=%fused_computation.39 | convolution fusion | flops 2013265920 | bytes 7733248 | tf_op jit(solution)/shard_map/dot_general | solution.py:40
  101.2 13.5 %shard_map.254 = (bf16[1024,256]{1,0:T(8,128)(2,1)}, bf16[1024,256]{1,0:T(8,128)(2,1)}, bf16[1024,256]{1,0:T(8,128)(2,1)}, bf16[1024,256]{1,0:T(8,128)(2,1)}, f32[8,1024]{1,0:T(8,128)}) custom-call(s32[3]{0:T(128)} %pad_add_fusion.sc, f32[1024,640]{1,0:T(8,128)} %fusion.20.qkv, f32[1024,128]{1,0:T(8,128)} %get-tuple-element.166.cosine, ...), custom_call_target="tpu_custom_call" | custom-call | flops 3221225472 | bytes 8388608 | tf_op jit(solution)/shard_map/pallas_call | solution.py:204
  126.4 6.9 %collective-permute-done.14 = bf16[128,1536]{1,0:T(8,128)(2,1)S(1)} collective-permute-done((bf16[128,1536]{1,0:T(8,128)(2,1)S(1)}, bf16[128,1536]{1,0:T(8,128)(2,1)S(1)}, u32[]{:S(2)}, u32[]{:S(2)}) %collective-permute-start.14) | collective-permute-done | bytes 393248 | tf_op jit(solution)/shard_map/ppermute | solution.py:72
  133.3 3.1 collective-permute-done.15
  136.3 9.4 %collective-permute-done.16 = bf16[128,1536]{1,0:T(8,128)(2,1)} collective-permute-done((bf16[128,1536]{1,0:T(8,128)(2,1)S(1)}, bf16[128,1536]{1,0:T(8,128)(2,1)}, u32[]{:S(2)}, u32[]{:S(2)}) %collective-permute-start.16) | collective-permute-done | bytes 393248 | tf_op jit(solution)/shard_map/ppermute | solution.py:72
  151.0 3.2 fusion.25.cq
  154.9 4.6 shard_map.255
  167.7 5.2 fusion.8
  173.0 3.2 collective-permute-done.21
  177.7 9.2 %collective-permute-done.19 = bf16[128,1536]{1,0:T(8,128)(2,1)} collective-permute-done((bf16[128,1536]{1,0:T(8,128)(2,1)S(1)}, bf16[128,1536]{1,0:T(8,128)(2,1)}, u32[]{:S(2)}, u32[]{:S(2)}) %collective-permute-start.19) | collective-permute-done | bytes 393248 | tf_op jit(solution)/shard_map/ppermute | solution.py:72
  196.2 5.0 fusion.2
  204.1 5.1 fusion
  209.2 6.9 %collective-permute-done.24.rest_6_ = bf16[128,1920]{1,0:T(8,128)(2,1)S(1)} collective-permute-done((bf16[128,1920]{1,0:T(8,128)(2,1)S(1)}, bf16[128,1920]{1,0:T(8,128)(2,1)S(1)}, u32[]{:S(2)}, u32[]{:S(2)}) %collective-permute-start.24) | collective-permute-done | bytes 491552 | tf_op jit(solution)/shard_map/ppermute | solution.py:72
  230.4 12.9 %shard_map.256 = bf16[1536,2304]{1,0:T(8,128)(2,1)} custom-call(bf16[1024,1536]{1,0:T(8,128)(2,1)} %copy-done.9, bf16[1024,1536]{1,0:T(8,128)(2,1)} %pad_maximum_fusion.3.refs_1_, bf16[1024,1536]{1,0:T(8,128)(2,1)} %pad_maximum_fusion.1.refs_2_, bf16[1024,768]{1,0:T(8,128)(2,1)} %get-tuple-element.225.refs_3_), custom_call_target="tpu_custom_call" | custom-call | flops 7247757312 | bytes 10485760 | tf_op jit(solution)/shard_map/pallas_call | solution.py:386
  245.9 4.3 collective-permute-done.29
  256.7 3.6 fusion.28.grad
  260.3 5.9 %shard_map.257 = (bf16[256,768]{1,0:T(8,128)(2,1)}, bf16[4,272,384]{2,1,0:T(8,128)(2,1)}) custom-call(s32[3]{0:T(128)} %pad_add_fusion.sc, bf16[256,768]{1,0:T(8,128)(2,1)} %fusion.25.cq, bf16[4,144,384]{2,1,0:T(8,128)(2,1)} %pad_maximum_fusion.18.kv, f32[144,256]{1,0:T(8,128)} %broadcast_in_dim.123.bias, bf16[256,768]{1,0:T(8,128)(2,1)} %fusion.28.grad), custom_call_target="tpu_custom_call" | custom-call | flops 566231040 | bytes 3145728 | tf_op jit(solution)/shard_map/pallas_call | solution.py:346
  267.7 9.1 %collective-permute-done.32 = bf16[128,1536]{1,0:T(8,128)(2,1)} collective-permute-done((bf16[128,1536]{1,0:T(8,128)(2,1)}, bf16[128,1536]{1,0:T(8,128)(2,1)}, u32[]{:S(2)}, u32[]{:S(2)}) %collective-permute-start.32) | collective-permute-done | bytes 393248 | tf_op jit(solution)/shard_map/ppermute | solution.py:72
  285.1 4.3 fusion.6
  291.5 9.2 %collective-permute-done.38 = bf16[128,1536]{1,0:T(8,128)(2,1)S(1)} collective-permute-done((bf16[128,1536]{1,0:T(8,128)(2,1)S(1)}, bf16[128,1536]{1,0:T(8,128)(2,1)S(1)}, u32[]{:S(2)}, u32[]{:S(2)}) %collective-permute-start.38) | collective-permute-done | bytes 393248 | tf_op jit(solution)/shard_map/ppermute | solution.py:72
  301.8 9.4 %collective-permute-done.36 = bf16[128,1536]{1,0:T(8,128)(2,1)S(1)} collective-permute-done((bf16[128,1536]{1,0:T(8,128)(2,1)S(1)}, bf16[128,1536]{1,0:T(8,128)(2,1)S(1)}, u32[]{:S(2)}, u32[]{:S(2)}) %collective-permute-start.36) | collective-permute-done | bytes 393248 | tf_op jit(solution)/shard_map/ppermute | solution.py:72
  318.6 3.6 convolution_convert_fusion.grad
  324.9 16.2 %shard_map.258.grad = bf16[1024,640]{1,0:T(8,128)(2,1)} custom-call(bf16[1024,256]{1,0:T(8,128)(2,1)} %get-tuple-element.168.qs, bf16[1024,256]{1,0:T(8,128)(2,1)} %get-tuple-element.169.ks, bf16[1024,256]{1,0:T(8,128)(2,1)} %get-tuple-element.170.vs, bf16[1024,256]{1,0:T(8,128)(2,1)} %convolution_convert_fusion.grad, f32[8,1024]{1,0:T(8,128)} %get-tuple-element.239.lse, ...), custom_call_target="tpu_custom_call" | custom-call | flops 8053063680 | bytes 8388608 | tf_op jit(solution)/shard_map/pallas_call | solution.py:254
  341.9 7.2 %fusion.18 = f32[1024,1536]{1,0:T(8,128)} fusion(bf16[1024,640]{1,0:T(8,128)(2,1)} %shard_map.258.grad, bf16[1536,2688]{1,0:T(8,128)(2,1)} %all-gather.5.cloned.1.call-done), kind=kOutput, calls=%fused_computation.37 | convolution fusion | flops 2013265920 | bytes 9568256 | tf_op jit(solution)/shard_map/dot_general | solution.py:44
  349.1 3.2 slice.755
  363.3 12.9 %shard_map.259 = bf16[1536,1536]{1,0:T(8,128)(2,1)} custom-call(bf16[1024,1536]{1,0:T(8,128)(2,1)} %pad_maximum_fusion.one, bf16[1024,640]{1,0:T(8,128)(2,1)} %shard_map.258.grad, bf16[1024,1536]{1,0:T(8,128)(2,1)} %copy-done.2, bf16[1024,256]{1,0:T(8,128)(2,1)} %get-tuple-element.173.att, bf16[144,1536]{1,0:T(8,128)(2,1)} %copy-done.14, ...), custom_call_target="tpu_custom_call" | custom-call | flops 4831838208 | bytes 16777216 | tf_op jit(solution)/shard_map/pallas_call | solution.py:424
  384.4 4.7 all-to-all-start
  401.8 28.2 %collective-permute-done.50 = bf16[128,1536]{1,0:T(8,128)(2,1)} collective-permute-done((bf16[128,1536]{1,0:T(8,128)(2,1)}, bf16[128,1536]{1,0:T(8,128)(2,1)}, u32[]{:S(2)}, u32[]{:S(2)}) %collective-permute-start.50) | collective-permute-done | bytes 393248 | tf_op jit(solution)/shard_map/ppermute | solution.py:72
  431.0 10.5 %collective-permute-start.56 = (bf16[130,384]{1,0:T(8,128)(2,1)}, bf16[130,384]{1,0:T(8,128)(2,1)}, u32[]{:S(2)}, u32[]{:S(2)}) collective-permute-start(bf16[130,384]{1,0:T(8,128)(2,1)} %get-tuple-element.385), channel_id=1, source_target_pairs={{0,12},{4,0},{8,4},{12,8},{1,13},{5,1},{9,5},{13,9},{2,14},{6,2},{... | collective-permute-start | bytes 299528 | tf_op jit(solution)/shard_map/ppermute | solution.py:72
  444.5 3.4 stack.123
  451.7 5.2 collective-permute-start.54
  458.8 5.7 %shard_map.260 = (f32[2,192,3072]{2,1,0:T(8,128)}, f32[192,3072]{1,0:T(8,128)}) custom-call(s32[2]{0:T(128)} %pad_add_fusion.1.at, bf16[2,96,2304]{2,1,0:T(8,128)(2,1)} %copy-done.6, bf16[2,96,2304]{2,1,0:T(8,128)(2,1)} %collective-permute-done.62.b1, bf16[2,96,2304]{2,1,0:T(8,128)(2,1)} %collective-permute-done.63.b2, ...), custom_call_target="tpu_custom_call" | custom-call | flops 4194304 | bytes 11534336 | tf_op jit(solution)/shard_map/pallas_call | solution.py:455
  474.9 3.1 convert_reduce_fusion
  479.4 3.5 collective-permute-start.69
  483.2 4.7 collective-permute-done.65
  492.8 5.3 all-gather
  498.1 15.4 %collective-permute-done.72 = f32[4,128]{1,0:T(4,128)S(1)} collective-permute-done((f32[4,128]{1,0:T(4,128)S(1)}, f32[4,128]{1,0:T(4,128)S(1)}, u32[]{:S(2)}, u32[]{:S(2)}) %collective-permute-start.72) | collective-permute-done | bytes 2080 | tf_op jit(solution)/shard_map/ppermute | solution.py:72
  515.4 5.5 all-gather.1
  528.4 8.3 %copy.44 = f32[192,2,3072]{2,1,0:T(2,128)} copy(f32[192,2,3072]{2,0,1:T(8,128)} %bitcast.103) | data formatting | bytes 9437184
  539.1 4.9 shard_map.262
  544.0 3.2 copy.43
  (403 shorter events, 205.2 us)
Async XLA Ops:
  7.2 82.0 %all-gather.5.cloned.1.call-start = ((), (), s32[]{:S(2)}) async-start(), calls=%async_computation.2 | async-start | bytes 8773632 | tf_op jit(solution)/shard_map/all_gather | solution.py:127
  14.5 153.2 %all-gather.7.cloned.1.call-start = ((), (), s32[]{:S(2)}) async-start(), calls=%async_computation.3 | async-start | bytes 7520256 | tf_op jit(solution)/shard_map/all_gather | solution.py:127
  15.3 36.5 %collective-permute-start.4 = (bf16[128,1536]{1,0:T(8,128)(2,1)}, bf16[128,1536]{1,0:T(8,128)(2,1)}, u32[]{:S(2)}, u32[]{:S(2)}) collective-permute-start(bf16[128,1536]{1,0:T(8,128)(2,1)} %dynamic-slice_bitcast_fusion.1), channel_id=1, source_target_pairs={{0,0},{1,2},{2,1},{3,3},{4,4},{5,6},{6,5},{7,7},{8,8},{9,10},{10,9... | collective-permute-start | bytes 1179656 | tf_op jit(solution)/shard_map/ppermute | solution.py:560
  43.4 297.7 %reduce-scatter.2.cloned.1.call-start = ((), (), s32[]{:S(2)}) async-start(), calls=%async_computation.4 | async-start | bytes 7520256 | tf_op jit(solution)/shard_map/reduce_scatter | solution.py:131
  51.9 26.8 %collective-permute-start.5 = (bf16[512,1536]{1,0:T(8,128)(2,1)S(1)}, bf16[512,1536]{1,0:T(8,128)(2,1)}, u32[]{:S(2)}, u32[]{:S(2)}) collective-permute-start(bf16[512,1536]{1,0:T(8,128)(2,1)S(1)} %pad_maximum_fusion.6), channel_id=1, source_target_pairs={{0,1},{1,0},{2,3},{3,2},{4,5},{5,4},{6,7},{7,6},{8,9},{9,8},{10,11... | collective-permute-start | bytes 4718600 | tf_op jit(solution)/shard_map/ppermute | solution.py:52
  58.3 20.2 %collective-permute-start.6 = (bf16[128,1536]{1,0:T(8,128)(2,1)S(1)}, bf16[128,1536]{1,0:T(8,128)(2,1)S(1)}, u32[]{:S(2)}, u32[]{:S(2)}) collective-permute-start(bf16[128,1536]{1,0:T(8,128)(2,1)S(1)} %concatenate.100), channel_id=1, source_target_pairs={{0,4},{4,8},{8,12},{12,0},{1,5},{5,9},{9,13},{13,1},{2,6},{6,10},{... | collective-permute-start | bytes 1179656 | tf_op jit(solution)/shard_map/ppermute | solution.py:72
  97.5 17.2 %collective-permute-start.12 = (bf16[144,384]{1,0:T(8,128)(2,1)S(1)}, bf16[144,384]{1,0:T(8,128)(2,1)S(1)}, u32[]{:S(2)}, u32[]{:S(2)}) collective-permute-start(bf16[144,384]{1,0:T(8,128)(2,1)S(1)} %convolution_convert_fusion.1), channel_id=1, source_target_pairs={{0,12},{4,0},{8,4},{12,8},{1,13},{5,1},{9,5},{13,9},{2,14},{6,2},{... | collective-permute-start | bytes 331784 | tf_op jit(solution)/shard_map/ppermute | solution.py:72
  99.9 14.8 %collective-permute-start.11 = (bf16[144,384]{1,0:T(8,128)(2,1)S(1)}, bf16[144,384]{1,0:T(8,128)(2,1)S(1)}, u32[]{:S(2)}, u32[]{:S(2)}) collective-permute-start(bf16[144,384]{1,0:T(8,128)(2,1)S(1)} %convolution_convert_fusion.1), channel_id=1, source_target_pairs={{0,8},{4,12},{8,0},{12,4},{1,9},{5,13},{9,1},{13,5},{2,10},{6,14},... | collective-permute-start | bytes 331784 | tf_op jit(solution)/shard_map/ppermute | solution.py:72
  100.5 14.2 %collective-permute-start.10 = (bf16[144,384]{1,0:T(8,128)(2,1)S(1)}, bf16[144,384]{1,0:T(8,128)(2,1)S(1)}, u32[]{:S(2)}, u32[]{:S(2)}) collective-permute-start(bf16[144,384]{1,0:T(8,128)(2,1)S(1)} %convolution_convert_fusion.1), channel_id=1, source_target_pairs={{0,4},{4,8},{8,12},{12,0},{1,5},{5,9},{9,13},{13,1},{2,6},{6,10},{... | collective-permute-start | bytes 331784 | tf_op jit(solution)/shard_map/ppermute | solution.py:72
  125.7 20.0 %collective-permute-start.16 = (bf16[128,1536]{1,0:T(8,128)(2,1)S(1)}, bf16[128,1536]{1,0:T(8,128)(2,1)}, u32[]{:S(2)}, u32[]{:S(2)}) collective-permute-start(bf16[128,1536]{1,0:T(8,128)(2,1)S(1)} %get-tuple-element.177), channel_id=1, source_target_pairs={{0,4},{4,8},{8,12},{12,0},{1,5},{5,9},{9,13},{13,1},{2,6},{6,10},{... | collective-permute-start | bytes 1179656 | tf_op jit(solution)/shard_map/ppermute | solution.py:72
  166.8 20.1 %collective-permute-start.19 = (bf16[128,1536]{1,0:T(8,128)(2,1)S(1)}, bf16[128,1536]{1,0:T(8,128)(2,1)}, u32[]{:S(2)}, u32[]{:S(2)}) collective-permute-start(bf16[128,1536]{1,0:T(8,128)(2,1)S(1)} %fusion.57), channel_id=1, source_target_pairs={{0,4},{4,8},{8,12},{12,0},{1,5},{5,9},{9,13},{13,1},{2,6},{6,10},{... | collective-permute-start | bytes 1179656 | tf_op jit(solution)/shard_map/ppermute | solution.py:72
  192.3 16.9 %collective-permute-start.25 = (bf16[128,1920]{1,0:T(8,128)(2,1)S(1)}, bf16[128,1920]{1,0:T(8,128)(2,1)S(1)}, u32[]{:S(2)}, u32[]{:S(2)}) collective-permute-start(bf16[128,1920]{1,0:T(8,128)(2,1)S(1)} %get-tuple-element.426), channel_id=1, source_target_pairs={{0,12},{4,0},{8,4},{12,8},{1,13},{5,1},{9,5},{13,9},{2,14},{6,2},{... | collective-permute-start | bytes 1474568 | tf_op jit(solution)/shard_map/ppermute | solution.py:72
  192.9 16.3 %collective-permute-start.23 = (bf16[128,1920]{1,0:T(8,128)(2,1)S(1)}, bf16[128,1920]{1,0:T(8,128)(2,1)S(1)}, u32[]{:S(2)}, u32[]{:S(2)}) collective-permute-start(bf16[128,1920]{1,0:T(8,128)(2,1)S(1)} %get-tuple-element.427), channel_id=1, source_target_pairs={{0,4},{4,8},{8,12},{12,0},{1,5},{5,9},{9,13},{13,1},{2,6},{6,10},{... | collective-permute-start | bytes 1474568 | tf_op jit(solution)/shard_map/ppermute | solution.py:72
  193.8 22.2 %collective-permute-start.24 = (bf16[128,1920]{1,0:T(8,128)(2,1)S(1)}, bf16[128,1920]{1,0:T(8,128)(2,1)S(1)}, u32[]{:S(2)}, u32[]{:S(2)}) collective-permute-start(bf16[128,1920]{1,0:T(8,128)(2,1)S(1)} %get-tuple-element.428), channel_id=1, source_target_pairs={{0,8},{4,12},{8,0},{12,4},{1,9},{5,13},{9,1},{13,5},{2,10},{6,14},... | collective-permute-start | bytes 1474568 | tf_op jit(solution)/shard_map/ppermute | solution.py:72
  228.0 15.3 %collective-permute-start.30 = (bf16[512,1536]{1,0:T(8,128)(2,1)}, bf16[512,1536]{1,0:T(8,128)(2,1)}, u32[]{:S(2)}, u32[]{:S(2)}) collective-permute-start(bf16[512,1536]{1,0:T(8,128)(2,1)} %pad_maximum_fusion.9), channel_id=1, source_target_pairs={{0,1},{1,0},{2,3},{3,2},{4,5},{5,4},{6,7},{7,6},{8,9},{9,8},{10,11... | collective-permute-start | bytes 4718600 | tf_op jit(solution)/shard_map/ppermute | solution.py:52
  228.3 17.6 %collective-permute-start.27 = (bf16[128,1536]{1,0:T(8,128)(2,1)}, bf16[128,1536]{1,0:T(8,128)(2,1)}, u32[]{:S(2)}, u32[]{:S(2)}) collective-permute-start(bf16[128,1536]{1,0:T(8,128)(2,1)} %get-tuple-element.206), channel_id=1, source_target_pairs={{0,12},{4,0},{8,4},{12,8},{1,13},{5,1},{9,5},{13,9},{2,14},{6,2},{... | collective-permute-start | bytes 1179656 | tf_op jit(solution)/shard_map/ppermute | solution.py:72
  229.0 17.0 %collective-permute-start.28 = (bf16[128,1536]{1,0:T(8,128)(2,1)}, bf16[128,1536]{1,0:T(8,128)(2,1)}, u32[]{:S(2)}, u32[]{:S(2)}) collective-permute-start(bf16[128,1536]{1,0:T(8,128)(2,1)} %get-tuple-element.207), channel_id=1, source_target_pairs={{0,8},{4,12},{8,0},{12,4},{1,9},{5,13},{9,1},{13,5},{2,10},{6,14},... | collective-permute-start | bytes 1179656 | tf_op jit(solution)/shard_map/ppermute | solution.py:72
  229.5 20.7 %collective-permute-start.29 = (bf16[128,1536]{1,0:T(8,128)(2,1)}, bf16[128,1536]{1,0:T(8,128)(2,1)}, u32[]{:S(2)}, u32[]{:S(2)}) collective-permute-start(bf16[128,1536]{1,0:T(8,128)(2,1)} %get-tuple-element.208), channel_id=1, source_target_pairs={{0,4},{4,8},{8,12},{12,0},{1,5},{5,9},{9,13},{13,1},{2,6},{6,10},{... | collective-permute-start | bytes 1179656 | tf_op jit(solution)/shard_map/ppermute | solution.py:72
  256.1 20.7 %collective-permute-start.32 = (bf16[128,1536]{1,0:T(8,128)(2,1)}, bf16[128,1536]{1,0:T(8,128)(2,1)}, u32[]{:S(2)}, u32[]{:S(2)}) collective-permute-start(bf16[128,1536]{1,0:T(8,128)(2,1)} %get-tuple-element.344), channel_id=1, source_target_pairs={{0,4},{4,8},{8,12},{12,0},{1,5},{5,9},{9,13},{13,1},{2,6},{6,10},{... | collective-permute-start | bytes 1179656 | tf_op jit(solution)/shard_map/ppermute | solution.py:72
  284.7 26.6 %collective-permute-start.39 = (bf16[512,1536]{1,0:T(8,128)(2,1)S(1)}, bf16[512,1536]{1,0:T(8,128)(2,1)S(1)}, u32[]{:S(2)}, u32[]{:S(2)}) collective-permute-start(bf16[512,1536]{1,0:T(8,128)(2,1)S(1)} %pad_maximum_fusion.10), channel_id=1, source_target_pairs={{0,1},{1,0},{2,3},{3,2},{4,5},{5,4},{6,7},{7,6},{8,9},{9,8},{10,11... | collective-permute-start | bytes 4718600 | tf_op jit(solution)/shard_map/ppermute | solution.py:52
  289.6 23.7 %collective-permute-start.40 = (bf16[512,1536]{1,0:T(8,128)(2,1)S(1)}, bf16[512,1536]{1,0:T(8,128)(2,1)S(1)}, u32[]{:S(2)}, u32[]{:S(2)}) collective-permute-start(bf16[512,1536]{1,0:T(8,128)(2,1)S(1)} %slice.756), channel_id=1, source_target_pairs={{0,1},{1,0},{2,3},{3,2},{4,5},{5,4},{6,7},{7,6},{8,9},{9,8},{10,11... | collective-permute-start | bytes 4718600 | tf_op jit(solution)/shard_map/ppermute | solution.py:52
  290.8 20.5 %collective-permute-start.36 = (bf16[128,1536]{1,0:T(8,128)(2,1)S(1)}, bf16[128,1536]{1,0:T(8,128)(2,1)S(1)}, u32[]{:S(2)}, u32[]{:S(2)}) collective-permute-start(bf16[128,1536]{1,0:T(8,128)(2,1)S(1)} %get-tuple-element.223), channel_id=1, source_target_pairs={{0,4},{4,8},{8,12},{12,0},{1,5},{5,9},{9,13},{13,1},{2,6},{6,10},{... | collective-permute-start | bytes 1179656 | tf_op jit(solution)/shard_map/ppermute | solution.py:72
  323.0 18.0 %collective-permute-start.44 = (bf16[272,384]{1,0:T(8,128)(2,1)}, bf16[272,384]{1,0:T(8,128)(2,1)S(1)}, u32[]{:S(2)}, u32[]{:S(2)}) collective-permute-start(bf16[272,384]{1,0:T(8,128)(2,1)} %get-tuple-element.373), channel_id=1, source_target_pairs={{0,12},{4,0},{8,4},{12,8},{1,13},{5,1},{9,5},{13,9},{2,14},{6,2},{... | collective-permute-start | bytes 626696 | tf_op jit(solution)/shard_map/ppermute | solution.py:72
  323.7 17.4 %collective-permute-start.43 = (bf16[272,384]{1,0:T(8,128)(2,1)S(1)}, bf16[272,384]{1,0:T(8,128)(2,1)S(1)}, u32[]{:S(2)}, u32[]{:S(2)}) collective-permute-start(bf16[272,384]{1,0:T(8,128)(2,1)S(1)} %get-tuple-element.374), channel_id=1, source_target_pairs={{0,8},{4,12},{8,0},{12,4},{1,9},{5,13},{9,1},{13,5},{2,10},{6,14},... | collective-permute-start | bytes 626696 | tf_op jit(solution)/shard_map/ppermute | solution.py:72
  323.9 17.2 %collective-permute-start.42 = (bf16[272,384]{1,0:T(8,128)(2,1)S(1)}, bf16[272,384]{1,0:T(8,128)(2,1)S(1)}, u32[]{:S(2)}, u32[]{:S(2)}) collective-permute-start(bf16[272,384]{1,0:T(8,128)(2,1)S(1)} %get-tuple-element.375), channel_id=1, source_target_pairs={{0,4},{4,8},{8,12},{12,0},{1,5},{5,9},{9,13},{13,1},{2,6},{6,10},{... | collective-permute-start | bytes 626696 | tf_op jit(solution)/shard_map/ppermute | solution.py:72
  352.3 23.9 %collective-permute-start.45 = (bf16[512,1536]{1,0:T(8,128)(2,1)}, bf16[512,1536]{1,0:T(8,128)(2,1)}, u32[]{:S(2)}, u32[]{:S(2)}) collective-permute-start(bf16[512,1536]{1,0:T(8,128)(2,1)} %slice.755), channel_id=1, source_target_pairs={{0,1},{1,0},{2,3},{3,2},{4,5},{5,4},{6,7},{7,6},{8,9},{9,8},{10,11... | collective-permute-start | bytes 4718600 | tf_op jit(solution)/shard_map/ppermute | solution.py:52
  354.8 25.3 %collective-permute-start.46 = (bf16[128,1536]{1,0:T(8,128)(2,1)}, bf16[128,1536]{1,0:T(8,128)(2,1)S(1)}, u32[]{:S(2)}, u32[]{:S(2)}) collective-permute-start(bf16[128,1536]{1,0:T(8,128)(2,1)} %get-tuple-element.254), channel_id=1, source_target_pairs={{0,12},{4,0},{8,4},{12,8},{1,13},{5,1},{9,5},{13,9},{2,14},{6,2},{... | collective-permute-start | bytes 1179656 | tf_op jit(solution)/shard_map/ppermute | solution.py:72
  357.0 23.1 %collective-permute-start.47 = (bf16[128,1536]{1,0:T(8,128)(2,1)}, bf16[128,1536]{1,0:T(8,128)(2,1)S(1)}, u32[]{:S(2)}, u32[]{:S(2)}) collective-permute-start(bf16[128,1536]{1,0:T(8,128)(2,1)} %get-tuple-element.255), channel_id=1, source_target_pairs={{0,8},{4,12},{8,0},{12,4},{1,9},{5,13},{9,1},{13,5},{2,10},{6,14},... | collective-permute-start | bytes 1179656 | tf_op jit(solution)/shard_map/ppermute | solution.py:72
  358.5 21.6 %collective-permute-start.48 = (bf16[128,1536]{1,0:T(8,128)(2,1)}, bf16[128,1536]{1,0:T(8,128)(2,1)S(1)}, u32[]{:S(2)}, u32[]{:S(2)}) collective-permute-start(bf16[128,1536]{1,0:T(8,128)(2,1)} %get-tuple-element.256), channel_id=1, source_target_pairs={{0,4},{4,8},{8,12},{12,0},{1,5},{5,9},{9,13},{13,1},{2,6},{6,10},{... | collective-permute-start | bytes 1179656 | tf_op jit(solution)/shard_map/ppermute | solution.py:72
  359.3 20.8 %collective-permute-start.49 = (bf16[96,2304]{1,0:T(8,128)(2,1)}, bf16[96,2304]{1,0:T(8,128)(2,1)}, u32[]{:S(2)}, u32[]{:S(2)}) collective-permute-start(bf16[96,2304]{1,0:T(8,128)(2,1)} %reduce-scatter.2.cloned.1.call-done), channel_id=1, source_target_pairs={{0,2},{2,0},{1,3},{3,1},{4,6},{6,4},{5,7},{7,5},{8,10},{10,8},{9,1... | collective-permute-start | bytes 1327112 | tf_op jit(solution)/shard_map/ppermute | solution.py:96
  382.2 68.2 %collective-permute-start.64 = (bf16[2,96,2304]{2,1,0:T(8,128)(2,1)S(1)}, bf16[2,96,2304]{2,1,0:T(8,128)(2,1)}, u32[]{:S(2)}, u32[]{:S(2)}) collective-permute-start(bf16[2,96,2304]{2,1,0:T(8,128)(2,1)S(1)} %pad_maximum_fusion.12.b0), channel_id=1, source_target_pairs={{0,12},{4,0},{8,4},{12,8},{1,13},{5,1},{9,5},{13,9},{2,14},{6,2},{... | collective-permute-start | bytes 2654216 | tf_op jit(solution)/shard_map/ppermute | solution.py:72
  384.0 67.6 %collective-permute-start.63 = (bf16[2,96,2304]{2,1,0:T(8,128)(2,1)S(1)}, bf16[2,96,2304]{2,1,0:T(8,128)(2,1)}, u32[]{:S(2)}, u32[]{:S(2)}) collective-permute-start(bf16[2,96,2304]{2,1,0:T(8,128)(2,1)S(1)} %pad_maximum_fusion.12.b0), channel_id=1, source_target_pairs={{0,8},{4,12},{8,0},{12,4},{1,9},{5,13},{9,1},{13,5},{2,10},{6,14},... | collective-permute-start | bytes 2654216 | tf_op jit(solution)/shard_map/ppermute | solution.py:72
  384.4 89.7 %all-to-all-start = ((bf16[16,96,1536]{2,1,0:T(8,128)(2,1)}), bf16[16,96,1536]{2,1,0:T(8,128)(2,1)}, u32[]{:S(2)}, u32[]{:S(2)}) async-start(bf16[16,96,1536]{2,1,0:T(8,128)(2,1)} %bitcast.100), calls=%async_computation.1 | async-start | bytes 9437184 | tf_op jit(solution)/shard_map/all_to_all | solution.py:56
  389.1 40.9 %collective-permute-start.50 = (bf16[128,1536]{1,0:T(8,128)(2,1)}, bf16[128,1536]{1,0:T(8,128)(2,1)}, u32[]{:S(2)}, u32[]{:S(2)}) collective-permute-start(bf16[128,1536]{1,0:T(8,128)(2,1)} %get-tuple-element.260), channel_id=1, source_target_pairs={{0,12},{4,0},{8,4},{12,8},{1,13},{5,1},{9,5},{13,9},{2,14},{6,2},{... | collective-permute-start | bytes 1179656 | tf_op jit(solution)/shard_map/ppermute | solution.py:72
  390.9 39.3 %collective-permute-start.51 = (bf16[128,1536]{1,0:T(8,128)(2,1)}, bf16[128,1536]{1,0:T(8,128)(2,1)}, u32[]{:S(2)}, u32[]{:S(2)}) collective-permute-start(bf16[128,1536]{1,0:T(8,128)(2,1)} %get-tuple-element.261), channel_id=1, source_target_pairs={{0,8},{4,12},{8,0},{12,4},{1,9},{5,13},{9,1},{13,5},{2,10},{6,14},... | collective-permute-start | bytes 1179656 | tf_op jit(solution)/shard_map/ppermute | solution.py:72
  399.2 30.9 %collective-permute-start.52 = (bf16[128,1536]{1,0:T(8,128)(2,1)}, bf16[128,1536]{1,0:T(8,128)(2,1)S(1)}, u32[]{:S(2)}, u32[]{:S(2)}) collective-permute-start(bf16[128,1536]{1,0:T(8,128)(2,1)} %get-tuple-element.262), channel_id=1, source_target_pairs={{0,4},{4,8},{8,12},{12,0},{1,5},{5,9},{9,13},{13,1},{2,6},{6,10},{... | collective-permute-start | bytes 1179656 | tf_op jit(solution)/shard_map/ppermute | solution.py:72
  430.0 26.8 %collective-permute-start.62 = (bf16[2,96,2304]{2,1,0:T(8,128)(2,1)S(1)}, bf16[2,96,2304]{2,1,0:T(8,128)(2,1)}, u32[]{:S(2)}, u32[]{:S(2)}) collective-permute-start(bf16[2,96,2304]{2,1,0:T(8,128)(2,1)S(1)} %pad_maximum_fusion.12.b0), channel_id=1, source_target_pairs={{0,4},{4,8},{8,12},{12,0},{1,5},{5,9},{9,13},{13,1},{2,6},{6,10},{... | collective-permute-start | bytes 2654216 | tf_op jit(solution)/shard_map/ppermute | solution.py:72
  431.0 33.5 %collective-permute-start.56 = (bf16[130,384]{1,0:T(8,128)(2,1)}, bf16[130,384]{1,0:T(8,128)(2,1)}, u32[]{:S(2)}, u32[]{:S(2)}) collective-permute-start(bf16[130,384]{1,0:T(8,128)(2,1)} %get-tuple-element.385), channel_id=1, source_target_pairs={{0,12},{4,0},{8,4},{12,8},{1,13},{5,1},{9,5},{13,9},{2,14},{6,2},{... | collective-permute-start | bytes 299528 | tf_op jit(solution)/shard_map/ppermute | solution.py:72
  441.5 23.0 %collective-permute-start.58 = (bf16[130,384]{1,0:T(8,128)(2,1)}, bf16[130,384]{1,0:T(8,128)(2,1)}, u32[]{:S(2)}, u32[]{:S(2)}) collective-permute-start(bf16[130,384]{1,0:T(8,128)(2,1)} %get-tuple-element.386), channel_id=1, source_target_pairs={{0,4},{4,8},{8,12},{12,0},{1,5},{5,9},{9,13},{13,1},{2,6},{6,10},{... | collective-permute-start | bytes 299528 | tf_op jit(solution)/shard_map/ppermute | solution.py:72
  450.4 14.1 %collective-permute-start.57 = (bf16[130,384]{1,0:T(8,128)(2,1)S(1)}, bf16[130,384]{1,0:T(8,128)(2,1)S(1)}, u32[]{:S(2)}, u32[]{:S(2)}) collective-permute-start(bf16[130,384]{1,0:T(8,128)(2,1)S(1)} %get-tuple-element.387), channel_id=1, source_target_pairs={{0,8},{4,12},{8,0},{12,4},{1,9},{5,13},{9,1},{13,5},{2,10},{6,14},... | collective-permute-start | bytes 299528 | tf_op jit(solution)/shard_map/ppermute | solution.py:72
  451.7 22.4 %collective-permute-start.54 = (bf16[128,1536]{1,0:T(8,128)(2,1)S(1)}, bf16[128,1536]{1,0:T(8,128)(2,1)S(1)}, u32[]{:S(2)}, u32[]{:S(2)}) collective-permute-start(bf16[128,1536]{1,0:T(8,128)(2,1)S(1)} %concatenate.122), channel_id=1, source_target_pairs={{0,0},{1,2},{2,1},{3,3},{4,4},{5,6},{6,5},{7,7},{8,8},{9,10},{10,9... | collective-permute-start | bytes 1179656 | tf_op jit(solution)/shard_map/ppermute | solution.py:689
  456.9 17.2 %collective-permute-start.55 = (bf16[128,1536]{1,0:T(8,128)(2,1)S(1)}, bf16[128,1536]{1,0:T(8,128)(2,1)S(1)}, u32[]{:S(2)}, u32[]{:S(2)}) collective-permute-start(bf16[128,1536]{1,0:T(8,128)(2,1)S(1)} %copy-done.39), channel_id=1, source_target_pairs={{0,0},{1,2},{2,1},{3,3},{4,4},{5,6},{6,5},{7,7},{8,8},{9,10},{10,9... | collective-permute-start | bytes 1179656 | tf_op jit(solution)/shard_map/ppermute | solution.py:690
  483.0 31.7 %collective-permute-start.73 = (bf16[4,130,384]{2,1,0:T(8,128)(2,1)S(1)}, bf16[4,130,384]{2,1,0:T(8,128)(2,1)S(1)}, u32[]{:S(2)}, u32[]{:S(2)}) collective-permute-start(bf16[4,130,384]{2,1,0:T(8,128)(2,1)S(1)} %pad_maximum_fusion.20.near), channel_id=1, source_target_pairs={{0,2},{2,0},{1,3},{3,1},{4,6},{6,4},{5,7},{7,5},{8,10},{10,8},{9,1... | collective-permute-start | bytes 1198088 | tf_op jit(solution)/shard_map/ppermute | solution.py:96
  487.9 36.8 %collective-permute-start.68 = (bf16[2,96,1536]{2,1,0:T(8,128)(2,1)S(1)}, bf16[2,96,1536]{2,1,0:T(8,128)(2,1)S(1)}, u32[]{:S(2)}, u32[]{:S(2)}) collective-permute-start(bf16[2,96,1536]{2,1,0:T(8,128)(2,1)S(1)} %pad_maximum_fusion.13.b0), channel_id=1, source_target_pairs={{0,12},{4,0},{8,4},{12,8},{1,13},{5,1},{9,5},{13,9},{2,14},{6,2},{... | collective-permute-start | bytes 1769480 | tf_op jit(solution)/shard_map/ppermute | solution.py:72
  488.0 36.7 %collective-permute-start.67 = (bf16[2,96,1536]{2,1,0:T(8,128)(2,1)S(1)}, bf16[2,96,1536]{2,1,0:T(8,128)(2,1)}, u32[]{:S(2)}, u32[]{:S(2)}) collective-permute-start(bf16[2,96,1536]{2,1,0:T(8,128)(2,1)S(1)} %pad_maximum_fusion.13.b0), channel_id=1, source_target_pairs={{0,8},{4,12},{8,0},{12,4},{1,9},{5,13},{9,1},{13,5},{2,10},{6,14},... | collective-permute-start | bytes 1769480 | tf_op jit(solution)/shard_map/ppermute | solution.py:72
  490.0 34.7 %collective-permute-start.66 = (bf16[2,96,1536]{2,1,0:T(8,128)(2,1)S(1)}, bf16[2,96,1536]{2,1,0:T(8,128)(2,1)}, u32[]{:S(2)}, u32[]{:S(2)}) collective-permute-start(bf16[2,96,1536]{2,1,0:T(8,128)(2,1)S(1)} %pad_maximum_fusion.13.b0), channel_id=1, source_target_pairs={{0,4},{4,8},{8,12},{12,0},{1,5},{5,9},{9,13},{13,1},{2,6},{6,10},{... | collective-permute-start | bytes 1769480 | tf_op jit(solution)/shard_map/ppermute | solution.py:72
  490.1 23.4 %collective-permute-start.72 = (f32[4,128]{1,0:T(4,128)S(1)}, f32[4,128]{1,0:T(4,128)S(1)}, u32[]{:S(2)}, u32[]{:S(2)}) collective-permute-start(f32[4,128]{1,0:T(4,128)S(1)} %fusion.94), channel_id=1, source_target_pairs={{0,12},{4,0},{8,4},{12,8},{1,13},{5,1},{9,5},{13,9},{2,14},{6,2},{... | collective-permute-start | bytes 6152 | tf_op jit(solution)/shard_map/ppermute | solution.py:72
  524.8 22.4 %collective-permute-start.74 = (f32[4,128]{1,0:T(4,128)S(1)}, f32[4,128]{1,0:T(4,128)S(1)}, u32[]{:S(2)}, u32[]{:S(2)}) collective-permute-start(f32[4,128]{1,0:T(4,128)S(1)} %bitcast.118), channel_id=1, source_target_pairs={{0,2},{2,0},{1,3},{3,1},{4,6},{6,4},{5,7},{7,5},{8,10},{10,8},{9,1... | collective-permute-start | bytes 6152 | tf_op jit(solution)/shard_map/ppermute | solution.py:709
  (89 other events, 961.4 us)
Sparse Core Ops, SparseCore 0:
  14.6 74.4 all-gather.4
  91.9 64.6 all-gather.6
  250.4 79.3 reduce-scatter.1

commit v4 on v3

--- a/solution.py
+++ b/solution.py
@@ -100,11 +100,14 @@
     return jnp.concatenate([mine, to_partner(mine)], axis=0)
 
 
+def halves_sum(near, far):
+    mine = (near.astype(f32) + to_partner(far).astype(f32)).astype(bf16)
+    return [mine[k * ROWS : (k + 1) * ROWS] for k in range(4)]
+
+
 def scatter_half(partial):
     half = 4 * ROWS
-    got = to_partner(partial[half:].astype(bf16))
-    mine = (partial[:half].astype(f32) + got.astype(f32)).astype(bf16)
-    return [mine[k * ROWS : (k + 1) * ROWS] for k in range(4)]
+    return halves_sum(partial[:half], partial[half:].astype(bf16))
 
 
 def plane_parts(grad):
@@ -435,28 +438,29 @@
     return (x + 4 - q) % 4
 
 
-def finish_feed_kernel(at, b0, b1, b2, b3, gain, grad_in, grad_down, held):
-    rows, width = b0.shape[1], grad_down.shape[1] // 4
-    for k, block in enumerate((b0, b1, b2, b3)):
-        held[k] = block[...]
+def finish_feed_kernel(at, *refs):
+    blocks, (gain, grad_in, grad_down, held) = refs[:8], refs[8:]
+    rows, width = blocks[0].shape[0], grad_down.shape[1] // 4
+    for k, block in enumerate(blocks):
+        held[k % 4, k // 4] = block[...]
     for h in range(2):
         scale = gain[h * rows : (h + 1) * rows, :]
         for q in range(4):
             part = held[held_at(q, at[0]), (at[1] + h) % 2]
             to = pl.ds(q * width, width)
             for kind in range(2):
-                grad_in[kind, h * rows : (h + 1) * rows, to] = part[:, kind * width : (kind + 1) * width].astype(f32) * scale
+                grad_in[h * rows : (h + 1) * rows, kind, to] = part[:, kind * width : (kind + 1) * width].astype(f32) * scale
             grad_down[h * rows : (h + 1) * rows, to] = part[:, 2 * width :].astype(f32)
 
 
 def finish_feed(at, blocks, gain):
-    _, rows, columns = blocks[0].shape
+    rows, columns = blocks[0].shape
     width = columns // 3
     return pl.pallas_call(
         finish_feed_kernel,
-        in_specs=[pl.BlockSpec(memory_space=pltpu.SMEM)] + [pl.BlockSpec(memory_space=pltpu.VMEM)] * 5,
+        in_specs=[pl.BlockSpec(memory_space=pltpu.SMEM)] + [pl.BlockSpec(memory_space=pltpu.VMEM)] * 9,
         out_shape=(
-            jax.ShapeDtypeStruct((2, 2 * rows, 4 * width), f32),
+            jax.ShapeDtypeStruct((2 * rows, 2, 4 * width), f32),
             jax.ShapeDtypeStruct((2 * rows, 4 * width), f32),
         ),
         scratch_shapes=[pltpu.VMEM((4, 2, rows, columns), bf16)],
@@ -468,8 +472,9 @@
     width = near.shape[2]
     for q in range(4):
         place = held_at(q, at[0])
-        out[at[1], :, q * width : (q + 1) * width] = near[place].astype(f32)
-        out[1 - at[1], :, q * width : (q + 1) * width] = far[place].astype(f32)
+        near_block, far_block = near[place].astype(f32), far[place].astype(f32)
+        for h in range(2):
+            out[:, h, q * width : (q + 1) * width] = jnp.where(at[1] == h, near_block, far_block)
 
 
 def finish_cond(at, near, far):
@@ -477,15 +482,16 @@
     return pl.pallas_call(
         finish_cond_kernel,
         in_specs=[pl.BlockSpec(memory_space=pltpu.SMEM)] + [pl.BlockSpec(memory_space=pltpu.VMEM)] * 2,
-        out_shape=jax.ShapeDtypeStruct((2, count, 4 * width), f32),
+        out_shape=jax.ShapeDtypeStruct((count, 2, 4 * width), f32),
         cost_estimate=pl.CostEstimate(flops=1 << 20, transcendentals=0, bytes_accessed=3 << 20),
     )(at, near, far)
 
 
-def finish_columns_kernel(at, b0, b1, b2, b3, gain, other_gain, proj, out, keyval, query, cross, held):
-    rows = b0.shape[1]
-    for k, block in enumerate((b0, b1, b2, b3)):
-        held[k] = block[...]
+def finish_columns_kernel(at, *refs):
+    blocks, (gain, other_gain, proj, out, keyval, query, cross, held) = refs[:8], refs[8:]
+    rows = blocks[0].shape[0]
+    for k, block in enumerate(blocks):
+        held[k % 4, k // 4] = block[...]
     for h in range(2):
         to = pl.ds(h * rows, rows)
         parts = [held[held_at(q, at[0]), (at[1] + h) % 2] for q in range(4)]
@@ -497,23 +503,23 @@
         for place, kind in enumerate((0, 2, 1)):
             proj[place, to, :] = kind_of(kind) * gain[to, :]
         out[to, :] = kind_of(3)
-        keyval[0, to, :] = kind_of(4)
-        keyval[1, to, :] = kind_of(5)
+        keyval[to, 0, :] = kind_of(4)
+        keyval[to, 1, :] = kind_of(5)
         query[to, :] = kind_of(6) * other_gain[to, :]
         cross[to, :] = kind_of(7)
 
 
 def finish_columns(at, blocks, gain, other_gain):
-    _, rows, columns = blocks[0].shape
+    rows, columns = blocks[0].shape
     width = columns // 2
     plain = jax.ShapeDtypeStruct((2 * rows, width), f32)
     return pl.pallas_call(
         finish_columns_kernel,
-        in_specs=[pl.BlockSpec(memory_space=pltpu.SMEM)] + [pl.BlockSpec(memory_space=pltpu.VMEM)] * 6,
+        in_specs=[pl.BlockSpec(memory_space=pltpu.SMEM)] + [pl.BlockSpec(memory_space=pltpu.VMEM)] * 10,
         out_shape=(
             jax.ShapeDtypeStruct((3, 2 * rows, width), f32),
             plain,
-            jax.ShapeDtypeStruct((2, 2 * rows, width), f32),
+            jax.ShapeDtypeStruct((2 * rows, 2, width), f32),
             plain,
             plain,
         ),
@@ -638,30 +644,36 @@
     grad_resid_one = grad_resid_two + unit_norm_back(norm_two, scale_two, grad_two)
 
     sent_back, mine_two, quarters, hidden = both(grad_resid_one.astype(bf16), mine_two, quarters, hidden)
-    mine_back, grad_two_all, feed_half = both(
-        gather_half(sent_back), with_partner(mine_two), scatter_half(dot_nt(hidden, w_down))
-    )
-    full_back, quarters, feed_half = both(with_partner(mine_back), quarters, feed_half)
-    grad_att, quarters, feed_half = both(dot(full_back, w_out).astype(bf16), quarters, feed_half)
+    mine_back, grad_two_all, hidden = both(gather_half(sent_back), with_partner(mine_two), hidden)
+    full_back, quarters, feed_part = both(with_partner(mine_back), quarters, dot_nt(hidden, w_down).astype(bf16))
+    grad_att, quarters, feed_part = both(dot(full_back, w_out).astype(bf16), quarters, feed_part)
+    feed_half = scatter_half(feed_part)
     quarter_parts = swapped_x([quarters[k] for k in range(4)])
     feed_parts = scatter_x(feed_half)
     grad_qvk = attn_backward(qs, ks, vs, grad_att, lse, cosine, sine)
     grad_qvk, quarter_parts, sum_feed = both(grad_qvk, quarter_parts, sum_feed)
     ckv_share = summed([part[ROWS:] for part in quarter_parts]).astype(bf16)
-    partial, grad_qvk, ckv_share, sum_feed = both(dot_nt(grad_qvk, w_qvk), grad_qvk, ckv_share, sum_feed)
-    grad_attn = attn_products(
-        full_one, grad_qvk, full_back, attended, own_context, ckv_share, full_two, grad_two_all, quarter_parts, att_quarter
-    )
-    blocks, grad_attn, ckv_share, feed_parts, sum_feed_far = both(
-        scatter_half(partial), grad_attn, ckv_share, feed_parts, to_far(sum_feed)
+    grad_attn, grad_qvk, ckv_share, sum_feed, sum_feed_far, feed_near = both(
+        attn_products(
+            full_one, grad_qvk, full_back, attended, own_context, ckv_share, full_two, grad_two_all, quarter_parts, att_quarter
+        ),
+        grad_qvk,
+        ckv_share,
+        sum_feed,
+        to_far(sum_feed),
+        gather_x(sum_feed),
     )
     parts_attn = plane_parts(grad_attn)
-    feed_all = gather_x(jnp.stack([sum_feed, sum_feed_far]))
+    half = 4 * ROWS
+    blocks = halves_sum(dot_nt(grad_qvk[:half], w_qvk), dot_nt(grad_qvk[half:], w_qvk).astype(bf16))
+    blocks, ckv_share, sum_feed_far, feed_near = both(blocks, ckv_share, sum_feed_far, feed_near)
+    feed_all = [*feed_near, *gather_x(sum_feed_far)]
     cond_part = dot_nt(ckv_share, w_kv)[:cond_count]
     cond_part = (cond_part + to_partner(cond_part)).astype(bf16)
+    grad_one, feed_parts = both(scatter_x(blocks), feed_parts)
     feed_branch = summed(feed_parts)
     output = resid_two + feed_branch
-    grad_one, cond_part, sent_out = both(scatter_x(blocks), cond_part, permuted(output.astype(bf16)))
+    sent_out = permuted(output.astype(bf16))
     in_grad = grad_resid_one + unit_norm_back(norm_one, scale_one, summed(grad_one))
 
     def columns_of(back):
@@ -675,7 +687,6 @@
         return gain.astype(f32)[:, None]
 
     grad_feed_in, grad_feed_out = finish_feed(at, feed_all, column(gain_feed))
-    grad_feed_in = grad_feed_in.transpose(1, 0, 2)
 
     def row_sums(w, grad):
         sums = jnp.sum(w.astype(f32) * grad.astype(f32), axis=1)
@@ -688,26 +699,23 @@
 
     moved_in = lax.ppermute(permuted(in_grad.astype(bf16)), ("yh", "tp"), SWAP)
     moved_out = lax.ppermute(sent_out, ("yh", "tp"), SWAP)
-    parts_attn, moved_in, moved_out, small, cond_near, grad_feed_in, grad_feed_out = both(
-        parts_attn, moved_in, moved_out, small, cond_near, grad_feed_in, grad_feed_out
+    parts_attn, moved_in, moved_out, small, grad_feed_in, grad_feed_out = both(
+        parts_attn, moved_in, moved_out, small, grad_feed_in, grad_feed_out
     )
     sum_attn = total(parts_attn)
     attn_own, cond_near = both(sum_attn.astype(bf16), cond_near)
-    attn_far = to_far(attn_own)
-    attn_all = gather_x(jnp.stack([attn_own, attn_far]))
+    attn_near, attn_far, sum_attn, small, moved_in, moved_out, cond_near = both(
+        gather_x(attn_own), to_far(attn_own), sum_attn, small, moved_in, moved_out, cond_near
+    )
+    attn_all = [*attn_near, *gather_x(attn_far)]
     more = [row_sums(qvk_cols, sum_attn[:, : 3 * quarter])]
     more += [row_sums(own_cols(cq_half, quarter), sum_attn[:, 6 * quarter : 7 * quarter])]
-    small = jnp.concatenate([*more, small]).reshape(4, 128)
-    small_blocks = gather_x(small + to_partner(small))
+    small = sent_to_all(jnp.concatenate([*more, small])[None], ("x", "yh", "tp"), 16).reshape(4, 2, 2, 4, 128)
     in_grad = lax.all_gather(moved_in, "tp", axis=0, tiled=False).astype(f32)
     layer_out = lax.all_gather(moved_out, "tp", axis=0, tiled=False)
-    cond_grad = finish_cond(at, cond_near, to_far(cond_near))
-    attn_all, small_blocks, cond_grad, in_grad, layer_out = both(attn_all, small_blocks, cond_grad, in_grad, layer_out)
+    cond_grad = finish_cond(at, cond_near, to_far(cond_near)).transpose(1, 0, 2)
     proj, out, keyval, query, cross = finish_columns(at, attn_all, column(gain_attn), column(gain_cross))
-    small = jnp.stack(small_blocks)
-    small = sum(lax.dynamic_index_in_dim(small, (x + 4 - q) % 4, 0, False) for q in range(4))
-    other = lax.ppermute(small, "yh", ((0, 1), (1, 0)))
-    small = jnp.where(yh == 0, jnp.stack([small, other]), jnp.stack([other, small]))
+    small = jnp.sum(small, axis=(0, 2))
     layer_stats = jnp.sqrt(small[:, 3, :5] / (lengths.astype(f32)[:, None] * D))
     gains = [small[:, k, :half_rows].reshape(2 * half_rows) for k in range(3)]
 
@@ -721,7 +729,7 @@
         out,
         gains[1],
         query,
-        keyval.transpose(1, 0, 2),
+        keyval,
         cross,
         gains[2],
         grad_feed_in,

time: 568 us -> 531 us (0.935)
  local copies, waits for them, and re-layouts: 59.3 us -> 39.2 us
  waiting for transfers between devices: 177 us -> 169 us
  other arithmetic: 62.5 us -> 55.4 us
  blocking collectives: 10.8 us -> 4.94 us
    unnamed x121 -> x126, local copies, waits for them, and re-layouts: 19 us -> 3.19 us
    ppermute x1, waiting for transfers between devices: 6.67 us -> 0.01 us  [per_device(): lax.ppermute(lax.dynamic_index_in_dim(hidden_in, tp, 0, False), ('yh', 't...]
    ppermute x16 -> x15, starting transfers between devices: 14.9 us -> 10.9 us  [to_partner(): return lax.ppermute(v, 'tp', ((0, 1), (1, 0)))]
    ppermute x16 -> x15, waiting for transfers between devices: 15.7 us -> 12.7 us  [to_partner(): return lax.ppermute(v, 'tp', ((0, 1), (1, 0)))]
    ppermute x51 -> x54, starting transfers between devices: 57.3 us -> 59.6 us  [along_x(): return lax.ppermute(v, 'x', [(i, (i + step) % 4) for i in range(4)])]
    ppermute x51 -> x54, waiting for transfers between devices: 148 us -> 149 us  [along_x(): return lax.ppermute(v, 'x', [(i, (i + step) % 4) for i in range(4)])]
    dot_general x7 -> x8, matrix products: 26.9 us -> 27 us  [dot_nt(): lax.dot_general(a, b, (((1,), (1,)), ((), ())), preferred_element_type=f32)]
  transfers between devices with their start and end apart: 79 -> 81, of which waited for: 33 -> 41; matrix products, arithmetic and copies ran while one was open for 25% -> 25% of each run, Pallas kernels for 14% -> 15%
where the time goes in v4:
time: 531 us; the launch traced here: 521 us
  waiting for transfers between devices  169 us (32%)
  starting transfers between devices  101 us (19%)
  Pallas kernels  80.3 us (15%)
  matrix products  55.8 us (11%)
  other arithmetic  55.4 us (10%)
  local copies, waits for them, and re-layouts  39.2 us (7%)
  between operations  15.3 us (3%)
    ppermute x54, waiting for transfers between devices, along_x(): return lax.ppermute(v, 'x', [(i, (i + step) % 4) for i in range(4)])  149 us
    ppermute x54, starting transfers between devices, along_x(): return lax.ppermute(v, 'x', [(i, (i + step) % 4) for i in range(4)])  59.6 us
    dot_general x7, matrix products, dot(): return jnp.dot(a, b, preferred_element_type=f32)  28.8 us
    dot_general x8, matrix products, dot_nt(): lax.dot_general(a, b, (((1,), (1,)), ((), ())), preferred_element_type=f32)  27 us
    pallas_call x1, Pallas kernels, attn_backward(): pl.pallas_call(attn_backward_kernel, in_specs=[pl.BlockSpec(memory_space=...  16.1 us
    pallas_call x1, Pallas kernels, attn_forward(): pl.pallas_call(attn_forward_kernel, in_specs=[pl.BlockSpec(memory_space=p...  13.3 us
    pallas_call x1, Pallas kernels, products(): pl.pallas_call(lambda *refs: products_kernel(len(pairs), *refs), grid=(D...  12.9 us
    pallas_call x1, Pallas kernels, attn_products(): pl.pallas_call(attn_products_kernel, grid=(D // tile,), in_specs=specs +...  12.9 us
  transfers between devices with their start and end apart: 81, of which 41 were waited for; matrix products, arithmetic and copies ran while one was open for 25% of the time, Pallas kernels for 15%

profile of v4, /device:TPU:1, one launch (start us, length us, event | category | flops | bytes accessed | tf_op | source)
XLA Modules:
  0.0 520.8 jit_solution(9343396904641349251)
XLA Ops:
  14.6 6.3 %collective-permute-start = (bf16[128,1536]{1,0:T(8,128)(2,1)S(1)}, bf16[128,1536]{1,0:T(8,128)(2,1)S(1)}, u32[]{:S(2)}, u32[]{:S(2)}) collective-permute-start(bf16[128,1536]{1,0:T(8,128)(2,1)S(1)} %dynamic-slice_bitcast_fusion.2), channel_id=1, source_target_pairs={{0,0},{1,2},{2,1},{3,3},{4,4},{5,6},{6,5},{7,7},{8,8},{9,10},{10,9... | collective-permute-start | bytes 1179656 | tf_op jit(solution)/shard_map/ppermute | solution.py:565
  24.7 3.1 fusion.61
  37.1 10.7 %collective-permute-done.3 = bf16[128,1536]{1,0:T(8,128)(2,1)} collective-permute-done((bf16[128,1536]{1,0:T(8,128)(2,1)S(1)}, bf16[128,1536]{1,0:T(8,128)(2,1)}, u32[]{:S(2)}, u32[]{:S(2)}) %collective-permute-start.3) | collective-permute-done | bytes 393248 | tf_op jit(solution)/shard_map/ppermute | solution.py:72
  47.8 4.0 collective-permute-done.1
  60.6 9.3 %collective-permute-done.8 = bf16[128,1536]{1,0:T(8,128)(2,1)S(1)} collective-permute-done((bf16[128,1536]{1,0:T(8,128)(2,1)S(1)}, bf16[128,1536]{1,0:T(8,128)(2,1)S(1)}, u32[]{:S(2)}, u32[]{:S(2)}) %collective-permute-start.8) | collective-permute-done | bytes 393248 | tf_op jit(solution)/shard_map/ppermute | solution.py:72
  71.2 9.1 %collective-permute-done.6 = bf16[128,1536]{1,0:T(8,128)(2,1)S(1)} collective-permute-done((bf16[128,1536]{1,0:T(8,128)(2,1)S(1)}, bf16[128,1536]{1,0:T(8,128)(2,1)S(1)}, u32[]{:S(2)}, u32[]{:S(2)}) %collective-permute-start.6) | collective-permute-done | bytes 393248 | tf_op jit(solution)/shard_map/ppermute | solution.py:72
  80.4 3.3 pad_maximum_fusion.one
  90.9 6.6 %fusion.19.qkv = f32[1024,640]{1,0:T(8,128)} fusion(bf16[1024,1536]{1,0:T(8,128)(2,1)} %pad_maximum_fusion.one, bf16[1536,2688]{1,0:T(8,128)(2,1)} %all-gather.5.cloned.1.call-done), kind=kOutput, calls=%fused_computation.44 | convolution fusion | flops 2013265920 | bytes 7733248 | tf_op jit(solution)/shard_map/dot_general | solution.py:40
  102.5 13.3 %shard_map.254 = (bf16[1024,256]{1,0:T(8,128)(2,1)}, bf16[1024,256]{1,0:T(8,128)(2,1)}, bf16[1024,256]{1,0:T(8,128)(2,1)}, bf16[1024,256]{1,0:T(8,128)(2,1)}, f32[8,1024]{1,0:T(8,128)}) custom-call(s32[3]{0:T(128)} %pad_add_fusion.sc, f32[1024,640]{1,0:T(8,128)} %fusion.19.qkv, f32[1024,128]{1,0:T(8,128)} %get-tuple-element.161.cosine, ...), custom_call_target="tpu_custom_call" | custom-call | flops 3221225472 | bytes 8388608 | tf_op jit(solution)/shard_map/pallas_call | solution.py:207
  120.0 3.0 collective-permute-done.13
  126.4 7.7 %collective-permute-done.14 = bf16[128,1536]{1,0:T(8,128)(2,1)S(1)} collective-permute-done((bf16[128,1536]{1,0:T(8,128)(2,1)S(1)}, bf16[128,1536]{1,0:T(8,128)(2,1)S(1)}, u32[]{:S(2)}, u32[]{:S(2)}) %collective-permute-start.14) | collective-permute-done | bytes 393248 | tf_op jit(solution)/shard_map/ppermute | solution.py:72
  135.6 9.2 %collective-permute-done.16 = bf16[128,1536]{1,0:T(8,128)(2,1)} collective-permute-done((bf16[128,1536]{1,0:T(8,128)(2,1)S(1)}, bf16[128,1536]{1,0:T(8,128)(2,1)}, u32[]{:S(2)}, u32[]{:S(2)}) %collective-permute-start.16) | collective-permute-done | bytes 393248 | tf_op jit(solution)/shard_map/ppermute | solution.py:72
  150.0 3.2 fusion.24.cq
  154.0 4.6 shard_map.255
  167.3 5.2 %fusion.7 = f32[1024,768]{1,0:T(8,128)S(1)} fusion(bf16[1024,1536]{1,0:T(8,128)(2,1)} %pad_maximum_fusion.1.refs_2_, bf16[1536,2304]{1,0:T(8,128)(2,1)} %all-gather.7.cloned.1.call-done), kind=kOutput, calls=%fused_computation.26 | convolution fusion | flops 2415919104 | bytes 8650752 | tf_op jit(solution)/shard_map/dot_general | solution.py:40
  177.3 9.2 %collective-permute-done.19 = bf16[128,1536]{1,0:T(8,128)(2,1)} collective-permute-done((bf16[128,1536]{1,0:T(8,128)(2,1)S(1)}, bf16[128,1536]{1,0:T(8,128)(2,1)}, u32[]{:S(2)}, u32[]{:S(2)}) %collective-permute-start.19) | collective-permute-done | bytes 393248 | tf_op jit(solution)/shard_map/ppermute | solution.py:72
  188.4 3.0 collective-permute-done.22
  195.8 5.0 fusion.2
  200.8 2.9 multiply_convert_fusion.2
  203.7 5.1 fusion
  208.8 7.3 %collective-permute-done.23.rest_5_ = bf16[128,1920]{1,0:T(8,128)(2,1)S(1)} collective-permute-done((bf16[128,1920]{1,0:T(8,128)(2,1)S(1)}, bf16[128,1920]{1,0:T(8,128)(2,1)S(1)}, u32[]{:S(2)}, u32[]{:S(2)}) %collective-permute-start.23) | collective-permute-done | bytes 491552 | tf_op jit(solution)/shard_map/ppermute | solution.py:72
  230.9 12.9 %shard_map.256 = bf16[1536,2304]{1,0:T(8,128)(2,1)} custom-call(bf16[1024,1536]{1,0:T(8,128)(2,1)} %copy-done.7, bf16[1024,1536]{1,0:T(8,128)(2,1)} %pad_maximum_fusion.3.refs_1_, bf16[1024,1536]{1,0:T(8,128)(2,1)} %pad_maximum_fusion.1.refs_2_, bf16[1024,768]{1,0:T(8,128)(2,1)} %get-tuple-element.223.refs_3_), custom_call_target="tpu_custom_call" | custom-call | flops 7247757312 | bytes 10485760 | tf_op jit(solution)/shard_map/pallas_call | solution.py:389
  247.3 4.3 collective-permute-done.29
  258.1 3.4 fusion.27.grad
  261.5 5.9 %shard_map.257 = (bf16[256,768]{1,0:T(8,128)(2,1)}, bf16[4,272,384]{2,1,0:T(8,128)(2,1)}) custom-call(s32[3]{0:T(128)} %pad_add_fusion.sc, bf16[256,768]{1,0:T(8,128)(2,1)} %fusion.24.cq, bf16[4,144,384]{2,1,0:T(8,128)(2,1)} %pad_maximum_fusion.16.kv, f32[144,256]{1,0:T(8,128)} %broadcast_in_dim.128.bias, bf16[256,768]{1,0:T(8,128)(2,1)} %fusion.27.grad), custom_call_target="tpu_custom_call" | custom-call | flops 566231040 | bytes 3145728 | tf_op jit(solution)/shard_map/pallas_call | solution.py:349
  269.0 9.1 %collective-permute-done.32 = bf16[128,1536]{1,0:T(8,128)(2,1)} collective-permute-done((bf16[128,1536]{1,0:T(8,128)(2,1)}, bf16[128,1536]{1,0:T(8,128)(2,1)}, u32[]{:S(2)}, u32[]{:S(2)}) %collective-permute-start.32) | collective-permute-done | bytes 393248 | tf_op jit(solution)/shard_map/ppermute | solution.py:72
  288.4 8.6 %collective-permute-done.38 = bf16[128,1536]{1,0:T(8,128)(2,1)S(1)} collective-permute-done((bf16[128,1536]{1,0:T(8,128)(2,1)S(1)}, bf16[128,1536]{1,0:T(8,128)(2,1)S(1)}, u32[]{:S(2)}, u32[]{:S(2)}) %collective-permute-start.38) | collective-permute-done | bytes 393248 | tf_op jit(solution)/shard_map/ppermute | solution.py:72
  299.1 9.2 %collective-permute-done.36 = bf16[128,1536]{1,0:T(8,128)(2,1)S(1)} collective-permute-done((bf16[128,1536]{1,0:T(8,128)(2,1)S(1)}, bf16[128,1536]{1,0:T(8,128)(2,1)S(1)}, u32[]{:S(2)}, u32[]{:S(2)}) %collective-permute-start.36) | collective-permute-done | bytes 393248 | tf_op jit(solution)/shard_map/ppermute | solution.py:72
  310.9 4.5 convolution_convert_fusion
  315.7 3.6 convolution_convert_fusion.2.grad
  324.6 16.1 %shard_map.258.grad = bf16[1024,640]{1,0:T(8,128)(2,1)} custom-call(bf16[1024,256]{1,0:T(8,128)(2,1)} %get-tuple-element.163.qs, bf16[1024,256]{1,0:T(8,128)(2,1)} %get-tuple-element.164.ks, bf16[1024,256]{1,0:T(8,128)(2,1)} %get-tuple-element.165.vs, bf16[1024,256]{1,0:T(8,128)(2,1)} %convolution_convert_fusion.2.grad, f32[8,1024]{1,0:T(8,128)} %get-tuple-element.228.lse, ...), custom_call_target="tpu_custom_call" | custom-call | flops 8053063680 | bytes 8388608 | tf_op jit(solution)/shard_map/pallas_call | solution.py:257
  349.1 12.9 %shard_map.259 = bf16[1536,1536]{1,0:T(8,128)(2,1)} custom-call(bf16[1024,1536]{1,0:T(8,128)(2,1)} %pad_maximum_fusion.one, bf16[1024,640]{1,0:T(8,128)(2,1)} %shard_map.258.grad, bf16[1024,1536]{1,0:T(8,128)(2,1)} %copy-done.2, bf16[1024,256]{1,0:T(8,128)(2,1)} %get-tuple-element.168.att, bf16[144,1536]{1,0:T(8,128)(2,1)} %copy-done.13, ...), custom_call_target="tpu_custom_call" | custom-call | flops 4831838208 | bytes 16777216 | tf_op jit(solution)/shard_map/pallas_call | solution.py:427
  362.0 4.5 collective-permute-done.46.refs_2_
  366.5 4.3 convolution_convert_fusion.1
  380.5 4.6 all-to-all-start
  385.1 3.6 fusion.5
  392.2 3.7 collective-permute-done.53
  403.9 18.6 %collective-permute-done.49 = bf16[128,1536]{1,0:T(8,128)(2,1)S(1)} collective-permute-done((bf16[128,1536]{1,0:T(8,128)(2,1)S(1)}, bf16[128,1536]{1,0:T(8,128)(2,1)S(1)}, u32[]{:S(2)}, u32[]{:S(2)}) %collective-permute-start.49) | collective-permute-done | bytes 393248 | tf_op jit(solution)/shard_map/ppermute | solution.py:72
  422.4 3.7 collective-permute-start.60
  427.1 2.9 fusion.90
  430.7 3.3 stack.78
  441.7 4.4 collective-permute-start.57
  446.2 6.6 %shard_map.260 = (f32[192,2,3072]{2,1,0:T(2,128)}, f32[192,3072]{1,0:T(8,128)}) custom-call(s32[2]{0:T(128)} %pad_add_fusion.1.at, bf16[96,2304]{1,0:T(8,128)(2,1)} %reduce-scatter.2.cloned.1.call-done.refs_0_, bf16[96,2304]{1,0:T(8,128)(2,1)} %copy-done.32, bf16[96,2304]{1,0:T(8,128)(2,1)} %collective-permute-done.46.refs_2_, ...), custom_call_target="tpu_custom_call" | custom-call | flops 4194304 | bytes 11534336 | tf_op jit(solution)/shard_map/pallas_call | solution.py:459
  463.4 3.2 convert_reduce_fusion
  472.7 5.2 %collective-permute-done.68.refs_1_ = bf16[96,1536]{1,0:T(8,128)(2,1)S(1)} collective-permute-done((bf16[96,1536]{1,0:T(8,128)(2,1)S(1)}, bf16[96,1536]{1,0:T(8,128)(2,1)S(1)}, u32[]{:S(2)}, u32[]{:S(2)}) %collective-permute-start.68) | collective-permute-done | bytes 294944 | tf_op jit(solution)/shard_map/ppermute | solution.py:72
  490.0 4.4 all-to-all-start.1
  498.1 3.6 all-to-all-done.1
  504.4 5.2 shard_map.262
  (407 shorter events, 201.8 us)
Async XLA Ops:
  7.2 82.0 %all-gather.5.cloned.1.call-start = ((), (), s32[]{:S(2)}) async-start(), calls=%async_computation.3 | async-start | bytes 8773632 | tf_op jit(solution)/shard_map/all_gather | solution.py:130
  14.5 152.9 %all-gather.7.cloned.1.call-start = ((), (), s32[]{:S(2)}) async-start(), calls=%async_computation.4 | async-start | bytes 7520256 | tf_op jit(solution)/shard_map/all_gather | solution.py:130
  22.7 30.8 %collective-permute-start.4 = (bf16[128,1536]{1,0:T(8,128)(2,1)}, bf16[128,1536]{1,0:T(8,128)(2,1)}, u32[]{:S(2)}, u32[]{:S(2)}) collective-permute-start(bf16[128,1536]{1,0:T(8,128)(2,1)} %dynamic-slice_bitcast_fusion.1), channel_id=1, source_target_pairs={{0,0},{1,2},{2,1},{3,3},{4,4},{5,6},{6,5},{7,7},{8,8},{9,10},{10,9... | collective-permute-start | bytes 1179656 | tf_op jit(solution)/shard_map/ppermute | solution.py:566
  29.1 18.7 %collective-permute-start.3 = (bf16[128,1536]{1,0:T(8,128)(2,1)S(1)}, bf16[128,1536]{1,0:T(8,128)(2,1)}, u32[]{:S(2)}, u32[]{:S(2)}) collective-permute-start(bf16[128,1536]{1,0:T(8,128)(2,1)S(1)} %fusion.37), channel_id=1, source_target_pairs={{0,12},{4,0},{8,4},{12,8},{1,13},{5,1},{9,5},{13,9},{2,14},{6,2},{... | collective-permute-start | bytes 1179656 | tf_op jit(solution)/shard_map/ppermute | solution.py:72
  31.4 16.4 %collective-permute-start.2 = (bf16[128,1536]{1,0:T(8,128)(2,1)S(1)}, bf16[128,1536]{1,0:T(8,128)(2,1)}, u32[]{:S(2)}, u32[]{:S(2)}) collective-permute-start(bf16[128,1536]{1,0:T(8,128)(2,1)S(1)} %fusion.37), channel_id=1, source_target_pairs={{0,8},{4,12},{8,0},{12,4},{1,9},{5,13},{9,1},{13,5},{2,10},{6,14},... | collective-permute-start | bytes 1179656 | tf_op jit(solution)/shard_map/ppermute | solution.py:72
  32.2 19.7 %collective-permute-start.1 = (bf16[128,1536]{1,0:T(8,128)(2,1)S(1)}, bf16[128,1536]{1,0:T(8,128)(2,1)}, u32[]{:S(2)}, u32[]{:S(2)}) collective-permute-start(bf16[128,1536]{1,0:T(8,128)(2,1)S(1)} %fusion.37), channel_id=1, source_target_pairs={{0,4},{4,8},{8,12},{12,0},{1,5},{5,9},{9,13},{13,1},{2,6},{6,10},{... | collective-permute-start | bytes 1179656 | tf_op jit(solution)/shard_map/ppermute | solution.py:72
  36.7 304.2 %reduce-scatter.2.cloned.1.call-start = ((), (), s32[]{:S(2)}) async-start(), calls=%async_computation.5 | async-start | bytes 7520256 | tf_op jit(solution)/shard_map/reduce_scatter | solution.py:134
  53.5 26.9 %collective-permute-start.5 = (bf16[512,1536]{1,0:T(8,128)(2,1)S(1)}, bf16[512,1536]{1,0:T(8,128)(2,1)}, u32[]{:S(2)}, u32[]{:S(2)}) collective-permute-start(bf16[512,1536]{1,0:T(8,128)(2,1)S(1)} %pad_maximum_fusion.6), channel_id=1, source_target_pairs={{0,1},{1,0},{2,3},{3,2},{4,5},{5,4},{6,7},{7,6},{8,9},{9,8},{10,11... | collective-permute-start | bytes 4718600 | tf_op jit(solution)/shard_map/ppermute | solution.py:52
  59.5 20.7 %collective-permute-start.6 = (bf16[128,1536]{1,0:T(8,128)(2,1)S(1)}, bf16[128,1536]{1,0:T(8,128)(2,1)S(1)}, u32[]{:S(2)}, u32[]{:S(2)}) collective-permute-start(bf16[128,1536]{1,0:T(8,128)(2,1)S(1)} %concatenate.100), channel_id=1, source_target_pairs={{0,4},{4,8},{8,12},{12,0},{1,5},{5,9},{9,13},{13,1},{2,6},{6,10},{... | collective-permute-start | bytes 1179656 | tf_op jit(solution)/shard_map/ppermute | solution.py:72
  97.5 18.2 %collective-permute-start.10 = (bf16[144,384]{1,0:T(8,128)(2,1)S(1)}, bf16[144,384]{1,0:T(8,128)(2,1)S(1)}, u32[]{:S(2)}, u32[]{:S(2)}) collective-permute-start(bf16[144,384]{1,0:T(8,128)(2,1)S(1)} %convolution_convert_fusion.3), channel_id=1, source_target_pairs={{0,4},{4,8},{8,12},{12,0},{1,5},{5,9},{9,13},{13,1},{2,6},{6,10},{... | collective-permute-start | bytes 331784 | tf_op jit(solution)/shard_map/ppermute | solution.py:72
  98.7 17.1 %collective-permute-start.11 = (bf16[144,384]{1,0:T(8,128)(2,1)S(1)}, bf16[144,384]{1,0:T(8,128)(2,1)S(1)}, u32[]{:S(2)}, u32[]{:S(2)}) collective-permute-start(bf16[144,384]{1,0:T(8,128)(2,1)S(1)} %convolution_convert_fusion.3), channel_id=1, source_target_pairs={{0,8},{4,12},{8,0},{12,4},{1,9},{5,13},{9,1},{13,5},{2,10},{6,14},... | collective-permute-start | bytes 331784 | tf_op jit(solution)/shard_map/ppermute | solution.py:72
  125.8 19.1 %collective-permute-start.16 = (bf16[128,1536]{1,0:T(8,128)(2,1)S(1)}, bf16[128,1536]{1,0:T(8,128)(2,1)}, u32[]{:S(2)}, u32[]{:S(2)}) collective-permute-start(bf16[128,1536]{1,0:T(8,128)(2,1)S(1)} %get-tuple-element.172), channel_id=1, source_target_pairs={{0,4},{4,8},{8,12},{12,0},{1,5},{5,9},{9,13},{13,1},{2,6},{6,10},{... | collective-permute-start | bytes 1179656 | tf_op jit(solution)/shard_map/ppermute | solution.py:72
  166.9 19.5 %collective-permute-start.19 = (bf16[128,1536]{1,0:T(8,128)(2,1)S(1)}, bf16[128,1536]{1,0:T(8,128)(2,1)}, u32[]{:S(2)}, u32[]{:S(2)}) collective-permute-start(bf16[128,1536]{1,0:T(8,128)(2,1)S(1)} %fusion.58), channel_id=1, source_target_pairs={{0,4},{4,8},{8,12},{12,0},{1,5},{5,9},{9,13},{13,1},{2,6},{6,10},{... | collective-permute-start | bytes 1179656 | tf_op jit(solution)/shard_map/ppermute | solution.py:72
  191.9 24.2 %collective-permute-start.23 = (bf16[128,1920]{1,0:T(8,128)(2,1)S(1)}, bf16[128,1920]{1,0:T(8,128)(2,1)S(1)}, u32[]{:S(2)}, u32[]{:S(2)}) collective-permute-start(bf16[128,1920]{1,0:T(8,128)(2,1)S(1)} %get-tuple-element.393), channel_id=1, source_target_pairs={{0,4},{4,8},{8,12},{12,0},{1,5},{5,9},{9,13},{13,1},{2,6},{6,10},{... | collective-permute-start | bytes 1474568 | tf_op jit(solution)/shard_map/ppermute | solution.py:72
  192.0 24.1 %collective-permute-start.24 = (bf16[128,1920]{1,0:T(8,128)(2,1)S(1)}, bf16[128,1920]{1,0:T(8,128)(2,1)S(1)}, u32[]{:S(2)}, u32[]{:S(2)}) collective-permute-start(bf16[128,1920]{1,0:T(8,128)(2,1)S(1)} %get-tuple-element.394), channel_id=1, source_target_pairs={{0,8},{4,12},{8,0},{12,4},{1,9},{5,13},{9,1},{13,5},{2,10},{6,14},... | collective-permute-start | bytes 1474568 | tf_op jit(solution)/shard_map/ppermute | solution.py:72
  193.6 22.9 %collective-permute-start.25 = (bf16[128,1920]{1,0:T(8,128)(2,1)S(1)}, bf16[128,1920]{1,0:T(8,128)(2,1)S(1)}, u32[]{:S(2)}, u32[]{:S(2)}) collective-permute-start(bf16[128,1920]{1,0:T(8,128)(2,1)S(1)} %get-tuple-element.392), channel_id=1, source_target_pairs={{0,12},{4,0},{8,4},{12,8},{1,13},{5,1},{9,5},{13,9},{2,14},{6,2},{... | collective-permute-start | bytes 1474568 | tf_op jit(solution)/shard_map/ppermute | solution.py:72
  228.0 19.3 %collective-permute-start.27 = (bf16[128,1536]{1,0:T(8,128)(2,1)}, bf16[128,1536]{1,0:T(8,128)(2,1)}, u32[]{:S(2)}, u32[]{:S(2)}) collective-permute-start(bf16[128,1536]{1,0:T(8,128)(2,1)} %get-tuple-element.201), channel_id=1, source_target_pairs={{0,12},{4,0},{8,4},{12,8},{1,13},{5,1},{9,5},{13,9},{2,14},{6,2},{... | collective-permute-start | bytes 1179656 | tf_op jit(solution)/shard_map/ppermute | solution.py:72
  230.3 17.0 %collective-permute-start.28 = (bf16[128,1536]{1,0:T(8,128)(2,1)}, bf16[128,1536]{1,0:T(8,128)(2,1)}, u32[]{:S(2)}, u32[]{:S(2)}) collective-permute-start(bf16[128,1536]{1,0:T(8,128)(2,1)} %get-tuple-element.202), channel_id=1, source_target_pairs={{0,8},{4,12},{8,0},{12,4},{1,9},{5,13},{9,1},{13,5},{2,10},{6,14},... | collective-permute-start | bytes 1179656 | tf_op jit(solution)/shard_map/ppermute | solution.py:72
  230.6 21.0 %collective-permute-start.29 = (bf16[128,1536]{1,0:T(8,128)(2,1)}, bf16[128,1536]{1,0:T(8,128)(2,1)}, u32[]{:S(2)}, u32[]{:S(2)}) collective-permute-start(bf16[128,1536]{1,0:T(8,128)(2,1)} %get-tuple-element.203), channel_id=1, source_target_pairs={{0,4},{4,8},{8,12},{12,0},{1,5},{5,9},{9,13},{13,1},{2,6},{6,10},{... | collective-permute-start | bytes 1179656 | tf_op jit(solution)/shard_map/ppermute | solution.py:72
  257.2 21.0 %collective-permute-start.32 = (bf16[128,1536]{1,0:T(8,128)(2,1)}, bf16[128,1536]{1,0:T(8,128)(2,1)}, u32[]{:S(2)}, u32[]{:S(2)}) collective-permute-start(bf16[128,1536]{1,0:T(8,128)(2,1)} %get-tuple-element.309), channel_id=1, source_target_pairs={{0,4},{4,8},{8,12},{12,0},{1,5},{5,9},{9,13},{13,1},{2,6},{6,10},{... | collective-permute-start | bytes 1179656 | tf_op jit(solution)/shard_map/ppermute | solution.py:72
  286.1 22.3 %collective-permute-start.39 = (bf16[512,1536]{1,0:T(8,128)(2,1)S(1)}, bf16[512,1536]{1,0:T(8,128)(2,1)S(1)}, u32[]{:S(2)}, u32[]{:S(2)}) collective-permute-start(bf16[512,1536]{1,0:T(8,128)(2,1)S(1)} %pad_maximum_fusion.10), channel_id=1, source_target_pairs={{0,1},{1,0},{2,3},{3,2},{4,5},{5,4},{6,7},{7,6},{8,9},{9,8},{10,11... | collective-permute-start | bytes 4718600 | tf_op jit(solution)/shard_map/ppermute | solution.py:52
  287.5 20.8 %collective-permute-start.36 = (bf16[128,1536]{1,0:T(8,128)(2,1)S(1)}, bf16[128,1536]{1,0:T(8,128)(2,1)S(1)}, u32[]{:S(2)}, u32[]{:S(2)}) collective-permute-start(bf16[128,1536]{1,0:T(8,128)(2,1)S(1)} %get-tuple-element.218), channel_id=1, source_target_pairs={{0,4},{4,8},{8,12},{12,0},{1,5},{5,9},{9,13},{13,1},{2,6},{6,10},{... | collective-permute-start | bytes 1179656 | tf_op jit(solution)/shard_map/ppermute | solution.py:72
  320.1 20.7 %collective-permute-start.41 = (bf16[272,384]{1,0:T(8,128)(2,1)}, bf16[272,384]{1,0:T(8,128)(2,1)S(1)}, u32[]{:S(2)}, u32[]{:S(2)}) collective-permute-start(bf16[272,384]{1,0:T(8,128)(2,1)} %get-tuple-element.341), channel_id=1, source_target_pairs={{0,4},{4,8},{8,12},{12,0},{1,5},{5,9},{9,13},{13,1},{2,6},{6,10},{... | collective-permute-start | bytes 626696 | tf_op jit(solution)/shard_map/ppermute | solution.py:72
  320.1 20.7 %collective-permute-start.42 = (bf16[272,384]{1,0:T(8,128)(2,1)S(1)}, bf16[272,384]{1,0:T(8,128)(2,1)S(1)}, u32[]{:S(2)}, u32[]{:S(2)}) collective-permute-start(bf16[272,384]{1,0:T(8,128)(2,1)S(1)} %get-tuple-element.340), channel_id=1, source_target_pairs={{0,8},{4,12},{8,0},{12,4},{1,9},{5,13},{9,1},{13,5},{2,10},{6,14},... | collective-permute-start | bytes 626696 | tf_op jit(solution)/shard_map/ppermute | solution.py:72
  321.6 19.2 %collective-permute-start.43 = (bf16[272,384]{1,0:T(8,128)(2,1)S(1)}, bf16[272,384]{1,0:T(8,128)(2,1)S(1)}, u32[]{:S(2)}, u32[]{:S(2)}) collective-permute-start(bf16[272,384]{1,0:T(8,128)(2,1)S(1)} %get-tuple-element.339), channel_id=1, source_target_pairs={{0,12},{4,0},{8,4},{12,8},{1,13},{5,1},{9,5},{13,9},{2,14},{6,2},{... | collective-permute-start | bytes 626696 | tf_op jit(solution)/shard_map/ppermute | solution.py:72
  324.0 49.7 %collective-permute-start.52 = (bf16[512,1536]{1,0:T(8,128)(2,1)}, bf16[512,1536]{1,0:T(8,128)(2,1)}, u32[]{:S(2)}, u32[]{:S(2)}) collective-permute-start(bf16[512,1536]{1,0:T(8,128)(2,1)} %slice.521), channel_id=1, source_target_pairs={{0,1},{1,0},{2,3},{3,2},{4,5},{5,4},{6,7},{7,6},{8,9},{9,8},{10,11... | collective-permute-start | bytes 4718600 | tf_op jit(solution)/shard_map/ppermute | solution.py:52
  340.8 21.1 %collective-permute-start.44 = (bf16[96,2304]{1,0:T(8,128)(2,1)}, bf16[96,2304]{1,0:T(8,128)(2,1)}, u32[]{:S(2)}, u32[]{:S(2)}) collective-permute-start(bf16[96,2304]{1,0:T(8,128)(2,1)} %reduce-scatter.2.cloned.1.call-done.refs_0_), channel_id=1, source_target_pairs={{0,2},{2,0},{1,3},{3,1},{4,6},{6,4},{5,7},{7,5},{8,10},{10,8},{9,1... | collective-permute-start | bytes 1327112 | tf_op jit(solution)/shard_map/ppermute | solution.py:96
  343.6 18.3 %collective-permute-start.45 = (bf16[96,2304]{1,0:T(8,128)(2,1)}, bf16[96,2304]{1,0:T(8,128)(2,1)S(1)}, u32[]{:S(2)}, u32[]{:S(2)}) collective-permute-start(bf16[96,2304]{1,0:T(8,128)(2,1)} %reduce-scatter.2.cloned.1.call-done.refs_0_), channel_id=1, source_target_pairs={{0,4},{4,8},{8,12},{12,0},{1,5},{5,9},{9,13},{13,1},{2,6},{6,10},{... | collective-permute-start | bytes 1327112 | tf_op jit(solution)/shard_map/ppermute | solution.py:72
  344.3 22.2 %collective-permute-start.46 = (bf16[96,2304]{1,0:T(8,128)(2,1)}, bf16[96,2304]{1,0:T(8,128)(2,1)}, u32[]{:S(2)}, u32[]{:S(2)}) collective-permute-start(bf16[96,2304]{1,0:T(8,128)(2,1)} %reduce-scatter.2.cloned.1.call-done.refs_0_), channel_id=1, source_target_pairs={{0,8},{4,12},{8,0},{12,4},{1,9},{5,13},{9,1},{13,5},{2,10},{6,14},... | collective-permute-start | bytes 1327112 | tf_op jit(solution)/shard_map/ppermute | solution.py:72
  346.3 20.2 %collective-permute-start.47 = (bf16[96,2304]{1,0:T(8,128)(2,1)}, bf16[96,2304]{1,0:T(8,128)(2,1)}, u32[]{:S(2)}, u32[]{:S(2)}) collective-permute-start(bf16[96,2304]{1,0:T(8,128)(2,1)} %reduce-scatter.2.cloned.1.call-done.refs_0_), channel_id=1, source_target_pairs={{0,12},{4,0},{8,4},{12,8},{1,13},{5,1},{9,5},{13,9},{2,14},{6,2},{... | collective-permute-start | bytes 1327112 | tf_op jit(solution)/shard_map/ppermute | solution.py:72
  377.0 18.9 %collective-permute-start.53 = (bf16[128,1536]{1,0:T(8,128)(2,1)S(1)}, bf16[128,1536]{1,0:T(8,128)(2,1)S(1)}, u32[]{:S(2)}, u32[]{:S(2)}) collective-permute-start(bf16[128,1536]{1,0:T(8,128)(2,1)S(1)} %get-tuple-element.322), channel_id=1, source_target_pairs={{0,12},{4,0},{8,4},{12,8},{1,13},{5,1},{9,5},{13,9},{2,14},{6,2},{... | collective-permute-start | bytes 1179656 | tf_op jit(solution)/shard_map/ppermute | solution.py:72
  379.3 19.4 %collective-permute-start.54 = (bf16[128,1536]{1,0:T(8,128)(2,1)}, bf16[128,1536]{1,0:T(8,128)(2,1)}, u32[]{:S(2)}, u32[]{:S(2)}) collective-permute-start(bf16[128,1536]{1,0:T(8,128)(2,1)} %get-tuple-element.321), channel_id=1, source_target_pairs={{0,8},{4,12},{8,0},{12,4},{1,9},{5,13},{9,1},{13,5},{2,10},{6,14},... | collective-permute-start | bytes 1179656 | tf_op jit(solution)/shard_map/ppermute | solution.py:72
  380.2 21.1 %collective-permute-start.55 = (bf16[128,1536]{1,0:T(8,128)(2,1)}, bf16[128,1536]{1,0:T(8,128)(2,1)}, u32[]{:S(2)}, u32[]{:S(2)}) collective-permute-start(bf16[128,1536]{1,0:T(8,128)(2,1)} %get-tuple-element.320), channel_id=1, source_target_pairs={{0,4},{4,8},{8,12},{12,0},{1,5},{5,9},{9,13},{13,1},{2,6},{6,10},{... | collective-permute-start | bytes 1179656 | tf_op jit(solution)/shard_map/ppermute | solution.py:72
  380.5 82.9 %all-to-all-start = ((bf16[16,96,1536]{2,1,0:T(8,128)(2,1)}), bf16[16,96,1536]{2,1,0:T(8,128)(2,1)}, u32[]{:S(2)}, u32[]{:S(2)}) async-start(bf16[16,96,1536]{2,1,0:T(8,128)(2,1)} %bitcast.68), calls=%async_computation.1 | async-start | bytes 9437184 | tf_op jit(solution)/shard_map/all_to_all | solution.py:56
  388.9 33.5 %collective-permute-start.49 = (bf16[128,1536]{1,0:T(8,128)(2,1)S(1)}, bf16[128,1536]{1,0:T(8,128)(2,1)S(1)}, u32[]{:S(2)}, u32[]{:S(2)}) collective-permute-start(bf16[128,1536]{1,0:T(8,128)(2,1)S(1)} %get-tuple-element.248), channel_id=1, source_target_pairs={{0,12},{4,0},{8,4},{12,8},{1,13},{5,1},{9,5},{13,9},{2,14},{6,2},{... | collective-permute-start | bytes 1179656 | tf_op jit(solution)/shard_map/ppermute | solution.py:72
  391.3 34.7 %collective-permute-start.50 = (bf16[128,1536]{1,0:T(8,128)(2,1)S(1)}, bf16[128,1536]{1,0:T(8,128)(2,1)S(1)}, u32[]{:S(2)}, u32[]{:S(2)}) collective-permute-start(bf16[128,1536]{1,0:T(8,128)(2,1)S(1)} %get-tuple-element.249), channel_id=1, source_target_pairs={{0,8},{4,12},{8,0},{12,4},{1,9},{5,13},{9,1},{13,5},{2,10},{6,14},... | collective-permute-start | bytes 1179656 | tf_op jit(solution)/shard_map/ppermute | solution.py:72
  395.9 31.2 %collective-permute-start.51 = (bf16[128,1536]{1,0:T(8,128)(2,1)S(1)}, bf16[128,1536]{1,0:T(8,128)(2,1)S(1)}, u32[]{:S(2)}, u32[]{:S(2)}) collective-permute-start(bf16[128,1536]{1,0:T(8,128)(2,1)S(1)} %get-tuple-element.250), channel_id=1, source_target_pairs={{0,4},{4,8},{8,12},{12,0},{1,5},{5,9},{9,13},{13,1},{2,6},{6,10},{... | collective-permute-start | bytes 1179656 | tf_op jit(solution)/shard_map/ppermute | solution.py:72
  398.8 38.5 %collective-permute-start.58 = (bf16[96,2304]{1,0:T(8,128)(2,1)}, bf16[96,2304]{1,0:T(8,128)(2,1)}, u32[]{:S(2)}, u32[]{:S(2)}) collective-permute-start(bf16[96,2304]{1,0:T(8,128)(2,1)} %collective-permute-done.44.refs_4_), channel_id=1, source_target_pairs={{0,4},{4,8},{8,12},{12,0},{1,5},{5,9},{9,13},{13,1},{2,6},{6,10},{... | collective-permute-start | bytes 1327112 | tf_op jit(solution)/shard_map/ppermute | solution.py:72
  401.3 37.8 %collective-permute-start.59 = (bf16[96,2304]{1,0:T(8,128)(2,1)}, bf16[96,2304]{1,0:T(8,128)(2,1)}, u32[]{:S(2)}, u32[]{:S(2)}) collective-permute-start(bf16[96,2304]{1,0:T(8,128)(2,1)} %collective-permute-done.44.refs_4_), channel_id=1, source_target_pairs={{0,8},{4,12},{8,0},{12,4},{1,9},{5,13},{9,1},{13,5},{2,10},{6,14},... | collective-permute-start | bytes 1327112 | tf_op jit(solution)/shard_map/ppermute | solution.py:72
  422.4 19.3 %collective-permute-start.60 = (bf16[96,2304]{1,0:T(8,128)(2,1)}, bf16[96,2304]{1,0:T(8,128)(2,1)}, u32[]{:S(2)}, u32[]{:S(2)}) collective-permute-start(bf16[96,2304]{1,0:T(8,128)(2,1)} %collective-permute-done.44.refs_4_), channel_id=1, source_target_pairs={{0,12},{4,0},{8,4},{12,8},{1,13},{5,1},{9,5},{13,9},{2,14},{6,2},{... | collective-permute-start | bytes 1327112 | tf_op jit(solution)/shard_map/ppermute | solution.py:72
  436.3 16.4 %collective-permute-start.64 = (bf16[130,384]{1,0:T(8,128)(2,1)S(1)}, bf16[130,384]{1,0:T(8,128)(2,1)S(1)}, u32[]{:S(2)}, u32[]{:S(2)}) collective-permute-start(bf16[130,384]{1,0:T(8,128)(2,1)S(1)} %get-tuple-element.352), channel_id=1, source_target_pairs={{0,4},{4,8},{8,12},{12,0},{1,5},{5,9},{9,13},{13,1},{2,6},{6,10},{... | collective-permute-start | bytes 299528 | tf_op jit(solution)/shard_map/ppermute | solution.py:72
  436.4 16.4 %collective-permute-start.63 = (bf16[130,384]{1,0:T(8,128)(2,1)S(1)}, bf16[130,384]{1,0:T(8,128)(2,1)S(1)}, u32[]{:S(2)}, u32[]{:S(2)}) collective-permute-start(bf16[130,384]{1,0:T(8,128)(2,1)S(1)} %get-tuple-element.353), channel_id=1, source_target_pairs={{0,8},{4,12},{8,0},{12,4},{1,9},{5,13},{9,1},{13,5},{2,10},{6,14},... | collective-permute-start | bytes 299528 | tf_op jit(solution)/shard_map/ppermute | solution.py:72
  439.1 21.6 %collective-permute-start.56 = (bf16[128,1536]{1,0:T(8,128)(2,1)S(1)}, bf16[128,1536]{1,0:T(8,128)(2,1)S(1)}, u32[]{:S(2)}, u32[]{:S(2)}) collective-permute-start(bf16[128,1536]{1,0:T(8,128)(2,1)S(1)} %concatenate.121), channel_id=1, source_target_pairs={{0,0},{1,2},{2,1},{3,3},{4,4},{5,6},{6,5},{7,7},{8,8},{9,10},{10,9... | collective-permute-start | bytes 1179656 | tf_op jit(solution)/shard_map/ppermute | solution.py:700
  441.7 21.7 %collective-permute-start.57 = (bf16[128,1536]{1,0:T(8,128)(2,1)S(1)}, bf16[128,1536]{1,0:T(8,128)(2,1)S(1)}, u32[]{:S(2)}, u32[]{:S(2)}) collective-permute-start(bf16[128,1536]{1,0:T(8,128)(2,1)S(1)} %concatenate.122), channel_id=1, source_target_pairs={{0,0},{1,2},{2,1},{3,3},{4,4},{5,6},{6,5},{7,7},{8,8},{9,10},{10,9... | collective-permute-start | bytes 1179656 | tf_op jit(solution)/shard_map/ppermute | solution.py:701
  480.7 23.7 %collective-permute-start.73 = (bf16[96,1536]{1,0:T(8,128)(2,1)}, bf16[96,1536]{1,0:T(8,128)(2,1)}, u32[]{:S(2)}, u32[]{:S(2)}) collective-permute-start(bf16[96,1536]{1,0:T(8,128)(2,1)} %collective-permute-done.71.refs_4_), channel_id=1, source_target_pairs={{0,4},{4,8},{8,12},{12,0},{1,5},{5,9},{9,13},{13,1},{2,6},{6,10},{... | collective-permute-start | bytes 884744 | tf_op jit(solution)/shard_map/ppermute | solution.py:72
  481.5 22.9 %collective-permute-start.74 = (bf16[96,1536]{1,0:T(8,128)(2,1)}, bf16[96,1536]{1,0:T(8,128)(2,1)}, u32[]{:S(2)}, u32[]{:S(2)}) collective-permute-start(bf16[96,1536]{1,0:T(8,128)(2,1)} %collective-permute-done.71.refs_4_), channel_id=1, source_target_pairs={{0,8},{4,12},{8,0},{12,4},{1,9},{5,13},{9,1},{13,5},{2,10},{6,14},... | collective-permute-start | bytes 884744 | tf_op jit(solution)/shard_map/ppermute | solution.py:72
  483.7 20.7 %collective-permute-start.75 = (bf16[96,1536]{1,0:T(8,128)(2,1)}, bf16[96,1536]{1,0:T(8,128)(2,1)}, u32[]{:S(2)}, u32[]{:S(2)}) collective-permute-start(bf16[96,1536]{1,0:T(8,128)(2,1)} %collective-permute-done.71.refs_4_), channel_id=1, source_target_pairs={{0,12},{4,0},{8,4},{12,8},{1,13},{5,1},{9,5},{13,9},{2,14},{6,2},{... | collective-permute-start | bytes 884744 | tf_op jit(solution)/shard_map/ppermute | solution.py:72
  486.6 23.0 %collective-permute-start.72 = (bf16[4,130,384]{2,1,0:T(8,128)(2,1)S(1)}, bf16[4,130,384]{2,1,0:T(8,128)(2,1)S(1)}, u32[]{:S(2)}, u32[]{:S(2)}) collective-permute-start(bf16[4,130,384]{2,1,0:T(8,128)(2,1)S(1)} %pad_maximum_fusion.18.near), channel_id=1, source_target_pairs={{0,2},{2,0},{1,3},{3,1},{4,6},{6,4},{5,7},{7,5},{8,10},{10,8},{9,1... | collective-permute-start | bytes 1198088 | tf_op jit(solution)/shard_map/ppermute | solution.py:96
  (95 other events, 1024.4 us)
Sparse Core Ops, SparseCore 0:
  14.6 74.5 all-gather.4
  91.9 64.6 all-gather.6
  251.8 79.0 reduce-scatter.1

commit v5 on v4

--- a/solution.py
+++ b/solution.py
@@ -680,7 +680,7 @@
         return lax.dynamic_slice_in_dim(cond_part, (x + 4 - back) % 4 * (D // 4), D // 4, 1)
 
     cond_parts = scatter_x([columns_of(back) for back in range(4)])
-    cond_near = jnp.stack(gather_x(permuted(summed(cond_parts).astype(bf16))))
+    cond_own = permuted(summed(cond_parts).astype(bf16))
     at = jnp.stack([x, yh]).astype(jnp.int32)
 
     def column(gain):
@@ -703,11 +703,12 @@
         parts_attn, moved_in, moved_out, small, grad_feed_in, grad_feed_out
     )
     sum_attn = total(parts_attn)
-    attn_own, cond_near = both(sum_attn.astype(bf16), cond_near)
-    attn_near, attn_far, sum_attn, small, moved_in, moved_out, cond_near = both(
-        gather_x(attn_own), to_far(attn_own), sum_attn, small, moved_in, moved_out, cond_near
+    attn_own, cond_own = both(sum_attn.astype(bf16), cond_own)
+    attn_near, attn_far, sum_attn, small, moved_in, moved_out, cond_own = both(
+        gather_x(attn_own), to_far(attn_own), sum_attn, small, moved_in, moved_out, cond_own
     )
     attn_all = [*attn_near, *gather_x(attn_far)]
+    cond_near = jnp.stack(gather_x(cond_own))
     more = [row_sums(qvk_cols, sum_attn[:, : 3 * quarter])]
     more += [row_sums(own_cols(cq_half, quarter), sum_attn[:, 6 * quarter : 7 * quarter])]
     small = sent_to_all(jnp.concatenate([*more, small])[None], ("x", "yh", "tp"), 16).reshape(4, 2, 2, 4, 128)

time: 531 us -> 535 us (level)
    ppermute x1, waiting for transfers between devices: 0.01 us -> 5.88 us  [per_device(): moved_in = lax.ppermute(permuted(in_grad.astype(bf16)), ('yh', 'tp'), SWAP)]
  transfers between devices with their start and end apart: 81 -> 81, of which waited for: 41 -> 38; matrix products, arithmetic and copies ran while one was open for 25% -> 25% of each run, Pallas kernels for 15% -> 15%
where the time goes in v5:
time: 535 us; the launch traced here: 525 us
  waiting for transfers between devices  170 us (32%)
  starting transfers between devices  105 us (20%)
  Pallas kernels  80.3 us (15%)
  matrix products  55.8 us (10%)
  other arithmetic  55.2 us (10%)
  local copies, waits for them, and re-layouts  39.1 us (7%)
  between operations  15.5 us (3%)
  blocking collectives  5.47 us (1%)
    ppermute x54, waiting for transfers between devices, along_x(): return lax.ppermute(v, 'x', [(i, (i + step) % 4) for i in range(4)])  145 us
    ppermute x54, starting transfers between devices, along_x(): return lax.ppermute(v, 'x', [(i, (i + step) % 4) for i in range(4)])  61.3 us
    dot_general x7, matrix products, dot(): return jnp.dot(a, b, preferred_element_type=f32)  28.8 us
    dot_general x8, matrix products, dot_nt(): lax.dot_general(a, b, (((1,), (1,)), ((), ())), preferred_element_type=f32)  27 us
    pallas_call x1, Pallas kernels, attn_backward(): pl.pallas_call(attn_backward_kernel, in_specs=[pl.BlockSpec(memory_space=...  16.1 us
    pallas_call x1, Pallas kernels, attn_forward(): pl.pallas_call(attn_forward_kernel, in_specs=[pl.BlockSpec(memory_space=p...  13.3 us
    pallas_call x1, Pallas kernels, products(): pl.pallas_call(lambda *refs: products_kernel(len(pairs), *refs), grid=(D...  12.9 us
    pallas_call x1, Pallas kernels, attn_products(): pl.pallas_call(attn_products_kernel, grid=(D // tile,), in_specs=specs +...  12.9 us
  transfers between devices with their start and end apart: 81, of which 38 were waited for; matrix products, arithmetic and copies ran while one was open for 25% of the time, Pallas kernels for 15%

profile of v5, /device:TPU:1, one launch (start us, length us, event | category | flops | bytes accessed | tf_op | source)
XLA Modules:
  0.0 525.4 jit_solution(2148508592314255798)
XLA Ops:
  14.6 6.3 %collective-permute-start = (bf16[128,1536]{1,0:T(8,128)(2,1)S(1)}, bf16[128,1536]{1,0:T(8,128)(2,1)S(1)}, u32[]{:S(2)}, u32[]{:S(2)}) collective-permute-start(bf16[128,1536]{1,0:T(8,128)(2,1)S(1)} %dynamic-slice_bitcast_fusion.2), channel_id=1, source_target_pairs={{0,0},{1,2},{2,1},{3,3},{4,4},{5,6},{6,5},{7,7},{8,8},{9,10},{10,9... | collective-permute-start | bytes 1179656 | tf_op jit(solution)/shard_map/ppermute | solution.py:565
  24.7 3.1 fusion.61
  37.1 10.7 %collective-permute-done.3 = bf16[128,1536]{1,0:T(8,128)(2,1)} collective-permute-done((bf16[128,1536]{1,0:T(8,128)(2,1)S(1)}, bf16[128,1536]{1,0:T(8,128)(2,1)}, u32[]{:S(2)}, u32[]{:S(2)}) %collective-permute-start.3) | collective-permute-done | bytes 393248 | tf_op jit(solution)/shard_map/ppermute | solution.py:72
  47.8 4.0 collective-permute-done.1
  60.5 9.2 %collective-permute-done.8 = bf16[128,1536]{1,0:T(8,128)(2,1)S(1)} collective-permute-done((bf16[128,1536]{1,0:T(8,128)(2,1)S(1)}, bf16[128,1536]{1,0:T(8,128)(2,1)S(1)}, u32[]{:S(2)}, u32[]{:S(2)}) %collective-permute-start.8) | collective-permute-done | bytes 393248 | tf_op jit(solution)/shard_map/ppermute | solution.py:72
  71.2 9.1 %collective-permute-done.6 = bf16[128,1536]{1,0:T(8,128)(2,1)S(1)} collective-permute-done((bf16[128,1536]{1,0:T(8,128)(2,1)S(1)}, bf16[128,1536]{1,0:T(8,128)(2,1)S(1)}, u32[]{:S(2)}, u32[]{:S(2)}) %collective-permute-start.6) | collective-permute-done | bytes 393248 | tf_op jit(solution)/shard_map/ppermute | solution.py:72
  80.4 3.3 pad_maximum_fusion.one
  90.9 6.6 %fusion.19.qkv = f32[1024,640]{1,0:T(8,128)} fusion(bf16[1024,1536]{1,0:T(8,128)(2,1)} %pad_maximum_fusion.one, bf16[1536,2688]{1,0:T(8,128)(2,1)} %all-gather.5.cloned.1.call-done), kind=kOutput, calls=%fused_computation.44 | convolution fusion | flops 2013265920 | bytes 7733248 | tf_op jit(solution)/shard_map/dot_general | solution.py:40
  102.4 13.3 %shard_map.254 = (bf16[1024,256]{1,0:T(8,128)(2,1)}, bf16[1024,256]{1,0:T(8,128)(2,1)}, bf16[1024,256]{1,0:T(8,128)(2,1)}, bf16[1024,256]{1,0:T(8,128)(2,1)}, f32[8,1024]{1,0:T(8,128)}) custom-call(s32[3]{0:T(128)} %pad_add_fusion.sc, f32[1024,640]{1,0:T(8,128)} %fusion.19.qkv, f32[1024,128]{1,0:T(8,128)} %get-tuple-element.161.cosine, ...), custom_call_target="tpu_custom_call" | custom-call | flops 3221225472 | bytes 8388608 | tf_op jit(solution)/shard_map/pallas_call | solution.py:207
  119.9 3.0 collective-permute-done.13
  126.4 7.7 %collective-permute-done.14 = bf16[128,1536]{1,0:T(8,128)(2,1)S(1)} collective-permute-done((bf16[128,1536]{1,0:T(8,128)(2,1)S(1)}, bf16[128,1536]{1,0:T(8,128)(2,1)S(1)}, u32[]{:S(2)}, u32[]{:S(2)}) %collective-permute-start.14) | collective-permute-done | bytes 393248 | tf_op jit(solution)/shard_map/ppermute | solution.py:72
  135.5 9.2 %collective-permute-done.16 = bf16[128,1536]{1,0:T(8,128)(2,1)} collective-permute-done((bf16[128,1536]{1,0:T(8,128)(2,1)S(1)}, bf16[128,1536]{1,0:T(8,128)(2,1)}, u32[]{:S(2)}, u32[]{:S(2)}) %collective-permute-start.16) | collective-permute-done | bytes 393248 | tf_op jit(solution)/shard_map/ppermute | solution.py:72
  150.0 3.2 fusion.24.cq
  154.0 4.6 shard_map.255
  167.1 5.2 fusion.7
  177.3 9.2 %collective-permute-done.19 = bf16[128,1536]{1,0:T(8,128)(2,1)} collective-permute-done((bf16[128,1536]{1,0:T(8,128)(2,1)S(1)}, bf16[128,1536]{1,0:T(8,128)(2,1)}, u32[]{:S(2)}, u32[]{:S(2)}) %collective-permute-start.19) | collective-permute-done | bytes 393248 | tf_op jit(solution)/shard_map/ppermute | solution.py:72
  188.4 3.0 collective-permute-done.22
  195.7 5.0 fusion.2
  203.7 5.1 fusion
  208.8 7.3 %collective-permute-done.23.rest_5_ = bf16[128,1920]{1,0:T(8,128)(2,1)S(1)} collective-permute-done((bf16[128,1920]{1,0:T(8,128)(2,1)S(1)}, bf16[128,1920]{1,0:T(8,128)(2,1)S(1)}, u32[]{:S(2)}, u32[]{:S(2)}) %collective-permute-start.23) | collective-permute-done | bytes 491552 | tf_op jit(solution)/shard_map/ppermute | solution.py:72
  231.1 12.9 %shard_map.256 = bf16[1536,2304]{1,0:T(8,128)(2,1)} custom-call(bf16[1024,1536]{1,0:T(8,128)(2,1)} %copy-done.7, bf16[1024,1536]{1,0:T(8,128)(2,1)} %pad_maximum_fusion.3.refs_1_, bf16[1024,1536]{1,0:T(8,128)(2,1)} %pad_maximum_fusion.1.refs_2_, bf16[1024,768]{1,0:T(8,128)(2,1)} %get-tuple-element.223.refs_3_), custom_call_target="tpu_custom_call" | custom-call | flops 7247757312 | bytes 10485760 | tf_op jit(solution)/shard_map/pallas_call | solution.py:389
  247.5 4.3 collective-permute-done.29
  258.3 3.4 fusion.27.grad
  261.7 5.9 %shard_map.257 = (bf16[256,768]{1,0:T(8,128)(2,1)}, bf16[4,272,384]{2,1,0:T(8,128)(2,1)}) custom-call(s32[3]{0:T(128)} %pad_add_fusion.sc, bf16[256,768]{1,0:T(8,128)(2,1)} %fusion.24.cq, bf16[4,144,384]{2,1,0:T(8,128)(2,1)} %pad_maximum_fusion.16.kv, f32[144,256]{1,0:T(8,128)} %broadcast_in_dim.128.bias, bf16[256,768]{1,0:T(8,128)(2,1)} %fusion.27.grad), custom_call_target="tpu_custom_call" | custom-call | flops 566231040 | bytes 3145728 | tf_op jit(solution)/shard_map/pallas_call | solution.py:349
  269.2 9.1 %collective-permute-done.32 = bf16[128,1536]{1,0:T(8,128)(2,1)} collective-permute-done((bf16[128,1536]{1,0:T(8,128)(2,1)}, bf16[128,1536]{1,0:T(8,128)(2,1)}, u32[]{:S(2)}, u32[]{:S(2)}) %collective-permute-start.32) | collective-permute-done | bytes 393248 | tf_op jit(solution)/shard_map/ppermute | solution.py:72
  288.3 8.9 %collective-permute-done.38 = bf16[128,1536]{1,0:T(8,128)(2,1)S(1)} collective-permute-done((bf16[128,1536]{1,0:T(8,128)(2,1)S(1)}, bf16[128,1536]{1,0:T(8,128)(2,1)S(1)}, u32[]{:S(2)}, u32[]{:S(2)}) %collective-permute-start.38) | collective-permute-done | bytes 393248 | tf_op jit(solution)/shard_map/ppermute | solution.py:72
  299.1 9.3 %collective-permute-done.36 = bf16[128,1536]{1,0:T(8,128)(2,1)S(1)} collective-permute-done((bf16[128,1536]{1,0:T(8,128)(2,1)S(1)}, bf16[128,1536]{1,0:T(8,128)(2,1)S(1)}, u32[]{:S(2)}, u32[]{:S(2)}) %collective-permute-start.36) | collective-permute-done | bytes 393248 | tf_op jit(solution)/shard_map/ppermute | solution.py:72
  310.8 4.5 convolution_convert_fusion
  315.6 3.6 convolution_convert_fusion.2.grad
  324.6 16.1 %shard_map.258.grad = bf16[1024,640]{1,0:T(8,128)(2,1)} custom-call(bf16[1024,256]{1,0:T(8,128)(2,1)} %get-tuple-element.163.qs, bf16[1024,256]{1,0:T(8,128)(2,1)} %get-tuple-element.164.ks, bf16[1024,256]{1,0:T(8,128)(2,1)} %get-tuple-element.165.vs, bf16[1024,256]{1,0:T(8,128)(2,1)} %convolution_convert_fusion.2.grad, f32[8,1024]{1,0:T(8,128)} %get-tuple-element.228.lse, ...), custom_call_target="tpu_custom_call" | custom-call | flops 8053063680 | bytes 8388608 | tf_op jit(solution)/shard_map/pallas_call | solution.py:257
  349.1 12.9 %shard_map.259 = bf16[1536,1536]{1,0:T(8,128)(2,1)} custom-call(bf16[1024,1536]{1,0:T(8,128)(2,1)} %pad_maximum_fusion.one, bf16[1024,640]{1,0:T(8,128)(2,1)} %shard_map.258.grad, bf16[1024,1536]{1,0:T(8,128)(2,1)} %copy-done.2, bf16[1024,256]{1,0:T(8,128)(2,1)} %get-tuple-element.168.att, bf16[144,1536]{1,0:T(8,128)(2,1)} %copy-done.13, ...), custom_call_target="tpu_custom_call" | custom-call | flops 4831838208 | bytes 16777216 | tf_op jit(solution)/shard_map/pallas_call | solution.py:427
  362.0 4.5 collective-permute-done.46.refs_2_
  366.5 4.3 convolution_convert_fusion.1
  380.5 4.6 all-to-all-start
  385.1 3.6 fusion.5
  392.3 3.7 collective-permute-done.53
  403.9 18.6 %collective-permute-done.49 = bf16[128,1536]{1,0:T(8,128)(2,1)S(1)} collective-permute-done((bf16[128,1536]{1,0:T(8,128)(2,1)S(1)}, bf16[128,1536]{1,0:T(8,128)(2,1)S(1)}, u32[]{:S(2)}, u32[]{:S(2)}) %collective-permute-start.49) | collective-permute-done | bytes 393248 | tf_op jit(solution)/shard_map/ppermute | solution.py:72
  422.4 3.7 collective-permute-start.60
  430.7 3.3 stack.78
  441.7 4.7 collective-permute-start.57
  446.4 6.6 %shard_map.260 = (f32[192,2,3072]{2,1,0:T(2,128)}, f32[192,3072]{1,0:T(8,128)}) custom-call(s32[2]{0:T(128)} %pad_add_fusion.1.at, bf16[96,2304]{1,0:T(8,128)(2,1)} %reduce-scatter.2.cloned.1.call-done.refs_0_, bf16[96,2304]{1,0:T(8,128)(2,1)} %copy-done.32, bf16[96,2304]{1,0:T(8,128)(2,1)} %collective-permute-done.46.refs_2_, ...), custom_call_target="tpu_custom_call" | custom-call | flops 4194304 | bytes 11534336 | tf_op jit(solution)/shard_map/pallas_call | solution.py:459
  453.4 5.9 %collective-permute-done.56 = bf16[128,1536]{1,0:T(8,128)(2,1)S(1)} collective-permute-done((bf16[128,1536]{1,0:T(8,128)(2,1)S(1)}, bf16[128,1536]{1,0:T(8,128)(2,1)S(1)}, u32[]{:S(2)}, u32[]{:S(2)}) %collective-permute-start.56) | collective-permute-done | bytes 393248 | tf_op jit(solution)/shard_map/ppermute | solution.py:700
  459.2 4.2 collective-permute-done.57
  463.4 3.0 convert_reduce_fusion
  483.9 3.0 collective-permute-start.74
  487.6 6.2 %all-to-all-start.1 = ((f32[16,1,512]{2,1,0:T(1,128)}), f32[16,1,512]{2,1,0:T(1,128)S(1)}, u32[]{:S(2)}, u32[]{:S(2)}) async-start(f32[16,1,512]{2,1,0:T(1,128)} %broadcast_in_dim.133), calls=%async_computation.2 | async-start | bytes 65536 | tf_op jit(solution)/shard_map/all_to_all | solution.py:56
  501.6 3.1 all-gather.1
  508.8 5.2 shard_map.262
  (402 shorter events, 202.4 us)
Async XLA Ops:
  7.2 82.0 %all-gather.5.cloned.1.call-start = ((), (), s32[]{:S(2)}) async-start(), calls=%async_computation.3 | async-start | bytes 8773632 | tf_op jit(solution)/shard_map/all_gather | solution.py:130
  14.5 152.7 %all-gather.7.cloned.1.call-start = ((), (), s32[]{:S(2)}) async-start(), calls=%async_computation.4 | async-start | bytes 7520256 | tf_op jit(solution)/shard_map/all_gather | solution.py:130
  22.7 30.8 %collective-permute-start.4 = (bf16[128,1536]{1,0:T(8,128)(2,1)}, bf16[128,1536]{1,0:T(8,128)(2,1)}, u32[]{:S(2)}, u32[]{:S(2)}) collective-permute-start(bf16[128,1536]{1,0:T(8,128)(2,1)} %dynamic-slice_bitcast_fusion.1), channel_id=1, source_target_pairs={{0,0},{1,2},{2,1},{3,3},{4,4},{5,6},{6,5},{7,7},{8,8},{9,10},{10,9... | collective-permute-start | bytes 1179656 | tf_op jit(solution)/shard_map/ppermute | solution.py:566
  29.1 18.7 %collective-permute-start.3 = (bf16[128,1536]{1,0:T(8,128)(2,1)S(1)}, bf16[128,1536]{1,0:T(8,128)(2,1)}, u32[]{:S(2)}, u32[]{:S(2)}) collective-permute-start(bf16[128,1536]{1,0:T(8,128)(2,1)S(1)} %fusion.37), channel_id=1, source_target_pairs={{0,12},{4,0},{8,4},{12,8},{1,13},{5,1},{9,5},{13,9},{2,14},{6,2},{... | collective-permute-start | bytes 1179656 | tf_op jit(solution)/shard_map/ppermute | solution.py:72
  32.2 19.7 %collective-permute-start.1 = (bf16[128,1536]{1,0:T(8,128)(2,1)S(1)}, bf16[128,1536]{1,0:T(8,128)(2,1)}, u32[]{:S(2)}, u32[]{:S(2)}) collective-permute-start(bf16[128,1536]{1,0:T(8,128)(2,1)S(1)} %fusion.37), channel_id=1, source_target_pairs={{0,4},{4,8},{8,12},{12,0},{1,5},{5,9},{9,13},{13,1},{2,6},{6,10},{... | collective-permute-start | bytes 1179656 | tf_op jit(solution)/shard_map/ppermute | solution.py:72
  36.7 304.2 %reduce-scatter.2.cloned.1.call-start = ((), (), s32[]{:S(2)}) async-start(), calls=%async_computation.5 | async-start | bytes 7520256 | tf_op jit(solution)/shard_map/reduce_scatter | solution.py:134
  53.5 26.8 %collective-permute-start.5 = (bf16[512,1536]{1,0:T(8,128)(2,1)S(1)}, bf16[512,1536]{1,0:T(8,128)(2,1)}, u32[]{:S(2)}, u32[]{:S(2)}) collective-permute-start(bf16[512,1536]{1,0:T(8,128)(2,1)S(1)} %pad_maximum_fusion.6), channel_id=1, source_target_pairs={{0,1},{1,0},{2,3},{3,2},{4,5},{5,4},{6,7},{7,6},{8,9},{9,8},{10,11... | collective-permute-start | bytes 4718600 | tf_op jit(solution)/shard_map/ppermute | solution.py:52
  59.5 20.7 %collective-permute-start.6 = (bf16[128,1536]{1,0:T(8,128)(2,1)S(1)}, bf16[128,1536]{1,0:T(8,128)(2,1)S(1)}, u32[]{:S(2)}, u32[]{:S(2)}) collective-permute-start(bf16[128,1536]{1,0:T(8,128)(2,1)S(1)} %concatenate.100), channel_id=1, source_target_pairs={{0,4},{4,8},{8,12},{12,0},{1,5},{5,9},{9,13},{13,1},{2,6},{6,10},{... | collective-permute-start | bytes 1179656 | tf_op jit(solution)/shard_map/ppermute | solution.py:72
  97.5 18.2 %collective-permute-start.10 = (bf16[144,384]{1,0:T(8,128)(2,1)S(1)}, bf16[144,384]{1,0:T(8,128)(2,1)S(1)}, u32[]{:S(2)}, u32[]{:S(2)}) collective-permute-start(bf16[144,384]{1,0:T(8,128)(2,1)S(1)} %convolution_convert_fusion.3), channel_id=1, source_target_pairs={{0,4},{4,8},{8,12},{12,0},{1,5},{5,9},{9,13},{13,1},{2,6},{6,10},{... | collective-permute-start | bytes 331784 | tf_op jit(solution)/shard_map/ppermute | solution.py:72
  98.7 17.0 %collective-permute-start.11 = (bf16[144,384]{1,0:T(8,128)(2,1)S(1)}, bf16[144,384]{1,0:T(8,128)(2,1)S(1)}, u32[]{:S(2)}, u32[]{:S(2)}) collective-permute-start(bf16[144,384]{1,0:T(8,128)(2,1)S(1)} %convolution_convert_fusion.3), channel_id=1, source_target_pairs={{0,8},{4,12},{8,0},{12,4},{1,9},{5,13},{9,1},{13,5},{2,10},{6,14},... | collective-permute-start | bytes 331784 | tf_op jit(solution)/shard_map/ppermute | solution.py:72
  125.7 19.1 %collective-permute-start.16 = (bf16[128,1536]{1,0:T(8,128)(2,1)S(1)}, bf16[128,1536]{1,0:T(8,128)(2,1)}, u32[]{:S(2)}, u32[]{:S(2)}) collective-permute-start(bf16[128,1536]{1,0:T(8,128)(2,1)S(1)} %get-tuple-element.172), channel_id=1, source_target_pairs={{0,4},{4,8},{8,12},{12,0},{1,5},{5,9},{9,13},{13,1},{2,6},{6,10},{... | collective-permute-start | bytes 1179656 | tf_op jit(solution)/shard_map/ppermute | solution.py:72
  166.9 19.5 %collective-permute-start.19 = (bf16[128,1536]{1,0:T(8,128)(2,1)S(1)}, bf16[128,1536]{1,0:T(8,128)(2,1)}, u32[]{:S(2)}, u32[]{:S(2)}) collective-permute-start(bf16[128,1536]{1,0:T(8,128)(2,1)S(1)} %fusion.58), channel_id=1, source_target_pairs={{0,4},{4,8},{8,12},{12,0},{1,5},{5,9},{9,13},{13,1},{2,6},{6,10},{... | collective-permute-start | bytes 1179656 | tf_op jit(solution)/shard_map/ppermute | solution.py:72
  191.9 24.2 %collective-permute-start.23 = (bf16[128,1920]{1,0:T(8,128)(2,1)S(1)}, bf16[128,1920]{1,0:T(8,128)(2,1)S(1)}, u32[]{:S(2)}, u32[]{:S(2)}) collective-permute-start(bf16[128,1920]{1,0:T(8,128)(2,1)S(1)} %get-tuple-element.393), channel_id=1, source_target_pairs={{0,4},{4,8},{8,12},{12,0},{1,5},{5,9},{9,13},{13,1},{2,6},{6,10},{... | collective-permute-start | bytes 1474568 | tf_op jit(solution)/shard_map/ppermute | solution.py:72
  192.0 24.1 %collective-permute-start.24 = (bf16[128,1920]{1,0:T(8,128)(2,1)S(1)}, bf16[128,1920]{1,0:T(8,128)(2,1)S(1)}, u32[]{:S(2)}, u32[]{:S(2)}) collective-permute-start(bf16[128,1920]{1,0:T(8,128)(2,1)S(1)} %get-tuple-element.394), channel_id=1, source_target_pairs={{0,8},{4,12},{8,0},{12,4},{1,9},{5,13},{9,1},{13,5},{2,10},{6,14},... | collective-permute-start | bytes 1474568 | tf_op jit(solution)/shard_map/ppermute | solution.py:72
  193.5 22.9 %collective-permute-start.25 = (bf16[128,1920]{1,0:T(8,128)(2,1)S(1)}, bf16[128,1920]{1,0:T(8,128)(2,1)S(1)}, u32[]{:S(2)}, u32[]{:S(2)}) collective-permute-start(bf16[128,1920]{1,0:T(8,128)(2,1)S(1)} %get-tuple-element.392), channel_id=1, source_target_pairs={{0,12},{4,0},{8,4},{12,8},{1,13},{5,1},{9,5},{13,9},{2,14},{6,2},{... | collective-permute-start | bytes 1474568 | tf_op jit(solution)/shard_map/ppermute | solution.py:72
  228.2 19.3 %collective-permute-start.27 = (bf16[128,1536]{1,0:T(8,128)(2,1)}, bf16[128,1536]{1,0:T(8,128)(2,1)}, u32[]{:S(2)}, u32[]{:S(2)}) collective-permute-start(bf16[128,1536]{1,0:T(8,128)(2,1)} %get-tuple-element.201), channel_id=1, source_target_pairs={{0,12},{4,0},{8,4},{12,8},{1,13},{5,1},{9,5},{13,9},{2,14},{6,2},{... | collective-permute-start | bytes 1179656 | tf_op jit(solution)/shard_map/ppermute | solution.py:72
  230.5 17.0 %collective-permute-start.28 = (bf16[128,1536]{1,0:T(8,128)(2,1)}, bf16[128,1536]{1,0:T(8,128)(2,1)}, u32[]{:S(2)}, u32[]{:S(2)}) collective-permute-start(bf16[128,1536]{1,0:T(8,128)(2,1)} %get-tuple-element.202), channel_id=1, source_target_pairs={{0,8},{4,12},{8,0},{12,4},{1,9},{5,13},{9,1},{13,5},{2,10},{6,14},... | collective-permute-start | bytes 1179656 | tf_op jit(solution)/shard_map/ppermute | solution.py:72
  230.8 21.0 %collective-permute-start.29 = (bf16[128,1536]{1,0:T(8,128)(2,1)}, bf16[128,1536]{1,0:T(8,128)(2,1)}, u32[]{:S(2)}, u32[]{:S(2)}) collective-permute-start(bf16[128,1536]{1,0:T(8,128)(2,1)} %get-tuple-element.203), channel_id=1, source_target_pairs={{0,4},{4,8},{8,12},{12,0},{1,5},{5,9},{9,13},{13,1},{2,6},{6,10},{... | collective-permute-start | bytes 1179656 | tf_op jit(solution)/shard_map/ppermute | solution.py:72
  257.4 21.0 %collective-permute-start.32 = (bf16[128,1536]{1,0:T(8,128)(2,1)}, bf16[128,1536]{1,0:T(8,128)(2,1)}, u32[]{:S(2)}, u32[]{:S(2)}) collective-permute-start(bf16[128,1536]{1,0:T(8,128)(2,1)} %get-tuple-element.309), channel_id=1, source_target_pairs={{0,4},{4,8},{8,12},{12,0},{1,5},{5,9},{9,13},{13,1},{2,6},{6,10},{... | collective-permute-start | bytes 1179656 | tf_op jit(solution)/shard_map/ppermute | solution.py:72
  286.3 22.2 %collective-permute-start.39 = (bf16[512,1536]{1,0:T(8,128)(2,1)S(1)}, bf16[512,1536]{1,0:T(8,128)(2,1)S(1)}, u32[]{:S(2)}, u32[]{:S(2)}) collective-permute-start(bf16[512,1536]{1,0:T(8,128)(2,1)S(1)} %pad_maximum_fusion.10), channel_id=1, source_target_pairs={{0,1},{1,0},{2,3},{3,2},{4,5},{5,4},{6,7},{7,6},{8,9},{9,8},{10,11... | collective-permute-start | bytes 4718600 | tf_op jit(solution)/shard_map/ppermute | solution.py:52
  287.4 20.9 %collective-permute-start.36 = (bf16[128,1536]{1,0:T(8,128)(2,1)S(1)}, bf16[128,1536]{1,0:T(8,128)(2,1)S(1)}, u32[]{:S(2)}, u32[]{:S(2)}) collective-permute-start(bf16[128,1536]{1,0:T(8,128)(2,1)S(1)} %get-tuple-element.218), channel_id=1, source_target_pairs={{0,4},{4,8},{8,12},{12,0},{1,5},{5,9},{9,13},{13,1},{2,6},{6,10},{... | collective-permute-start | bytes 1179656 | tf_op jit(solution)/shard_map/ppermute | solution.py:72
  320.0 20.8 %collective-permute-start.41 = (bf16[272,384]{1,0:T(8,128)(2,1)}, bf16[272,384]{1,0:T(8,128)(2,1)S(1)}, u32[]{:S(2)}, u32[]{:S(2)}) collective-permute-start(bf16[272,384]{1,0:T(8,128)(2,1)} %get-tuple-element.341), channel_id=1, source_target_pairs={{0,4},{4,8},{8,12},{12,0},{1,5},{5,9},{9,13},{13,1},{2,6},{6,10},{... | collective-permute-start | bytes 626696 | tf_op jit(solution)/shard_map/ppermute | solution.py:72
  320.0 20.8 %collective-permute-start.42 = (bf16[272,384]{1,0:T(8,128)(2,1)S(1)}, bf16[272,384]{1,0:T(8,128)(2,1)S(1)}, u32[]{:S(2)}, u32[]{:S(2)}) collective-permute-start(bf16[272,384]{1,0:T(8,128)(2,1)S(1)} %get-tuple-element.340), channel_id=1, source_target_pairs={{0,8},{4,12},{8,0},{12,4},{1,9},{5,13},{9,1},{13,5},{2,10},{6,14},... | collective-permute-start | bytes 626696 | tf_op jit(solution)/shard_map/ppermute | solution.py:72
  321.5 19.3 %collective-permute-start.43 = (bf16[272,384]{1,0:T(8,128)(2,1)S(1)}, bf16[272,384]{1,0:T(8,128)(2,1)S(1)}, u32[]{:S(2)}, u32[]{:S(2)}) collective-permute-start(bf16[272,384]{1,0:T(8,128)(2,1)S(1)} %get-tuple-element.339), channel_id=1, source_target_pairs={{0,12},{4,0},{8,4},{12,8},{1,13},{5,1},{9,5},{13,9},{2,14},{6,2},{... | collective-permute-start | bytes 626696 | tf_op jit(solution)/shard_map/ppermute | solution.py:72
  323.9 49.8 %collective-permute-start.52 = (bf16[512,1536]{1,0:T(8,128)(2,1)}, bf16[512,1536]{1,0:T(8,128)(2,1)}, u32[]{:S(2)}, u32[]{:S(2)}) collective-permute-start(bf16[512,1536]{1,0:T(8,128)(2,1)} %slice.521), channel_id=1, source_target_pairs={{0,1},{1,0},{2,3},{3,2},{4,5},{5,4},{6,7},{7,6},{8,9},{9,8},{10,11... | collective-permute-start | bytes 4718600 | tf_op jit(solution)/shard_map/ppermute | solution.py:52
  340.8 21.1 %collective-permute-start.44 = (bf16[96,2304]{1,0:T(8,128)(2,1)}, bf16[96,2304]{1,0:T(8,128)(2,1)}, u32[]{:S(2)}, u32[]{:S(2)}) collective-permute-start(bf16[96,2304]{1,0:T(8,128)(2,1)} %reduce-scatter.2.cloned.1.call-done.refs_0_), channel_id=1, source_target_pairs={{0,2},{2,0},{1,3},{3,1},{4,6},{6,4},{5,7},{7,5},{8,10},{10,8},{9,1... | collective-permute-start | bytes 1327112 | tf_op jit(solution)/shard_map/ppermute | solution.py:96
  343.6 18.3 %collective-permute-start.45 = (bf16[96,2304]{1,0:T(8,128)(2,1)}, bf16[96,2304]{1,0:T(8,128)(2,1)S(1)}, u32[]{:S(2)}, u32[]{:S(2)}) collective-permute-start(bf16[96,2304]{1,0:T(8,128)(2,1)} %reduce-scatter.2.cloned.1.call-done.refs_0_), channel_id=1, source_target_pairs={{0,4},{4,8},{8,12},{12,0},{1,5},{5,9},{9,13},{13,1},{2,6},{6,10},{... | collective-permute-start | bytes 1327112 | tf_op jit(solution)/shard_map/ppermute | solution.py:72
  344.2 22.2 %collective-permute-start.46 = (bf16[96,2304]{1,0:T(8,128)(2,1)}, bf16[96,2304]{1,0:T(8,128)(2,1)}, u32[]{:S(2)}, u32[]{:S(2)}) collective-permute-start(bf16[96,2304]{1,0:T(8,128)(2,1)} %reduce-scatter.2.cloned.1.call-done.refs_0_), channel_id=1, source_target_pairs={{0,8},{4,12},{8,0},{12,4},{1,9},{5,13},{9,1},{13,5},{2,10},{6,14},... | collective-permute-start | bytes 1327112 | tf_op jit(solution)/shard_map/ppermute | solution.py:72
  346.3 20.2 %collective-permute-start.47 = (bf16[96,2304]{1,0:T(8,128)(2,1)}, bf16[96,2304]{1,0:T(8,128)(2,1)}, u32[]{:S(2)}, u32[]{:S(2)}) collective-permute-start(bf16[96,2304]{1,0:T(8,128)(2,1)} %reduce-scatter.2.cloned.1.call-done.refs_0_), channel_id=1, source_target_pairs={{0,12},{4,0},{8,4},{12,8},{1,13},{5,1},{9,5},{13,9},{2,14},{6,2},{... | collective-permute-start | bytes 1327112 | tf_op jit(solution)/shard_map/ppermute | solution.py:72
  377.0 18.9 %collective-permute-start.53 = (bf16[128,1536]{1,0:T(8,128)(2,1)S(1)}, bf16[128,1536]{1,0:T(8,128)(2,1)S(1)}, u32[]{:S(2)}, u32[]{:S(2)}) collective-permute-start(bf16[128,1536]{1,0:T(8,128)(2,1)S(1)} %get-tuple-element.322), channel_id=1, source_target_pairs={{0,12},{4,0},{8,4},{12,8},{1,13},{5,1},{9,5},{13,9},{2,14},{6,2},{... | collective-permute-start | bytes 1179656 | tf_op jit(solution)/shard_map/ppermute | solution.py:72
  379.3 19.4 %collective-permute-start.54 = (bf16[128,1536]{1,0:T(8,128)(2,1)}, bf16[128,1536]{1,0:T(8,128)(2,1)}, u32[]{:S(2)}, u32[]{:S(2)}) collective-permute-start(bf16[128,1536]{1,0:T(8,128)(2,1)} %get-tuple-element.321), channel_id=1, source_target_pairs={{0,8},{4,12},{8,0},{12,4},{1,9},{5,13},{9,1},{13,5},{2,10},{6,14},... | collective-permute-start | bytes 1179656 | tf_op jit(solution)/shard_map/ppermute | solution.py:72
  380.2 21.1 %collective-permute-start.55 = (bf16[128,1536]{1,0:T(8,128)(2,1)}, bf16[128,1536]{1,0:T(8,128)(2,1)}, u32[]{:S(2)}, u32[]{:S(2)}) collective-permute-start(bf16[128,1536]{1,0:T(8,128)(2,1)} %get-tuple-element.320), channel_id=1, source_target_pairs={{0,4},{4,8},{8,12},{12,0},{1,5},{5,9},{9,13},{13,1},{2,6},{6,10},{... | collective-permute-start | bytes 1179656 | tf_op jit(solution)/shard_map/ppermute | solution.py:72
  380.5 82.9 %all-to-all-start = ((bf16[16,96,1536]{2,1,0:T(8,128)(2,1)}), bf16[16,96,1536]{2,1,0:T(8,128)(2,1)}, u32[]{:S(2)}, u32[]{:S(2)}) async-start(bf16[16,96,1536]{2,1,0:T(8,128)(2,1)} %bitcast.67), calls=%async_computation.1 | async-start | bytes 9437184 | tf_op jit(solution)/shard_map/all_to_all | solution.py:56
  388.9 33.5 %collective-permute-start.49 = (bf16[128,1536]{1,0:T(8,128)(2,1)S(1)}, bf16[128,1536]{1,0:T(8,128)(2,1)S(1)}, u32[]{:S(2)}, u32[]{:S(2)}) collective-permute-start(bf16[128,1536]{1,0:T(8,128)(2,1)S(1)} %get-tuple-element.248), channel_id=1, source_target_pairs={{0,12},{4,0},{8,4},{12,8},{1,13},{5,1},{9,5},{13,9},{2,14},{6,2},{... | collective-permute-start | bytes 1179656 | tf_op jit(solution)/shard_map/ppermute | solution.py:72
  391.4 34.7 %collective-permute-start.50 = (bf16[128,1536]{1,0:T(8,128)(2,1)S(1)}, bf16[128,1536]{1,0:T(8,128)(2,1)S(1)}, u32[]{:S(2)}, u32[]{:S(2)}) collective-permute-start(bf16[128,1536]{1,0:T(8,128)(2,1)S(1)} %get-tuple-element.249), channel_id=1, source_target_pairs={{0,8},{4,12},{8,0},{12,4},{1,9},{5,13},{9,1},{13,5},{2,10},{6,14},... | collective-permute-start | bytes 1179656 | tf_op jit(solution)/shard_map/ppermute | solution.py:72
  395.9 31.2 %collective-permute-start.51 = (bf16[128,1536]{1,0:T(8,128)(2,1)S(1)}, bf16[128,1536]{1,0:T(8,128)(2,1)S(1)}, u32[]{:S(2)}, u32[]{:S(2)}) collective-permute-start(bf16[128,1536]{1,0:T(8,128)(2,1)S(1)} %get-tuple-element.250), channel_id=1, source_target_pairs={{0,4},{4,8},{8,12},{12,0},{1,5},{5,9},{9,13},{13,1},{2,6},{6,10},{... | collective-permute-start | bytes 1179656 | tf_op jit(solution)/shard_map/ppermute | solution.py:72
  398.8 38.5 %collective-permute-start.58 = (bf16[96,2304]{1,0:T(8,128)(2,1)}, bf16[96,2304]{1,0:T(8,128)(2,1)}, u32[]{:S(2)}, u32[]{:S(2)}) collective-permute-start(bf16[96,2304]{1,0:T(8,128)(2,1)} %collective-permute-done.44.refs_4_), channel_id=1, source_target_pairs={{0,4},{4,8},{8,12},{12,0},{1,5},{5,9},{9,13},{13,1},{2,6},{6,10},{... | collective-permute-start | bytes 1327112 | tf_op jit(solution)/shard_map/ppermute | solution.py:72
  401.3 37.8 %collective-permute-start.59 = (bf16[96,2304]{1,0:T(8,128)(2,1)}, bf16[96,2304]{1,0:T(8,128)(2,1)}, u32[]{:S(2)}, u32[]{:S(2)}) collective-permute-start(bf16[96,2304]{1,0:T(8,128)(2,1)} %collective-permute-done.44.refs_4_), channel_id=1, source_target_pairs={{0,8},{4,12},{8,0},{12,4},{1,9},{5,13},{9,1},{13,5},{2,10},{6,14},... | collective-permute-start | bytes 1327112 | tf_op jit(solution)/shard_map/ppermute | solution.py:72
  422.4 19.3 %collective-permute-start.60 = (bf16[96,2304]{1,0:T(8,128)(2,1)}, bf16[96,2304]{1,0:T(8,128)(2,1)}, u32[]{:S(2)}, u32[]{:S(2)}) collective-permute-start(bf16[96,2304]{1,0:T(8,128)(2,1)} %collective-permute-done.44.refs_4_), channel_id=1, source_target_pairs={{0,12},{4,0},{8,4},{12,8},{1,13},{5,1},{9,5},{13,9},{2,14},{6,2},{... | collective-permute-start | bytes 1327112 | tf_op jit(solution)/shard_map/ppermute | solution.py:72
  436.3 16.7 %collective-permute-start.64 = (bf16[130,384]{1,0:T(8,128)(2,1)S(1)}, bf16[130,384]{1,0:T(8,128)(2,1)S(1)}, u32[]{:S(2)}, u32[]{:S(2)}) collective-permute-start(bf16[130,384]{1,0:T(8,128)(2,1)S(1)} %get-tuple-element.352), channel_id=1, source_target_pairs={{0,4},{4,8},{8,12},{12,0},{1,5},{5,9},{9,13},{13,1},{2,6},{6,10},{... | collective-permute-start | bytes 299528 | tf_op jit(solution)/shard_map/ppermute | solution.py:72
  439.1 20.1 %collective-permute-start.56 = (bf16[128,1536]{1,0:T(8,128)(2,1)S(1)}, bf16[128,1536]{1,0:T(8,128)(2,1)S(1)}, u32[]{:S(2)}, u32[]{:S(2)}) collective-permute-start(bf16[128,1536]{1,0:T(8,128)(2,1)S(1)} %concatenate.121), channel_id=1, source_target_pairs={{0,0},{1,2},{2,1},{3,3},{4,4},{5,6},{6,5},{7,7},{8,8},{9,10},{10,9... | collective-permute-start | bytes 1179656 | tf_op jit(solution)/shard_map/ppermute | solution.py:700
  441.7 21.7 %collective-permute-start.57 = (bf16[128,1536]{1,0:T(8,128)(2,1)S(1)}, bf16[128,1536]{1,0:T(8,128)(2,1)S(1)}, u32[]{:S(2)}, u32[]{:S(2)}) collective-permute-start(bf16[128,1536]{1,0:T(8,128)(2,1)S(1)} %concatenate.122), channel_id=1, source_target_pairs={{0,0},{1,2},{2,1},{3,3},{4,4},{5,6},{6,5},{7,7},{8,8},{9,10},{10,9... | collective-permute-start | bytes 1179656 | tf_op jit(solution)/shard_map/ppermute | solution.py:701
  479.3 16.8 %collective-permute-start.71 = (bf16[130,384]{1,0:T(8,128)(2,1)S(1)}, bf16[130,384]{1,0:T(8,128)(2,1)S(1)}, u32[]{:S(2)}, u32[]{:S(2)}) collective-permute-start(bf16[130,384]{1,0:T(8,128)(2,1)S(1)} %pad_maximum_fusion.20), channel_id=1, source_target_pairs={{0,12},{4,0},{8,4},{12,8},{1,13},{5,1},{9,5},{13,9},{2,14},{6,2},{... | collective-permute-start | bytes 299528 | tf_op jit(solution)/shard_map/ppermute | solution.py:72
  479.9 18.9 %collective-permute-start.70 = (bf16[130,384]{1,0:T(8,128)(2,1)S(1)}, bf16[130,384]{1,0:T(8,128)(2,1)S(1)}, u32[]{:S(2)}, u32[]{:S(2)}) collective-permute-start(bf16[130,384]{1,0:T(8,128)(2,1)S(1)} %pad_maximum_fusion.20), channel_id=1, source_target_pairs={{0,8},{4,12},{8,0},{12,4},{1,9},{5,13},{9,1},{13,5},{2,10},{6,14},... | collective-permute-start | bytes 299528 | tf_op jit(solution)/shard_map/ppermute | solution.py:72
  481.8 17.0 %collective-permute-start.69 = (bf16[130,384]{1,0:T(8,128)(2,1)S(1)}, bf16[130,384]{1,0:T(8,128)(2,1)S(1)}, u32[]{:S(2)}, u32[]{:S(2)}) collective-permute-start(bf16[130,384]{1,0:T(8,128)(2,1)S(1)} %pad_maximum_fusion.20), channel_id=1, source_target_pairs={{0,4},{4,8},{8,12},{12,0},{1,5},{5,9},{9,13},{13,1},{2,6},{6,10},{... | collective-permute-start | bytes 299528 | tf_op jit(solution)/shard_map/ppermute | solution.py:72
  483.1 25.7 %collective-permute-start.73 = (bf16[96,1536]{1,0:T(8,128)(2,1)}, bf16[96,1536]{1,0:T(8,128)(2,1)}, u32[]{:S(2)}, u32[]{:S(2)}) collective-permute-start(bf16[96,1536]{1,0:T(8,128)(2,1)} %collective-permute-done.68.refs_4_), channel_id=1, source_target_pairs={{0,4},{4,8},{8,12},{12,0},{1,5},{5,9},{9,13},{13,1},{2,6},{6,10},{... | collective-permute-start | bytes 884744 | tf_op jit(solution)/shard_map/ppermute | solution.py:72
  483.9 24.8 %collective-permute-start.74 = (bf16[96,1536]{1,0:T(8,128)(2,1)}, bf16[96,1536]{1,0:T(8,128)(2,1)}, u32[]{:S(2)}, u32[]{:S(2)}) collective-permute-start(bf16[96,1536]{1,0:T(8,128)(2,1)} %collective-permute-done.68.refs_4_), channel_id=1, source_target_pairs={{0,8},{4,12},{8,0},{12,4},{1,9},{5,13},{9,1},{13,5},{2,10},{6,14},... | collective-permute-start | bytes 884744 | tf_op jit(solution)/shard_map/ppermute | solution.py:72
  487.6 18.5 %all-to-all-start.1 = ((f32[16,1,512]{2,1,0:T(1,128)}), f32[16,1,512]{2,1,0:T(1,128)S(1)}, u32[]{:S(2)}, u32[]{:S(2)}) async-start(f32[16,1,512]{2,1,0:T(1,128)} %broadcast_in_dim.133), calls=%async_computation.2 | async-start | bytes 65536 | tf_op jit(solution)/shard_map/all_to_all | solution.py:56
  (93 other events, 1074.5 us)
Sparse Core Ops, SparseCore 0:
  14.6 74.5 all-gather.4
  91.9 64.6 all-gather.6
  251.9 79.1 reduce-scatter.1
